TPU v7x, 32 devices: a whole 2x2x4 slice. The times are simulated.
32 devices in a mesh: row: 16 (over z, y, core), col: 2 (over x).
Axes of the slice: x: 2, y: 2, z: 4, core: 2. Of those that a mesh axis runs over, the one named last changes fastest.
Arguments:
- charges: bfloat16 [64, 131072], P(None, ('row', 'col')), may hold values from -6 to 6
- points: float32 [3, 131072], P(None, ('row', 'col')), may hold values from 0 to 64, as said below
- leaf_basis: bfloat16 [32, 131072], P(None, ('row', 'col')), may hold values from -0.75 to 0.75
- transfer_one: bfloat16 [2048, 32, 32], P(('row', 'col')), may hold values from -0.5 to 0.5
- transfer_two: bfloat16 [256, 32, 32], P(('row', 'col')), may hold values from -0.5 to 0.5
- couple_one: bfloat16 [256, 12, 32, 32], P(('row', 'col')), may hold values from -0.3125 to 0.3125
- couple_two: bfloat16 [32, 16, 32, 32], P(('row', 'col')), may hold values from -0.25 to 0.25
- near_list: int32 [2048, 27], P(('row', 'col')), may hold values from -1 to 2047, as said below
- list_one: int32 [256, 12], P(('row', 'col')), may hold values from -1 to 255, as said below
- list_two: int32 [32, 16], P(('row', 'col')), may hold values from 0 to 31
Outputs:
- potential: bfloat16 [64, 131072], P(None, ('row', 'col'))
Inputs may be any that keep to these rules, and one draw needn't show every extreme that they name: `points`: point p of the leaf at grid position (x, y, z) lies in the unit cube [x, x + 1) x [y, y + 1) x [z, z + 1). `near_list`: slot s = 9 (dz + 1) + 3 (dy + 1) + (dx + 1), with dx, dy, dz in -1, 0, 1, names the leaf at grid offset (dx, dy, dz) from the row's leaf, or is -1; it is -1 wherever that position lies outside the grid; slot 13 names the leaf itself. `list_one`: in each row the named nodes come first and the -1 entries last, at least 6 named; each named node has the same index // 16 as the row's node.
All inputs are finite; a program needn't handle non-finite values.
Results may differ from a plain program's by a relative error of at most 0.0053.
Values may be sent and summed in bfloat16 or wider, within the bound.
No kernel may reach another device: no remote copies, remote signals or barrier semaphores. Data moves between devices by JAX's collectives and lax.ppermute only.
A program may use at most 128 MiB of HBM per device.

v0:
```python
import jax
import jax.numpy as jnp
from jax import lax
from jax.sharding import PartitionSpec as P

PTS = 64
BX = 4
BY = 4
NEAR = 27


softening = 0.0025


def padded(value, sides, width):
    for axis, dim in sides:
        devices, length = (lax.axis_size(axis), value.shape[dim])
        up = [(i, (i + 1) % devices) for i in range(devices - 1)]
        down = [(j, i) for i, j in up]
        last = lax.slice_in_dim(value, length - width, length, axis=dim)
        initial = lax.slice_in_dim(value, 0, width, axis=dim)
        before = lax.ppermute(last, axis, up)
        after = lax.ppermute(initial, axis, down)
        value = jnp.concatenate([before, value, after], axis=dim)
    return value


def leaf_block(source, remote, values, active):
    distance = source[:, None, :, :, None] - remote[:, :, :, None, :]
    kernel = (
        active[:, :, None, None] / jnp.sqrt(jnp.sum(distance * distance, axis=2) + softening)
    ).astype(jnp.bfloat16)
    return jnp.einsum("lsij,lsrj->lri", kernel, values, preferred_element_type=jnp.float32)


def to_grid(flat, depth, upper, per_leaf):
    shaped = flat.reshape(depth, upper, 2, 2, 2, 2, 2, 2, per_leaf)
    moved = shaped.transpose(4, 7, 3, 6, 1, 2, 5, 0, 8)
    return moved.reshape(BX, BY, upper * 4, depth * per_leaf)


def shards(
    charges,
    points,
    leaf_basis,
    transfer_one,
    transfer_two,
    couple_one,
    couple_two,
    near_list,
    list_one,
    list_two,
):
    rhs_count, columns = charges.shape
    leaves = near_list.shape[0]
    per_leaf = columns // leaves
    rank_size = leaf_basis.shape[0]
    col_size = lax.axis_size("col")
    upper = leaves // 64
    depth_z = upper * 4
    charge_grid = to_grid(charges, rhs_count, upper, per_leaf)
    point_grid = to_grid(points, 3, upper, per_leaf)
    mask_grid = (
        near_list.reshape(upper, 2, 2, 2, 2, 2, 2, 27)
        .transpose(3, 6, 2, 5, 0, 1, 4, 7)
        .reshape(BX, BY, depth_z, 27)
    )
    wide_charges = padded(charge_grid, (("row", 1), ("col", 0)), 1)
    wide_points = padded(point_grid, (("row", 1), ("col", 0)), 1)
    wide_charges = jnp.pad(wide_charges, ((0, 0), (0, 0), (1, 1), (0, 0)))
    wide_points = jnp.pad(wide_points, ((0, 0), (0, 0), (1, 1), (0, 0)))
    block_leaves = BX * BY

    def near_step(layer_index):
        charge_layer = lax.dynamic_slice_in_dim(wide_charges, layer_index, 3, 2)
        point_layer = lax.dynamic_slice_in_dim(wide_points, layer_index, 3, 2)
        own_points = lax.dynamic_slice_in_dim(point_grid, layer_index, 1, 2)
        own_mask = lax.dynamic_slice_in_dim(mask_grid, layer_index, 1, 2)
        value_list = []
        place_list = []
        for step_z in range(3):
            for step_y in range(3):
                for step_x in range(3):
                    value_list.append(
                        charge_layer[step_x : step_x + BX, step_y : step_y + BY, step_z]
                    )
                    place_list.append(
                        point_layer[step_x : step_x + BX, step_y : step_y + BY, step_z]
                    )
        values = jnp.stack(value_list, axis=2).reshape(block_leaves, 27, rhs_count, per_leaf)
        remote = jnp.stack(place_list, axis=2).reshape(block_leaves, 27, 3, per_leaf)
        source = own_points.reshape(block_leaves, 3, per_leaf)
        active = (own_mask.reshape(block_leaves, 27) >= 0).astype(jnp.float32)
        return leaf_block(source, remote, values, active)

    near_layers = lax.map(near_step, jnp.arange(depth_z, dtype=jnp.int32))
    near_part = (
        near_layers.reshape(upper, 2, 2, 2, 2, 2, 2, rhs_count, per_leaf)
        .transpose(7, 0, 1, 5, 3, 2, 6, 4, 8)
        .reshape(rhs_count, leaves, per_leaf)
    )
    charge_leaf = charges.reshape(rhs_count, leaves, per_leaf)
    basis_leaf = leaf_basis.reshape(rank_size, leaves, per_leaf)
    coef_leaf = jnp.einsum(
        "kln,rln->lkr", basis_leaf, charge_leaf, preferred_element_type=jnp.float32
    ).astype(jnp.bfloat16)
    nodes_one = leaves // 8
    lifted = jnp.einsum("lab,lar->lbr", transfer_one, coef_leaf, preferred_element_type=jnp.float32)
    coef_one = lifted.reshape(nodes_one, 8, rank_size, rhs_count).sum(axis=1).astype(jnp.bfloat16)
    lifted_two = jnp.einsum(
        "lab,lar->lbr", transfer_two, coef_one, preferred_element_type=jnp.float32
    )
    coef_two = (
        lifted_two.reshape(nodes_one // 8, 8, rank_size, rhs_count).sum(axis=1).astype(jnp.bfloat16)
    )
    gathered, group_top = (
        lax.all_gather(coef_one, "col", axis=0, tiled=True),
        lax.all_gather(coef_two, "col", axis=0, tiled=True),
    )
    every_top = lax.all_gather(group_top, "row", axis=0, tiled=True)
    group_start = lax.axis_index("row") * col_size * nodes_one
    partner_ids = jnp.clip(list_one - group_start, 0, col_size * nodes_one - 1)
    active = (list_one >= 0).astype(jnp.bfloat16)
    partner = gathered[partner_ids] * active[:, :, None, None]
    field_one = jnp.einsum(
        "psab,psbr->par", couple_one, partner, preferred_element_type=jnp.float32
    )
    field_two = jnp.einsum(
        "psab,psbr->par", couple_two, every_top[list_two], preferred_element_type=jnp.float32
    )
    down_one = field_one + jnp.einsum(
        "pab,pbr->par",
        transfer_two.astype(jnp.float32),
        jnp.repeat(field_two, 8, axis=0),
        precision=lax.Precision.HIGHEST,
    )
    down_leaf = jnp.einsum(
        "lab,lbr->lar",
        transfer_one.astype(jnp.float32),
        jnp.repeat(down_one, 8, axis=0),
        precision=lax.Precision.HIGHEST,
    ).astype(jnp.bfloat16)
    far_part = jnp.einsum("kln,lkr->rln", basis_leaf, down_leaf, preferred_element_type=jnp.float32)
    potential = near_part * (NEAR * PTS) ** (-0.5) + far_part
    return potential.reshape(rhs_count, leaves * per_leaf).astype(jnp.bfloat16)


def solution(mesh):
    in_specs = (
        P(None, ("row", "col")),
        P(None, ("row", "col")),
        P(None, ("row", "col")),
        P(("row", "col"), None, None),
        P(("row", "col"), None, None),
        P(("row", "col"), None, None, None),
        P(("row", "col"), None, None, None),
        P(("row", "col"), None),
        P(("row", "col"), None),
        P(("row", "col"), None),
    )
    out_specs = P(None, ("row", "col"))
    return jax.shard_map(shards, mesh=mesh, in_specs=in_specs, out_specs=out_specs, check_vma=False)
```

profile of v0, /device:TPU:0, one launch (start us, length us, event | category | flops | bytes accessed | tf_op | source)
XLA Modules:
  0.0 429.5 jit_solution(8402552185586271822)
XLA Ops:
  0.0 3.6 reshape.72
  3.6 1.9 copy.176
  7.5 2.5 collective-permute-start
  12.3 5.7 %collective-permute-start.4 = (f32[4,1,4,192]{3,2,1,0:T(4,128)}, f32[4,1,4,192]{3,2,1,0:T(4,128)}, u32[]{:S(2)}, u32[]{:S(2)}) collective-permute-start(f32[4,1,4,192]{3,2,1,0:T(4,128)} %get-tuple-element.127), channel_id=1, source_target_pairs={{0,2},{2,4},{4,6},{6,8},{8,10},{10,12},{12,14},{14,16},{16,18},{18... | collective-permute-start | bytes 36872 | tf_op jit(solution)/shard_map/ppermute | solution.py:22
  19.3 2.1 reshape.79
  21.5 1.8 copy.94
  25.5 2.6 bitcast_reduce_fusion
  28.1 4.9 %all_gather.9 = bf16[16,32,64]{2,1,0:T(8,128)(2,1)S(1)} all-gather(bf16[8,32,64]{2,1,0:T(8,128)(2,1)S(1)} %bitcast_reduce_fusion), channel_id=1, replica_groups=mesh['row'=16,'col'=2] {'col'}, dimensions={0}, use_global_device_ids=true | all-gather | bytes 98304 | tf_op jit(solution)/shard_map/all_gather | solution.py:117
  34.2 4.4 %all-gather = bf16[64,64]{1,0:T(8,128)(2,1)S(1)} all-gather(bf16[32,64]{1,0:T(8,128)(2,1)S(1)} %fusion.18), channel_id=2, replica_groups=mesh['row'=16,'col'=2] {'col'}, dimensions={0}, use_global_device_ids=true | all-gather | bytes 12288 | tf_op jit(solution)/shard_map/all_gather | solution.py:118
  38.6 24.2 %all_gather.11 = bf16[32,32,64]{2,1,0:T(8,128)(2,1)S(1)} all-gather(bf16[2,32,64]{2,1,0:T(8,128)(2,1)S(1)} %bitcast.97), channel_id=1, replica_groups=mesh['row'=16,'col'=2] {'row'}, dimensions={0}, use_global_device_ids=true | all-gather | bytes 139264 | tf_op jit(solution)/shard_map/all_gather | solution.py:120
  69.1 3.4 collective-permute-start.6
  75.0 5.2 %collective-permute-start.2 = (bf16[1,6,4,4096]{3,1,0,2:T(8,128)(2,1)}, bf16[1,6,4,4096]{3,1,0,2:T(8,128)(2,1)}, u32[]{:S(2)}, u32[]{:S(2)}) collective-permute-start(bf16[1,6,4,4096]{3,1,0,2:T(8,128)(2,1)} %get-tuple-element.120), channel_id=1, source_target_pairs={{0,1},{2,3},{4,5},{6,7},{8,9},{10,11},{12,13},{14,15},{16,17},{18,... | collective-permute-start | bytes 589832 | tf_op jit(solution)/shard_map/ppermute | solution.py:22
  85.3 4.6 %collective-permute-done.3 = bf16[1,6,4,4096]{3,1,0,2:T(8,128)(2,1)} collective-permute-done((bf16[1,6,4,4096]{3,1,0,2:T(8,128)(2,1)S(1)}, bf16[1,6,4,4096]{3,1,0,2:T(8,128)(2,1)}, u32[]{:S(2)}, u32[]{:S(2)}) %collective-permute-start.3) | collective-permute-done | bytes 196640 | tf_op jit(solution)/shard_map/ppermute | solution.py:23
  89.9 2.2 select_maximum_fusion
  92.1 332.3 %while.10 = (s32[]{:T(128)}, f32[4,16,64,64]{3,2,1,0:T(8,128)}, s32[4]{0:T(128)S(1)}, bf16[6,6,6,4096]{3,1,0,2:T(8,128)(2,1)S(1)}, s32[4,4,4,27]{3,2,1,0:T(4,128...) while((s32[]{:T(128)}, f32[4,16,64,64]{3,2,1,0:T(8,128)}, ...), condition=%wide.region_2.3_spmd, body=%wide.region_0.2_spmd.sunk | while | flops 245957488 | bytes 45520492 | solution.py:96
  113.9 10.9 %reshape.114 = bf16[16,27,64,64]{3,2,0,1:T(8,128)(2,1)} reshape(bf16[4,4,27,4096]{3,1,0,2:T(4,128)(2,1)} %dynamic-slice_dynamic-update-slice_fusion.80) | data formatting | bytes 7077888 | tf_op jit(solution)/shard_map/while/body/eval_jaxpr/reshape | solution.py:90
  143.2 2.3 sub.39
  145.6 18.7 %multiply_reduce_fusion.2 = f32[16,27,64,64]{3,2,1,0:T(8,128)} fusion(f32[16,3,64]{2,1,0:T(4,128)S(1)} %sub.38, f32[16,27,3,64]{3,2,0,1:T(4,128)} %sub.39), kind=kLoop, calls=%fused_computation.2.clone.1 | loop fusion | flops 14155776 | bytes 7421952 | tf_op jit(solution)/shard_map/while/body/eval_jaxpr/reduce_sum | solution.py:31
  165.1 10.2 %fusion.53 = f32[4,16,64,64]{3,2,1,0:T(8,128)} fusion(f32[4,16,64,64]{3,2,1,0:T(8,128)} %get-tuple-element.241, s32[]{:T(128)} %get-tuple-element.240, bf16[16,27,64,64]{3,2,0,1:T(8,128)(2,1)} %reshape.114, f32[16,27,64,64]{3,2,1,0:T(8,128)} %multiply_reduce_fusion.2, f32[16,27]{1,0:T(8,128)S(1)} %bitcast.94), kind=kOutput, calls=%fused_computation.7.clone.1 | convolution fusion | flops 231800832 | bytes 21760192 | tf_op jit(solution)/shard_map/while/body/eval_jaxpr/lsij,lsrj->lri/dot_general | solution.py:33
  197.0 10.9 %reshape.114 = bf16[16,27,64,64]{3,2,0,1:T(8,128)(2,1)} reshape(bf16[4,4,27,4096]{3,1,0,2:T(4,128)(2,1)} %dynamic-slice_dynamic-update-slice_fusion.80) | data formatting | bytes 7077888 | tf_op jit(solution)/shard_map/while/body/eval_jaxpr/reshape | solution.py:90
  226.3 2.3 sub.39
  228.7 18.7 %multiply_reduce_fusion.2 = f32[16,27,64,64]{3,2,1,0:T(8,128)} fusion(f32[16,3,64]{2,1,0:T(4,128)S(1)} %sub.38, f32[16,27,3,64]{3,2,0,1:T(4,128)} %sub.39), kind=kLoop, calls=%fused_computation.2.clone.1 | loop fusion | flops 14155776 | bytes 7421952 | tf_op jit(solution)/shard_map/while/body/eval_jaxpr/reduce_sum | solution.py:31
  248.1 10.2 %fusion.53 = f32[4,16,64,64]{3,2,1,0:T(8,128)} fusion(f32[4,16,64,64]{3,2,1,0:T(8,128)} %get-tuple-element.241, s32[]{:T(128)} %get-tuple-element.240, bf16[16,27,64,64]{3,2,0,1:T(8,128)(2,1)} %reshape.114, f32[16,27,64,64]{3,2,1,0:T(8,128)} %multiply_reduce_fusion.2, f32[16,27]{1,0:T(8,128)S(1)} %bitcast.94), kind=kOutput, calls=%fused_computation.7.clone.1 | convolution fusion | flops 231800832 | bytes 21760192 | tf_op jit(solution)/shard_map/while/body/eval_jaxpr/lsij,lsrj->lri/dot_general | solution.py:33
  280.1 10.9 %reshape.114 = bf16[16,27,64,64]{3,2,0,1:T(8,128)(2,1)} reshape(bf16[4,4,27,4096]{3,1,0,2:T(4,128)(2,1)} %dynamic-slice_dynamic-update-slice_fusion.80) | data formatting | bytes 7077888 | tf_op jit(solution)/shard_map/while/body/eval_jaxpr/reshape | solution.py:90
  309.3 2.3 sub.39
  311.7 18.7 %multiply_reduce_fusion.2 = f32[16,27,64,64]{3,2,1,0:T(8,128)} fusion(f32[16,3,64]{2,1,0:T(4,128)S(1)} %sub.38, f32[16,27,3,64]{3,2,0,1:T(4,128)} %sub.39), kind=kLoop, calls=%fused_computation.2.clone.1 | loop fusion | flops 14155776 | bytes 7421952 | tf_op jit(solution)/shard_map/while/body/eval_jaxpr/reduce_sum | solution.py:31
  331.2 10.1 %fusion.53 = f32[4,16,64,64]{3,2,1,0:T(8,128)} fusion(f32[4,16,64,64]{3,2,1,0:T(8,128)} %get-tuple-element.241, s32[]{:T(128)} %get-tuple-element.240, bf16[16,27,64,64]{3,2,0,1:T(8,128)(2,1)} %reshape.114, f32[16,27,64,64]{3,2,1,0:T(8,128)} %multiply_reduce_fusion.2, f32[16,27]{1,0:T(8,128)S(1)} %bitcast.94), kind=kOutput, calls=%fused_computation.7.clone.1 | convolution fusion | flops 231800832 | bytes 21760192 | tf_op jit(solution)/shard_map/while/body/eval_jaxpr/lsij,lsrj->lri/dot_general | solution.py:33
  363.1 10.9 %reshape.114 = bf16[16,27,64,64]{3,2,0,1:T(8,128)(2,1)} reshape(bf16[4,4,27,4096]{3,1,0,2:T(4,128)(2,1)} %dynamic-slice_dynamic-update-slice_fusion.80) | data formatting | bytes 7077888 | tf_op jit(solution)/shard_map/while/body/eval_jaxpr/reshape | solution.py:90
  392.4 2.3 sub.39
  394.8 18.7 %multiply_reduce_fusion.2 = f32[16,27,64,64]{3,2,1,0:T(8,128)} fusion(f32[16,3,64]{2,1,0:T(4,128)S(1)} %sub.38, f32[16,27,3,64]{3,2,0,1:T(4,128)} %sub.39), kind=kLoop, calls=%fused_computation.2.clone.1 | loop fusion | flops 14155776 | bytes 7421952 | tf_op jit(solution)/shard_map/while/body/eval_jaxpr/reduce_sum | solution.py:31
  414.2 10.2 %fusion.53 = f32[4,16,64,64]{3,2,1,0:T(8,128)} fusion(f32[4,16,64,64]{3,2,1,0:T(8,128)} %get-tuple-element.241, s32[]{:T(128)} %get-tuple-element.240, bf16[16,27,64,64]{3,2,0,1:T(8,128)(2,1)} %reshape.114, f32[16,27,64,64]{3,2,1,0:T(8,128)} %multiply_reduce_fusion.2, f32[16,27]{1,0:T(8,128)S(1)} %bitcast.94), kind=kOutput, calls=%fused_computation.7.clone.1 | convolution fusion | flops 231800832 | bytes 21760192 | tf_op jit(solution)/shard_map/while/body/eval_jaxpr/lsij,lsrj->lri/dot_general | solution.py:33
  424.4 1.9 broadcast_multiply_fusion
  (328 shorter events, 176.7 us)
Async XLA Ops:
  0.0 65.2 %copy-start = (bf16[8,12,32,32]{3,2,1,0:T(8,128)(2,1)S(1)}, bf16[8,12,32,32]{3,2,1,0:T(8,128)(2,1)}, u32[]{:S(2)}) copy-start(bf16[8,12,32,32]{3,2,1,0:T(8,128)(2,1)} %param.17) | copy-start | bytes 589828
  0.0 19.3 %copy-start.2 = (bf16[64,4096]{1,0:T(8,128)(2,1)S(1)}, bf16[64,4096]{1,0:T(8,128)(2,1)}, u32[]{:S(2)}) copy-start(bf16[64,4096]{1,0:T(8,128)(2,1)} %param.12) | copy-start | bytes 1572868
  0.0 11.4 %copy-start.10 = (f32[3,4096]{1,0:T(4,128)S(1)}, f32[3,4096]{1,0:T(4,128)}, u32[]{:S(2)}) copy-start(f32[3,4096]{1,0:T(4,128)} %param.13) | copy-start | bytes 147460
  6.1 67.7 %copy-start.1 = (bf16[4,4,4,4096]{3,1,0,2:T(4,128)(2,1)}, bf16[4,4,4,4096]{3,1,0,2:T(4,128)(2,1)S(1)}, u32[]{:S(2)}) copy-start(bf16[4,4,4,4096]{3,1,0,2:T(4,128)(2,1)S(1)} %reshape.73) | copy-start | bytes 1572868
  6.2 26.9 %copy-start.11 = (s32[8,12]{1,0:T(8,128)S(1)}, s32[8,12]{1,0:T(8,128)}, u32[]{:S(2)}) copy-start(s32[8,12]{1,0:T(8,128)} %param.20) | copy-start | bytes 1156
  7.5 55.3 %copy-start.12 = (s32[1,16]{1,0:T(1,128)S(1)}, s32[1,16]{1,0:T(1,128)}, u32[]{:S(2)}) copy-start(s32[1,16]{1,0:T(1,128)} %param.21) | copy-start | bytes 196
  7.5 66.3 %collective-permute-start = (bf16[4,1,4,4096]{3,1,0,2:T(2,128)(2,1)}, bf16[4,1,4,4096]{3,1,0,2:T(2,128)(2,1)S(1)}, u32[]{:S(2)}, u32[]{:S(2)}) collective-permute-start(bf16[4,1,4,4096]{3,1,0,2:T(2,128)(2,1)} %get-tuple-element.122), channel_id=1, source_target_pairs={{0,2},{2,4},{4,6},{6,8},{8,10},{10,12},{12,14},{14,16},{16,18},{18... | collective-permute-start | bytes 393224 | tf_op jit(solution)/shard_map/ppermute | solution.py:22
  10.1 63.7 %collective-permute-start.1 = (bf16[4,1,4,4096]{3,1,0,2:T(2,128)(2,1)}, bf16[4,1,4,4096]{3,1,0,2:T(2,128)(2,1)S(1)}, u32[]{:S(2)}, u32[]{:S(2)}) collective-permute-start(bf16[4,1,4,4096]{3,1,0,2:T(2,128)(2,1)} %get-tuple-element.123), channel_id=1, source_target_pairs={{2,0},{4,2},{6,4},{8,6},{10,8},{12,10},{14,12},{16,14},{18,16},{20... | collective-permute-start | bytes 393224 | tf_op jit(solution)/shard_map/ppermute | solution.py:23
  12.3 54.7 %collective-permute-start.4 = (f32[4,1,4,192]{3,2,1,0:T(4,128)}, f32[4,1,4,192]{3,2,1,0:T(4,128)}, u32[]{:S(2)}, u32[]{:S(2)}) collective-permute-start(f32[4,1,4,192]{3,2,1,0:T(4,128)} %get-tuple-element.127), channel_id=1, source_target_pairs={{0,2},{2,4},{4,6},{6,8},{8,10},{10,12},{12,14},{14,16},{16,18},{18... | collective-permute-start | bytes 36872 | tf_op jit(solution)/shard_map/ppermute | solution.py:22
  18.0 49.7 %collective-permute-start.5 = (f32[4,1,4,192]{3,2,1,0:T(4,128)}, f32[4,1,4,192]{3,2,1,0:T(4,128)}, u32[]{:S(2)}, u32[]{:S(2)}) collective-permute-start(f32[4,1,4,192]{3,2,1,0:T(4,128)} %get-tuple-element.126), channel_id=1, source_target_pairs={{2,0},{4,2},{6,4},{8,6},{10,8},{12,10},{14,12},{16,14},{18,16},{20... | collective-permute-start | bytes 36872 | tf_op jit(solution)/shard_map/ppermute | solution.py:23
  21.5 43.5 %copy-start.9 = (bf16[1,16,32,32]{3,2,1,0:T(8,128)(2,1)S(1)}, bf16[1,16,32,32]{3,2,1,0:T(8,128)(2,1)}, u32[]{:S(2)}) copy-start(bf16[1,16,32,32]{3,2,1,0:T(8,128)(2,1)} %param.18) | copy-start | bytes 98308
  24.7 0.8 copy-start.3
  25.5 41.3 %copy-start.8 = (bf16[8,32,32]{2,1,0:T(8,128)(2,1)S(1)}, bf16[8,32,32]{2,1,0:T(8,128)(2,1)}, u32[]{:S(2)}) copy-start(bf16[8,32,32]{2,1,0:T(8,128)(2,1)} %param.16) | copy-start | bytes 49156
  69.1 15.6 %collective-permute-start.6 = (f32[1,6,4,192]{3,2,1,0:T(4,128)}, f32[1,6,4,192]{3,2,1,0:T(4,128)S(1)}, u32[]{:S(2)}, u32[]{:S(2)}) collective-permute-start(f32[1,6,4,192]{3,2,1,0:T(4,128)} %get-tuple-element.124), channel_id=1, source_target_pairs={{0,1},{2,3},{4,5},{6,7},{8,9},{10,11},{12,13},{14,15},{16,17},{18,... | collective-permute-start | bytes 55304 | tf_op jit(solution)/shard_map/ppermute | solution.py:22
  72.5 12.3 %collective-permute-start.7 = (f32[1,6,4,192]{3,2,1,0:T(4,128)S(1)}, f32[1,6,4,192]{3,2,1,0:T(4,128)S(1)}, u32[]{:S(2)}, u32[]{:S(2)}) collective-permute-start(f32[1,6,4,192]{3,2,1,0:T(4,128)S(1)} %get-tuple-element.125), channel_id=1, source_target_pairs={{1,0},{3,2},{5,4},{7,6},{9,8},{11,10},{13,12},{15,14},{17,16},{19,... | collective-permute-start | bytes 55304 | tf_op jit(solution)/shard_map/ppermute | solution.py:23
  73.8 11.5 %copy-start.6 = (bf16[4,1,4,4096]{3,1,0,2:T(2,128)(2,1)}, bf16[4,1,4,4096]{3,1,0,2:T(2,128)(2,1)S(1)}, u32[]{:S(2)}) copy-start(bf16[4,1,4,4096]{3,1,0,2:T(2,128)(2,1)S(1)} %collective-permute-done) | copy-start | bytes 393220
  73.8 10.9 %copy-start.7 = (bf16[4,1,4,4096]{3,1,0,2:T(2,128)(2,1)}, bf16[4,1,4,4096]{3,1,0,2:T(2,128)(2,1)S(1)}, u32[]{:S(2)}) copy-start(bf16[4,1,4,4096]{3,1,0,2:T(2,128)(2,1)S(1)} %collective-permute-done.1) | copy-start | bytes 393220
  75.0 10.4 %collective-permute-start.2 = (bf16[1,6,4,4096]{3,1,0,2:T(8,128)(2,1)}, bf16[1,6,4,4096]{3,1,0,2:T(8,128)(2,1)}, u32[]{:S(2)}, u32[]{:S(2)}) collective-permute-start(bf16[1,6,4,4096]{3,1,0,2:T(8,128)(2,1)} %get-tuple-element.120), channel_id=1, source_target_pairs={{0,1},{2,3},{4,5},{6,7},{8,9},{10,11},{12,13},{14,15},{16,17},{18,... | collective-permute-start | bytes 589832 | tf_op jit(solution)/shard_map/ppermute | solution.py:22
  80.2 9.7 %collective-permute-start.3 = (bf16[1,6,4,4096]{3,1,0,2:T(8,128)(2,1)S(1)}, bf16[1,6,4,4096]{3,1,0,2:T(8,128)(2,1)}, u32[]{:S(2)}, u32[]{:S(2)}) collective-permute-start(bf16[1,6,4,4096]{3,1,0,2:T(8,128)(2,1)S(1)} %get-tuple-element.121), channel_id=1, source_target_pairs={{1,0},{3,2},{5,4},{7,6},{9,8},{11,10},{13,12},{15,14},{17,16},{19,... | collective-permute-start | bytes 589832 | tf_op jit(solution)/shard_map/ppermute | solution.py:23
  92.1 21.8 %copy-start.13 = (s32[4]{0:T(128)}, s32[4]{0:T(128)S(1)}, u32[]{:S(2)}) copy-start(s32[4]{0:T(128)S(1)} %get-tuple-element.255) | copy-start | bytes 52 | tf_op jit(solution)/shard_map/while
  165.0 10.2 %copy-start.14 = (s32[4]{0:T(128)S(1)}, s32[4]{0:T(128)}, u32[]{:S(2)}) copy-start(s32[4]{0:T(128)} %copy-done.13) | copy-start | bytes 52 | tf_op jit(solution)/shard_map/while
  175.2 21.8 %copy-start.13 = (s32[4]{0:T(128)}, s32[4]{0:T(128)S(1)}, u32[]{:S(2)}) copy-start(s32[4]{0:T(128)S(1)} %get-tuple-element.255) | copy-start | bytes 52 | tf_op jit(solution)/shard_map/while
  248.1 10.2 %copy-start.14 = (s32[4]{0:T(128)S(1)}, s32[4]{0:T(128)}, u32[]{:S(2)}) copy-start(s32[4]{0:T(128)} %copy-done.13) | copy-start | bytes 52 | tf_op jit(solution)/shard_map/while
  258.3 21.8 %copy-start.13 = (s32[4]{0:T(128)}, s32[4]{0:T(128)S(1)}, u32[]{:S(2)}) copy-start(s32[4]{0:T(128)S(1)} %get-tuple-element.255) | copy-start | bytes 52 | tf_op jit(solution)/shard_map/while
  331.2 10.2 %copy-start.14 = (s32[4]{0:T(128)S(1)}, s32[4]{0:T(128)}, u32[]{:S(2)}) copy-start(s32[4]{0:T(128)} %copy-done.13) | copy-start | bytes 52 | tf_op jit(solution)/shard_map/while
  341.3 21.8 %copy-start.13 = (s32[4]{0:T(128)}, s32[4]{0:T(128)S(1)}, u32[]{:S(2)}) copy-start(s32[4]{0:T(128)S(1)} %get-tuple-element.255) | copy-start | bytes 52 | tf_op jit(solution)/shard_map/while
  414.2 10.2 %copy-start.14 = (s32[4]{0:T(128)S(1)}, s32[4]{0:T(128)}, u32[]{:S(2)}) copy-start(s32[4]{0:T(128)} %copy-done.13) | copy-start | bytes 52 | tf_op jit(solution)/shard_map/while
  424.4 2.1 copy-start.4
  424.4 2.1 copy-start.5
where the time goes:
time: 432 us; the launch traced here: 429 us
  local copies, waits for them, and re-layouts  227 us (53%)
  other arithmetic  80 us (19%)
  matrix products  48.5 us (11%)
  blocking collectives  33.5 us (8%)
  starting transfers between devices  22.2 us (5%)
  loops' own time  13.2 us (3%)
  waiting for transfers between devices  5.1 us (1%)
    while x224, local copies, waits for them, and re-layouts  137 us
    reduce_sum x4, other arithmetic, leaf_block(): jnp.sum(distance * distance, axis=2) + softening  74.7 us
    reshape x4, local copies, waits for them, and re-layouts, near_step(): jnp.stack(value_list, axis=2).reshape(block_leaves, 27, rhs_count, per_leaf)  43.7 us
    dot_general x4, matrix products, leaf_block(): jnp.einsum('lsij,lsrj->lri', kernel, values, preferred_element_type=jnp.f...  40.6 us
    all_gather x1, blocking collectives, shards(): every_top = lax.all_gather(group_top, 'row', axis=0, tiled=True)  24.2 us
    ppermute x4, starting transfers between devices, padded(): before = lax.ppermute(last, axis, up)  16.9 us
    another operation x1, loops' own time, shards(): near_layers = lax.map(near_step, jnp.arange(depth_z, dtype=jnp.int32))  13.2 us
    sub x8, local copies, waits for them, and re-layouts, leaf_block(): distance = source[:, None, :, :, None] - remote[:, :, :, None, :]  9.59 us
  transfers between devices with their start and end apart: 8, of which 2 were waited for; matrix products, arithmetic and copies ran while one was open for 5% of the time, Pallas kernels for 0%

commit v1 on v0

v1 whole, which is shorter than its diff:
```python
import functools

import jax
import jax.numpy as jnp
import numpy as np
from jax import lax
from jax.experimental import pallas as pl
from jax.experimental.pallas import tpu as pltpu
from jax.sharding import PartitionSpec as P

NEAR = 27
SIDE = 4
SOFTENING = 0.0025
F32 = jnp.float32
BF16 = jnp.bfloat16
NT = (((1,), (1,)), ((), ()))
TN = (((0,), (0,)), ((), ()))
NN = (((1,), (0,)), ((), ()))


def dot(a, b, dims=NN):
    return lax.dot_general(a, b, dims, preferred_element_type=F32)


def split2(v):
    hi = v.astype(BF16)
    lo = (v - hi.astype(F32)).astype(BF16)
    return hi, lo


def tile_of(z, y, x1):
    return (z // 4) * 32 + (z // 2 % 2) * 16 + (y // 2) * 8 + x1 * 4 + (z % 2) * 2 + (y % 2)


def lower_half(shape):
    return lax.broadcasted_iota(jnp.int32, shape, len(shape) - 1) % 128 < 64


def swap_matrix():
    a = lax.broadcasted_iota(jnp.int32, (128, 128), 0)
    b = lax.broadcasted_iota(jnp.int32, (128, 128), 1)
    return jnp.where((a + 64) % 128 == b, 1.0, 0.0).astype(BF16)


def block_basis(basis):
    rank, width = basis.shape
    leaf = lax.broadcasted_iota(jnp.int32, (rank, width), 1) // 64
    zero = jnp.zeros_like(basis)
    return jnp.concatenate([jnp.where(leaf == k, basis, zero) for k in range(8)], axis=0)


def up_kernel(merge, depth, q_ref, pts_ref, basis_ref, t1_ref, t2_ref, pb_ref, xpay_ref, coef_ref, *more):
    row, col = lax.axis_index("row"), lax.axis_index("col")
    columns = q_ref.shape[1]
    nodes = columns // 512
    centre = (
        (SIDE * col + SIDE // 2).astype(F32),
        (SIDE * row + SIDE // 2).astype(F32),
        jnp.float32(depth / 2),
    )
    index = lax.broadcasted_iota(jnp.int32, (16, columns), 0)
    rows = jnp.zeros((16, columns), F32)
    for c in range(3):
        local = pts_ref[c : c + 1, :] - centre[c]
        hi, lo = split2(local)
        rows = jnp.where(index == c, hi.astype(F32), rows)
        rows = jnp.where(index == c + 3, lo.astype(F32), rows)
    pb_ref[...] = rows.astype(BF16)
    swap = swap_matrix()
    low = lower_half((80, 128))
    for z in range(depth):
        for y1 in range(2):
            out = z * 2 + y1

            def tile(y, x1):
                at = tile_of(z, y, x1) * 128
                return jnp.concatenate([q_ref[:, at : at + 128], pb_ref[:, at : at + 128]], axis=0)

            high = jnp.where(low, dot(tile(2 * y1, 1), swap).astype(BF16), tile(2 * y1 + 1, 1))
            base = jnp.where(low, tile(2 * y1, 0), dot(tile(2 * y1 + 1, 0), swap).astype(BF16))
            if merge:
                xpay_ref[:, out * 128 : out * 128 + 128] = jnp.where(col == 0, high, base)
            else:
                xpay_ref[:, out * 128 : out * 128 + 128] = high
                more[0][:, out * 128 : out * 128 + 128] = base
    ones = []
    for n in range(nodes):
        chunk = slice(512 * n, 512 * n + 512)
        leaf = dot(block_basis(basis_ref[:, chunk]), q_ref[:, chunk], NT).astype(BF16)
        ones.append(dot(t1_ref[256 * n : 256 * n + 256, :], leaf, TN).astype(BF16))
        coef_ref[32 * n : 32 * n + 32, :] = ones[-1]
    for m in range(nodes // 8):
        part = jnp.concatenate(ones[8 * m : 8 * m + 8], axis=0)
        two = dot(t2_ref[256 * m : 256 * m + 256, :], part, TN).astype(BF16)
        coef_ref[32 * (nodes + m) : 32 * (nodes + m) + 32, :] = two


def pack_kernel(merge, depth, q_ref, pb_ref, *refs):
    if merge:
        xr_ref, h_ref, even_ref, odd_ref = refs
    else:
        xl_ref, xr_ref, h_ref, even_ref, odd_ref = refs
    row, col = lax.axis_index("row"), lax.axis_index("col")
    swap = swap_matrix()
    low = lower_half((80, 128))
    for z in range(depth):
        for y1 in range(2):
            at = (z * 2 + y1) * 128
            right = xr_ref[:, at : at + 128]
            left = right if merge else xl_ref[:, at : at + 128]
            h0 = jnp.where(low, right, dot(left, swap).astype(BF16))
            h1 = jnp.where(low, dot(right, swap).astype(BF16), left)
            at = (z * 4 + 2 * y1) * 128
            h_ref[:, at : at + 128] = h0
            h_ref[:, at + 128 : at + 256] = h1
    even = row % 2 == 0
    for z in range(depth):
        for k in range(3):

            def piece(y):
                if k < 2:
                    at = tile_of(z, y, k) * 128
                    return jnp.concatenate([q_ref[:, at : at + 128], pb_ref[:, at : at + 128]], axis=0)
                at = (z * 4 + y) * 128
                return h_ref[:, at : at + 128]

            first, last = piece(0), piece(SIDE - 1)
            at = (z * 3 + k) * 128
            even_ref[:, at : at + 128] = jnp.where(even, last, first)
            odd_ref[:, at : at + 128] = jnp.where(even, first, last)


def features(hi_lo, shift, scale):
    x = [hi_lo[c : c + 1, :] + hi_lo[c + 3 : c + 4, :] + shift[c] for c in range(3)]
    norm = x[0] * x[0] + x[1] * x[1] + x[2] * x[2]
    pairs = [split2(v) for v in x]
    hi = [a.astype(F32) * scale for a, _ in pairs]
    lo = [b.astype(F32) * scale for _, b in pairs]
    return norm, hi, lo


def split3(v):
    a = v.astype(BF16).astype(F32)
    b = (v - a).astype(BF16).astype(F32)
    c = (v - a - b).astype(BF16).astype(F32)
    return a, b, c


def stack_rows(pieces, width):
    index = lax.broadcasted_iota(jnp.int32, (32, width), 0)
    out = jnp.zeros((32, width), F32)
    for k, piece in enumerate(pieces):
        out = jnp.where(index == k, piece, out)
    return out


def source_rows(points, shift):
    norm, hi, lo = features(points, shift, 1.0)
    return stack_rows(hi + lo + hi + lo + [1.0, 1.0, 1.0] + list(split3(norm)), points.shape[1])


def target_rows(points):
    zero = [0.0, 0.0, 0.0]
    norm, hi, lo = features(points, zero, -2.0)
    return stack_rows(hi + hi + lo + lo + list(split3(norm + SOFTENING)) + [1.0, 1.0, 1.0], points.shape[1])


def near_kernel(
    depth, group, q_ref, pb_ref, h_ref, even_ref, odd_ref, nl_ref, pick_a_ref, pick_b_ref,
    basis_ref, t1_ref, t2_ref, k1_ref, k2_ref, coef_ref, top_ref, l1_ref, l2_ref,
    out_ref, cx_ref, yt_ref, rows_ref, w_ref, mask_ref, acc_ref, near_ref,
):
    row, col = lax.axis_index("row"), lax.axis_index("col")
    columns = q_ref.shape[1]
    leaves = columns // 64
    even = row % 2 == 0
    low = lower_half((80, 128))
    lane = lax.broadcasted_iota(jnp.int32, (1, 256), 1)
    for z in range(depth):
        for ye in range(SIDE + 2):
            def piece(k):
                if 1 <= ye <= SIDE:
                    y = ye - 1
                    if k < 2:
                        at = tile_of(z, y, k) * 128
                        return jnp.concatenate([q_ref[:, at : at + 128], pb_ref[:, at : at + 128]], axis=0)
                    at = (z * 4 + y) * 128
                    return h_ref[:, at : at + 128]
                at = (z * 3 + k) * 128
                a, b = even_ref[:, at : at + 128], odd_ref[:, at : at + 128]
                if ye == 0:
                    return jnp.where(even, b, a)
                return jnp.where(even, a, b)

            t0, t1, th = piece(0), piece(1), piece(2)
            for xp, (first, second) in enumerate(((t0, jnp.where(low, t1, th)), (t1, jnp.where(low, th, t0)))):
                cx_ref[xp, z * (SIDE + 2) + ye, :, 0:128] = first[0:64]
                cx_ref[xp, z * (SIDE + 2) + ye, :, 128:256] = second[0:64]
                hl = jnp.concatenate([first[64:80], second[64:80]], axis=1).astype(F32)
                if xp == 0:
                    shift_x = jnp.where(lane >= 192, -float(SIDE), 0.0)
                else:
                    shift_x = jnp.where((lane >= 128) & (lane < 192), float(SIDE), 0.0)
                shift_y = -float(SIDE) if ye == 0 else float(SIDE) if ye == SIDE + 1 else 0.0
                rows_ref[xp, 32 * ye : 32 * ye + 32, :] = source_rows(hl, [shift_x, shift_y, 0.0])
        for xp in range(2):
            for dy in range(3):
                block = rows_ref[xp, 32 * dy : 32 * dy + 128, :]
                yt_ref[xp, dy * depth + z] = block.T.astype(BF16)
    active = jnp.where(nl_ref[...] >= 0, 1.0, 0.0).astype(BF16)
    pick = jnp.where(
        lax.broadcasted_iota(jnp.int32, (48, leaves), 1) % 2 == 0,
        dot(pick_a_ref[...], active, NT),
        dot(pick_b_ref[...], active, NT),
    ).astype(BF16)
    spread = jnp.where(
        lax.broadcasted_iota(jnp.int32, (leaves, columns), 0)
        == lax.broadcasted_iota(jnp.int32, (leaves, columns), 1) // 64,
        1.0,
        0.0,
    ).astype(BF16)
    mask_ref[...] = dot(pick, spread)
    w_ref[...] = jnp.zeros_like(w_ref)

    def target(index, carry):
        tz, xp = index // 2, index % 2
        base = (tz // 4) * 32 + (tz // 2 % 2) * 16 + xp * 4 + (tz % 2) * 2
        for ty in range(SIDE):
            at = pl.multiple_of((base + (ty // 2) * 8 + ty % 2) * 128, 128)
            hl = pb_ref[:, pl.ds(at, 128)].astype(F32)
            w_ref[32 * ty : 32 * ty + 32, 128 * ty : 128 * ty + 128] = target_rows(hl).astype(BF16)
        acc_ref[...] = jnp.zeros_like(acc_ref)

        def layer(dz, carry):
            z = tz + dz - 1
            for dy in range(3):
                left = yt_ref[xp, dy * depth + z]
                for pair in range(2):
                    d2 = dot(left, w_ref[:, 256 * pair : 256 * pair + 256])
                    inv = lax.rsqrt(d2)
                    for half in range(2):
                        ty = 2 * pair + half
                        at = pl.multiple_of((base + (ty // 2) * 8 + ty % 2) * 128, 128)
                        parts = []
                        masks = mask_ref[pl.ds(pl.multiple_of(dz * 16, 16), 16), pl.ds(at, 128)]
                        for k in range(4):
                            m = masks[dy * 4 + k : dy * 4 + k + 1, :]
                            parts.append((inv[64 * k : 64 * k + 64, 128 * half : 128 * half + 128] * m).astype(BF16))
                        kernel = jnp.concatenate(parts, axis=0)
                        acc_ref[ty] += dot(cx_ref[xp, z * (SIDE + 2) + ty + dy], kernel)
            return carry

        lax.fori_loop(jnp.maximum(1 - tz, 0), jnp.minimum(depth + 1 - tz, 3), layer, 0)
        for ty in range(SIDE):
            at = pl.multiple_of((base + (ty // 2) * 8 + ty % 2) * 128, 128)
            near_ref[:, pl.ds(at, 128)] = acc_ref[ty]
        return carry

    lax.fori_loop(0, 2 * depth, target, 0)
    nodes = leaves // 8
    me = row * lax.axis_size("col") + col
    start = row * group
    for m in range(nodes // 8):
        f2 = jnp.zeros((32, 64), F32)
        for s in range(l2_ref.shape[1]):
            v = l2_ref[m, s]
            per = nodes // 8
            at = ((v // per) ^ me) * per + v % per
            f2 = f2 + dot(k2_ref[m, s], top_ref[at])
        hi2, lo2 = split2(f2)
        for n in range(8 * m, 8 * m + 8):
            f1 = dot(t2_ref[32 * n : 32 * n + 32, :], hi2) + dot(t2_ref[32 * n : 32 * n + 32, :], lo2)
            for s in range(l1_ref.shape[1]):
                v = l1_ref[n, s]
                i = jnp.clip(v - start, 0, group - 1)
                at = ((i // nodes) ^ col) * nodes + i % nodes
                term = dot(k1_ref[n, s], coef_ref[at])
                f1 = f1 + jnp.where(v >= 0, term, 0.0)
            hi1, lo1 = split2(f1)
            t1 = t1_ref[256 * n : 256 * n + 256, :]
            leaf = (dot(t1, hi1) + dot(t1, lo1)).astype(BF16)
            chunk = slice(512 * n, 512 * n + 512)
            far = dot(leaf, block_basis(basis_ref[:, chunk]), TN)
            out_ref[:, chunk] = (near_ref[:, chunk] * (NEAR * 64) ** (-0.5) + far).astype(BF16)


def picks():
    a = np.zeros((48, NEAR), np.float32)
    b = np.zeros((48, NEAR), np.float32)
    for dz in range(3):
        for dy in range(3):
            for k in range(4):
                da = (0, 1, None, -1)[k]
                db = (-1, 0, 1, None)[k]
                at = dz * 16 + dy * 4 + k
                if da is not None:
                    a[at, 9 * dz + 3 * dy + da + 1] = 1
                if db is not None:
                    b[at, 9 * dz + 3 * dy + db + 1] = 1
    return jnp.asarray(a, BF16), jnp.asarray(b, BF16)


def doubled(value, axis):
    size = lax.axis_size(axis)
    step = 1
    while step < size:
        other = lax.ppermute(value, axis, [(i, i ^ step) for i in range(size)])
        value = jnp.concatenate([value, other], axis=0)
        step *= 2
    return value


VMEM = pl.BlockSpec(memory_space=pltpu.VMEM)
SMEM = pl.BlockSpec(memory_space=pltpu.SMEM)


def shards(
    charges, points, leaf_basis, transfer_one, transfer_two, couple_one, couple_two, near_list, list_one, list_two
):
    columns = charges.shape[1]
    leaves = near_list.shape[0]
    nodes = leaves // 8
    upper = leaves // 64
    depth = 4 * upper
    rows, cols = lax.axis_size("row"), lax.axis_size("col")
    merge = cols == 2
    t1 = transfer_one.reshape(leaves * 32, 32)
    t2 = transfer_two.reshape(nodes * 32, 32)
    face = jax.ShapeDtypeStruct((80, 2 * depth * 128), BF16)
    params = pltpu.CompilerParams(vmem_limit_bytes=56 * 1024 * 1024)
    outs = pl.pallas_call(
        functools.partial(up_kernel, merge, depth),
        out_shape=[
            jax.ShapeDtypeStruct((16, columns), BF16),
            face,
            jax.ShapeDtypeStruct(((nodes + nodes // 8) * 32, 64), BF16),
        ]
        + ([] if merge else [face]),
        in_specs=[VMEM] * 5,
        out_specs=[VMEM] * (3 if merge else 4),
        compiler_params=params,
        name="up",
    )(charges, points, leaf_basis, t1, t2)
    pb, pay, coef = outs[:3]
    if merge:
        faces = [lax.ppermute(pay, "col", [(0, 1), (1, 0)])]
    else:
        up = [(i, i + 1) for i in range(cols - 1)]
        faces = [
            lax.ppermute(pay, "col", up),
            lax.ppermute(outs[3], "col", [(j, i) for i, j in up]),
        ]
    edge = jax.ShapeDtypeStruct((80, 3 * depth * 128), BF16)
    halo, even, odd = pl.pallas_call(
        functools.partial(pack_kernel, merge, depth),
        out_shape=[jax.ShapeDtypeStruct((80, 4 * depth * 128), BF16), edge, edge],
        in_specs=[VMEM] * (2 + len(faces)),
        out_specs=[VMEM] * 3,
        compiler_params=params,
        name="pack",
    )(charges, pb, *faces)
    even = lax.ppermute(even, "row", [(i, i ^ 1) for i in range(rows)])
    odd = lax.ppermute(odd, "row", [p for i in range(1, rows - 1, 2) for p in ((i, i + 1), (i + 1, i))])
    coef = coef.reshape(1, nodes + nodes // 8, 32, 64)
    coef = doubled(coef, "col")
    ones = coef[:, :nodes].reshape(cols * nodes, 32, 64)
    tops = doubled(coef[:, nodes:].reshape(1, cols * (nodes // 8), 32, 64), "row").reshape(-1, 32, 64)
    pick_a, pick_b = picks()
    return pl.pallas_call(
        functools.partial(near_kernel, depth, cols * nodes),
        out_shape=jax.ShapeDtypeStruct((64, columns), BF16),
        in_specs=[VMEM] * 15 + [SMEM] * 2,
        out_specs=VMEM,
        scratch_shapes=[
            pltpu.VMEM((2, depth * (SIDE + 2), 64, 256), BF16),
            pltpu.VMEM((2, 3 * depth, 256, 128), BF16),
            pltpu.VMEM((2, 32 * (SIDE + 2), 256), F32),
            pltpu.VMEM((128, 512), BF16),
            pltpu.VMEM((48, columns), F32),
            pltpu.VMEM((4, 64, 128), F32),
            pltpu.VMEM((64, columns), F32),
        ],
        compiler_params=params,
        name="near",
    )(
        charges, pb, halo, even, odd, near_list, pick_a, pick_b,
        leaf_basis, t1, t2, couple_one, couple_two, ones, tops, list_one, list_two,
    )


def solution(mesh):
    line, block = P(None, ("row", "col")), P(("row", "col"))
    in_specs = (line, line, line) + (block,) * 7
    return jax.shard_map(shards, mesh=mesh, in_specs=in_specs, out_specs=line, check_vma=False)
```

time: 432 us -> 78.5 us (0.18)
  local copies, waits for them, and re-layouts: 227 us -> 5.38 us
  other arithmetic: 80 us -> 0.8 us
  matrix products: 48.5 us -> 0 us
  Pallas kernels: 0 us -> 45 us
  blocking collectives: 33.5 us -> 0 us
  loops' own time: 13.2 us -> 0 us
  starting transfers between devices: 22.2 us -> 12.5 us
  waiting for transfers between devices: 5.1 us -> 14.5 us
    while x224 -> x0, local copies, waits for them, and re-layouts: 137 us -> none
    reduce_sum x4 -> x0, other arithmetic: 74.7 us -> none  [leaf_block(): jnp.sum(distance * distance, axis=2) + softening]
    reshape x12 -> x0, local copies, waits for them, and re-layouts: 53.7 us -> none  [the longest x4 43.7 us: near_step(): jnp.stack(value_list, axis=2).reshape(block_leaves, 27, rhs_count, per_leaf)]
    dot_general x11 -> x0, matrix products: 48.5 us -> none  [the longest x4 40.6 us: leaf_block(): jnp.einsum('lsij,lsrj->lri', kernel, values, preferred_element_type=jnp.f...]
    pallas_call x0 -> x3, Pallas kernels: none -> 45 us  [the longest x1 38.1 us: shards(): pl.pallas_call(functools.partial(near_kernel, depth, cols * nodes), out_s...]
    all_gather x3 -> x0, blocking collectives: 33.5 us -> none  [the longest x1 24.2 us: shards(): every_top = lax.all_gather(group_top, 'row', axis=0, tiled=True)]
    another operation x1 -> x0, loops' own time: 13.2 us -> none  [shards(): near_layers = lax.map(near_step, jnp.arange(depth_z, dtype=jnp.int32))]
    ppermute x8, starting transfers between devices: 22.2 us -> 12.5 us  [the longest x5 11.8 us: doubled(): other = lax.ppermute(value, axis, [(i, i ^ step) for i in range(size)])]
  transfers between devices with their start and end apart: 8 -> 8, of which waited for: 2 -> 4; matrix products, arithmetic and copies ran while one was open for 5% -> 3% of each run, Pallas kernels for 0% -> 3%
where the time goes in v1:
time: 78.5 us; the launch traced here: 78.3 us
  Pallas kernels  45 us (57%)
  waiting for transfers between devices  14.5 us (18%)
  starting transfers between devices  12.5 us (16%)
  local copies, waits for them, and re-layouts  5.38 us (7%)
  other arithmetic  0.8 us (1%)
    pallas_call x1, Pallas kernels, shards(): pl.pallas_call(functools.partial(near_kernel, depth, cols * nodes), out_s...  38.1 us
    ppermute x5, waiting for transfers between devices, doubled(): other = lax.ppermute(value, axis, [(i, i ^ step) for i in range(size)])  14.4 us
    ppermute x5, starting transfers between devices, doubled(): other = lax.ppermute(value, axis, [(i, i ^ step) for i in range(size)])  11.8 us
    unnamed x17, local copies, waits for them, and re-layouts  4.71 us
    pallas_call x1, Pallas kernels, shards(): pl.pallas_call(functools.partial(up_kernel, merge, depth), out_shape=[jax...  4.58 us
    pallas_call x1, Pallas kernels, shards(): pl.pallas_call(functools.partial(pack_kernel, merge, depth), out_shape=[j...  2.3 us
  transfers between devices with their start and end apart: 8, of which 4 were waited for; matrix products, arithmetic and copies ran while one was open for 3% of the time, Pallas kernels for 3%

profile of v1, /device:TPU:0, one launch (start us, length us, event | category | flops | bytes accessed | tf_op | source)
XLA Modules:
  0.0 78.3 jit_solution(8408685165371381377)
XLA Ops:
  0.0 2.5 %copy.13 = bf16[64,32,32]{2,1,0:T(8,128)(2,1)} copy(bf16[64,32,32]{0,2,1:T(8,128)(2,1)} %param.15) | data formatting | bytes 262144 | tf_op args[3]
  2.5 4.6 %up.1 = (bf16[16,4096]{1,0:T(8,128)(2,1)}, bf16[80,1024]{1,0:T(8,128)(2,1)}, bf16[288,64]{1,0:T(8,128)(2,1)}) custom-call(bf16[64,4096]{1,0:T(8,128)(2,1)} %q_ref.5, f32[3,4096]{1,0:T(4,128)} %pts_ref.1, bf16[32,4096]{1,0:T(8,128)(2,1)} %basis_ref.3, bf16[2048,32]{1,0:T(8,128)(2,1)} %bitcast.10, bf16[256,32]{1,0:T(8,128)(2,1)} %bitcast.17), custom_call_target="tpu_custom_call" | custom-call | tf_op jit(solution)/shard_map/up/pallas_call | solution.py:331
  7.0 3.0 %collective-permute-start.3 = (bf16[1,9,32,64]{3,2,0,1:T(8,128)(2,1)}, bf16[1,9,32,64]{3,2,0,1:T(8,128)(2,1)S(1)}, u32[]{:S(2)}, u32[]{:S(2)}) collective-permute-start(bf16[1,9,32,64]{3,2,0,1:T(8,128)(2,1)} %bitcast.14), channel_id=1, source_target_pairs={{0,1},{1,0},{2,3},{3,2},{4,5},{5,4},{6,7},{7,6},{8,9},{9,8},{10,11... | collective-permute-start | bytes 110600 | tf_op jit(solution)/shard_map/ppermute | solution.py:307
  10.0 0.0 collective-permute-start
  10.0 0.0 copy-done.5
  10.0 0.7 copy.17.nl_ref
  10.7 2.2 %collective-permute-done.3 = bf16[1,9,32,64]{3,2,0,1:T(8,128)(2,1)S(1)} collective-permute-done((bf16[1,9,32,64]{3,2,0,1:T(8,128)(2,1)}, bf16[1,9,32,64]{3,2,0,1:T(8,128)(2,1)S(1)}, u32[]{:S(2)}, u32[]{:S(2)}) %collective-permute-start.3) | collective-permute-done | bytes 36896 | tf_op jit(solution)/shard_map/ppermute | solution.py:307
  13.0 0.7 constant_dynamic-update-slice_fusion.4
  13.7 0.1 collective-permute-start.4
  13.8 0.0 copy-done.1
  13.8 0.7 copy.16
  14.5 0.5 collective-permute-done.4
  15.0 2.4 %collective-permute-start.5 = (bf16[2,2,32,64]{3,2,1,0:T(8,128)(2,1)S(1)}, bf16[2,2,32,64]{3,2,1,0:T(8,128)(2,1)S(1)}, u32[]{:S(2)}, u32[]{:S(2)}) collective-permute-start(bf16[2,2,32,64]{3,2,1,0:T(8,128)(2,1)S(1)} %pad_maximum_fusion.2), channel_id=1, source_target_pairs={{0,4},{2,6},{4,0},{6,2},{8,12},{10,14},{12,8},{14,10},{16,20},{18,... | collective-permute-start | bytes 49160 | tf_op jit(solution)/shard_map/ppermute | solution.py:307
  17.3 1.9 %collective-permute-done.5 = bf16[2,2,32,64]{3,2,1,0:T(8,128)(2,1)S(1)} collective-permute-done((bf16[2,2,32,64]{3,2,1,0:T(8,128)(2,1)S(1)}, bf16[2,2,32,64]{3,2,1,0:T(8,128)(2,1)S(1)}, u32[]{:S(2)}, u32[]{:S(2)}) %collective-permute-start.5) | collective-permute-done | bytes 16416 | tf_op jit(solution)/shard_map/ppermute | solution.py:307
  19.3 2.1 %collective-permute-start.6 = (bf16[4,2,32,64]{3,2,1,0:T(8,128)(2,1)S(1)}, bf16[4,2,32,64]{3,2,1,0:T(8,128)(2,1)S(1)}, u32[]{:S(2)}, u32[]{:S(2)}) collective-permute-start(bf16[4,2,32,64]{3,2,1,0:T(8,128)(2,1)S(1)} %pad_maximum_fusion.1), channel_id=1, source_target_pairs={{0,8},{2,10},{4,12},{6,14},{8,0},{10,2},{12,4},{14,6},{16,24},{18,... | collective-permute-start | bytes 98312 | tf_op jit(solution)/shard_map/ppermute | solution.py:307
  21.4 0.0 collective-permute-done.refs_0_
  21.4 0.7 copy-done.4
  22.1 2.3 %pack.1 = (bf16[80,2048]{1,0:T(8,128)(2,1)}, bf16[80,1536]{1,0:T(8,128)(2,1)}, bf16[80,1536]{1,0:T(8,128)(2,1)}) custom-call(bf16[64,4096]{1,0:T(8,128)(2,1)} %q_ref.5, bf16[16,4096]{1,0:T(8,128)(2,1)} %get-tuple-element.11.pb_ref, bf16[80,1024]{1,0:T(8,128)(2,1)} %copy-done.4), custom_call_target="tpu_custom_call" | custom-call | tf_op jit(solution)/shard_map/pack/pallas_call | solution.py:354
  24.4 0.0 collective-permute-start.1
  24.4 0.7 collective-permute-start.2
  25.1 0.0 collective-permute-done.6
  25.1 4.3 %collective-permute-start.7 = (bf16[8,2,32,64]{3,2,1,0:T(8,128)(2,1)S(1)}, bf16[8,2,32,64]{3,2,1,0:T(8,128)(2,1)S(1)}, u32[]{:S(2)}, u32[]{:S(2)}) collective-permute-start(bf16[8,2,32,64]{3,2,1,0:T(8,128)(2,1)S(1)} %pad_maximum_fusion), channel_id=1, source_target_pairs={{0,16},{2,18},{4,20},{6,22},{8,24},{10,26},{12,28},{14,30},{16,0},... | collective-permute-start | bytes 196616 | tf_op jit(solution)/shard_map/ppermute | solution.py:307
  29.4 9.8 %collective-permute-done.7 = bf16[8,2,32,64]{3,2,1,0:T(8,128)(2,1)S(1)} collective-permute-done((bf16[8,2,32,64]{3,2,1,0:T(8,128)(2,1)S(1)}, bf16[8,2,32,64]{3,2,1,0:T(8,128)(2,1)S(1)}, u32[]{:S(2)}, u32[]{:S(2)}) %collective-permute-start.7) | collective-permute-done | bytes 65568 | tf_op jit(solution)/shard_map/ppermute | solution.py:307
  39.3 0.0 copy-start
  39.3 0.0 collective-permute-done.1.even_ref
  39.3 0.0 copy-start.2
  39.3 0.0 collective-permute-done.2.odd_ref
  39.3 0.0 copy-start.3
  39.3 0.6 copy-done
  40.0 0.1 copy-done.2
  40.1 0.1 copy-done.3
  40.2 38.1 %near.1 = bf16[64,4096]{1,0:T(8,128)(2,1)} custom-call(bf16[64,4096]{1,0:T(8,128)(2,1)} %q_ref.5, bf16[16,4096]{1,0:T(8,128)(2,1)} %get-tuple-element.11.pb_ref, bf16[80,2048]{1,0:T(8,128)(2,1)} %get-tuple-element.13.h_ref, bf16[80,1536]{1,0:T(8,128)(2,1)} %copy-done.2, bf16[80,1536]{1,0:T(8,128)(2,1)} %copy-done.3, s32[64,27]{1,0:T(8,128)} %copy.17.nl_ref, ...), custom_call_target="tpu_custom_call" | custom-call | tf_op jit(solution)/shard_map/near/pallas_call | solution.py:369
  (11 shorter events, 0.1 us)
Async XLA Ops:
  2.5 7.6 %copy-start.5 = (s32[64,27]{0,1:T(8,128)S(1)}, s32[64,27]{0,1:T(8,128)}, u32[]{:S(2)}) copy-start(s32[64,27]{0,1:T(8,128)} %param.19) | copy-start | bytes 20740
  7.0 5.9 %collective-permute-start.3 = (bf16[1,9,32,64]{3,2,0,1:T(8,128)(2,1)}, bf16[1,9,32,64]{3,2,0,1:T(8,128)(2,1)S(1)}, u32[]{:S(2)}, u32[]{:S(2)}) collective-permute-start(bf16[1,9,32,64]{3,2,0,1:T(8,128)(2,1)} %bitcast.14), channel_id=1, source_target_pairs={{0,1},{1,0},{2,3},{3,2},{4,5},{5,4},{6,7},{7,6},{8,9},{9,8},{10,11... | collective-permute-start | bytes 110600 | tf_op jit(solution)/shard_map/ppermute | solution.py:307
  10.0 11.4 %collective-permute-start = (bf16[80,1024]{1,0:T(8,128)(2,1)}, bf16[80,1024]{1,0:T(8,128)(2,1)S(1)}, u32[]{:S(2)}, u32[]{:S(2)}) collective-permute-start(bf16[80,1024]{1,0:T(8,128)(2,1)} %get-tuple-element.12), channel_id=1, source_target_pairs={{0,1},{1,0},{2,3},{3,2},{4,5},{5,4},{6,7},{7,6},{8,9},{9,8},{10,11... | collective-permute-start | bytes 491528 | tf_op jit(solution)/shard_map/ppermute | solution.py:346
  10.7 3.0 %copy-start.1 = (bf16[288,64]{1,0:T(8,128)(2,1)S(1)}, bf16[288,64]{1,0:T(8,128)(2,1)}, u32[]{:S(2)}) copy-start(bf16[288,64]{1,0:T(8,128)(2,1)} %get-tuple-element.16) | copy-start | bytes 110596
  13.7 1.2 %collective-permute-start.4 = (bf16[1,2,32,64]{3,2,1,0:T(8,128)(2,1)S(1)}, bf16[1,2,32,64]{3,2,1,0:T(8,128)(2,1)S(1)}, u32[]{:S(2)}, u32[]{:S(2)}) collective-permute-start(bf16[1,2,32,64]{3,2,1,0:T(8,128)(2,1)S(1)} %get-tuple-element.18), channel_id=1, source_target_pairs={{0,2},{2,0},{4,6},{6,4},{8,10},{10,8},{12,14},{14,12},{16,18},{18,... | collective-permute-start | bytes 24584 | tf_op jit(solution)/shard_map/ppermute | solution.py:307
  15.0 4.3 %collective-permute-start.5 = (bf16[2,2,32,64]{3,2,1,0:T(8,128)(2,1)S(1)}, bf16[2,2,32,64]{3,2,1,0:T(8,128)(2,1)S(1)}, u32[]{:S(2)}, u32[]{:S(2)}) collective-permute-start(bf16[2,2,32,64]{3,2,1,0:T(8,128)(2,1)S(1)} %pad_maximum_fusion.2), channel_id=1, source_target_pairs={{0,4},{2,6},{4,0},{6,2},{8,12},{10,14},{12,8},{14,10},{16,20},{18,... | collective-permute-start | bytes 49160 | tf_op jit(solution)/shard_map/ppermute | solution.py:307
  19.3 5.8 %collective-permute-start.6 = (bf16[4,2,32,64]{3,2,1,0:T(8,128)(2,1)S(1)}, bf16[4,2,32,64]{3,2,1,0:T(8,128)(2,1)S(1)}, u32[]{:S(2)}, u32[]{:S(2)}) collective-permute-start(bf16[4,2,32,64]{3,2,1,0:T(8,128)(2,1)S(1)} %pad_maximum_fusion.1), channel_id=1, source_target_pairs={{0,8},{2,10},{4,12},{6,14},{8,0},{10,2},{12,4},{14,6},{16,24},{18,... | collective-permute-start | bytes 98312 | tf_op jit(solution)/shard_map/ppermute | solution.py:307
  21.4 0.7 copy-start.4
  24.4 14.9 %collective-permute-start.1 = (bf16[80,1536]{1,0:T(8,128)(2,1)}, bf16[80,1536]{1,0:T(8,128)(2,1)S(1)}, u32[]{:S(2)}, u32[]{:S(2)}) collective-permute-start(bf16[80,1536]{1,0:T(8,128)(2,1)} %get-tuple-element.14), channel_id=1, source_target_pairs={{0,2},{2,0},{4,6},{6,4},{8,10},{10,8},{12,14},{14,12},{16,18},{18,... | collective-permute-start | bytes 737288 | tf_op jit(solution)/shard_map/ppermute | solution.py:362
  24.4 14.9 %collective-permute-start.2 = (bf16[80,1536]{1,0:T(8,128)(2,1)}, bf16[80,1536]{1,0:T(8,128)(2,1)S(1)}, u32[]{:S(2)}, u32[]{:S(2)}) collective-permute-start(bf16[80,1536]{1,0:T(8,128)(2,1)} %get-tuple-element.15), channel_id=1, source_target_pairs={{2,4},{4,2},{6,8},{8,6},{10,12},{12,10},{14,16},{16,14},{18,20},{2... | collective-permute-start | bytes 737288 | tf_op jit(solution)/shard_map/ppermute | solution.py:363
  25.1 14.1 %collective-permute-start.7 = (bf16[8,2,32,64]{3,2,1,0:T(8,128)(2,1)S(1)}, bf16[8,2,32,64]{3,2,1,0:T(8,128)(2,1)S(1)}, u32[]{:S(2)}, u32[]{:S(2)}) collective-permute-start(bf16[8,2,32,64]{3,2,1,0:T(8,128)(2,1)S(1)} %pad_maximum_fusion), channel_id=1, source_target_pairs={{0,16},{2,18},{4,20},{6,22},{8,24},{10,26},{12,28},{14,30},{16,0},... | collective-permute-start | bytes 196616 | tf_op jit(solution)/shard_map/ppermute | solution.py:307
  39.3 0.7 copy-start
  39.3 0.8 %copy-start.2 = (bf16[80,1536]{1,0:T(8,128)(2,1)}, bf16[80,1536]{1,0:T(8,128)(2,1)S(1)}, u32[]{:S(2)}) copy-start(bf16[80,1536]{1,0:T(8,128)(2,1)S(1)} %collective-permute-done.1.even_ref) | copy-start | bytes 737284
  39.3 0.9 %copy-start.3 = (bf16[80,1536]{1,0:T(8,128)(2,1)}, bf16[80,1536]{1,0:T(8,128)(2,1)S(1)}, u32[]{:S(2)}) copy-start(bf16[80,1536]{1,0:T(8,128)(2,1)S(1)} %collective-permute-done.2.odd_ref) | copy-start | bytes 737284

commit v2 on v1

v2 whole, which is shorter than its diff:
```python
import functools

import jax
import jax.numpy as jnp
import numpy as np
from jax import lax
from jax.experimental import pallas as pl
from jax.experimental.pallas import tpu as pltpu
from jax.sharding import PartitionSpec as P

NEAR = 27
SIDE = 4
SOFTENING = 0.0025
F32 = jnp.float32
BF16 = jnp.bfloat16
NT = (((1,), (1,)), ((), ()))
TN = (((0,), (0,)), ((), ()))
NN = (((1,), (0,)), ((), ()))
VMEM = pl.BlockSpec(memory_space=pltpu.VMEM)
SMEM = pl.BlockSpec(memory_space=pltpu.SMEM)


def dot(a, b, dims=NN):
    return lax.dot_general(a, b, dims, preferred_element_type=F32)


def split2(v):
    hi = v.astype(BF16)
    lo = (v - hi.astype(F32)).astype(BF16)
    return hi, lo


def tile_of(z, y, x1):
    return (z // 4) * 32 + (z // 2 % 2) * 16 + (y // 2) * 8 + x1 * 4 + (z % 2) * 2 + (y % 2)


def lower_half(shape):
    return lax.broadcasted_iota(jnp.int32, shape, len(shape) - 1) % 128 < 64


def swap_matrix():
    a = lax.broadcasted_iota(jnp.int32, (128, 128), 0)
    b = lax.broadcasted_iota(jnp.int32, (128, 128), 1)
    return jnp.where((a + 64) % 128 == b, 1.0, 0.0).astype(BF16)


def block_basis(basis):
    rank, width = basis.shape
    leaf = lax.broadcasted_iota(jnp.int32, (rank, width), 1) // 64
    zero = jnp.zeros_like(basis)
    return jnp.concatenate([jnp.where(leaf == k, basis, zero) for k in range(8)], axis=0)


def feature_rows(x):
    pairs = [split2(v) for v in x]
    hi = [a.astype(F32) for a, _ in pairs]
    lo = [b.astype(F32) for _, b in pairs]
    y = [a + b for a, b in zip(hi, lo)]
    norm = y[0] * y[0] + y[1] * y[1] + y[2] * y[2]
    n1 = norm.astype(BF16).astype(F32)
    n2 = (norm - n1).astype(BF16).astype(F32)
    n3 = norm - n1 - n2
    width = norm.shape[1]
    index = lax.broadcasted_iota(jnp.int32, (16, width), 0)
    out = jnp.where(index == 9, 1.0, 0.0)
    for k, piece in enumerate(hi + lo + [n1, n2, n3]):
        out = jnp.where(index == k, piece, out)
    return out.astype(BF16)


def with_ones(rows):
    index = lax.broadcasted_iota(jnp.int32, rows.shape, 0)
    return jnp.where(index == 9, jnp.ones_like(rows), rows)


def coordinates(rows):
    return [rows[c : c + 1].astype(F32) + rows[c + 3 : c + 4].astype(F32) for c in range(3)]


def up_kernel(merge, depth, q_ref, pts_ref, basis_ref, t1_ref, t2_ref, feat_ref, xpay_ref, coef_ref, *more):
    row, col = lax.axis_index("row"), lax.axis_index("col")
    columns = q_ref.shape[1]
    nodes = columns // 512
    centre = (
        (SIDE * col + SIDE // 2).astype(F32),
        (SIDE * row + SIDE // 2).astype(F32),
        jnp.float32(depth / 2),
    )
    local = [pts_ref[c : c + 1, :] - centre[c] for c in range(3)]
    feat_ref[...] = feature_rows(local)
    pair_x = lax.broadcasted_iota(jnp.int32, (1, columns), 1) // 512 % 2
    shift = jnp.where(pair_x == 1, -float(SIDE), float(SIDE))
    moved = feature_rows([local[0] + shift, local[1], local[2]])
    swap = swap_matrix()
    low = lower_half((80, 128))
    for z in range(depth):
        for y1 in range(2):
            out = z * 2 + y1

            def tile(y, x1):
                at = tile_of(z, y, x1) * 128
                return jnp.concatenate([q_ref[:, at : at + 128], moved[:, at : at + 128]], axis=0)

            high = jnp.where(low, dot(tile(2 * y1, 1), swap).astype(BF16), tile(2 * y1 + 1, 1))
            base = jnp.where(low, tile(2 * y1, 0), dot(tile(2 * y1 + 1, 0), swap).astype(BF16))
            if merge:
                xpay_ref[:, out * 128 : out * 128 + 128] = jnp.where(col == 0, high, base)
            else:
                xpay_ref[:, out * 128 : out * 128 + 128] = high
                more[0][:, out * 128 : out * 128 + 128] = base
    ones = []
    for n in range(nodes):
        chunk = slice(512 * n, 512 * n + 512)
        leaf = dot(block_basis(basis_ref[:, chunk]), q_ref[:, chunk], NT).astype(BF16)
        ones.append(dot(t1_ref[256 * n : 256 * n + 256, :], leaf, TN).astype(BF16))
    tops = []
    for m in range(nodes // 8):
        part = jnp.concatenate(ones[8 * m : 8 * m + 8], axis=0)
        tops.append(dot(t2_ref[256 * m : 256 * m + 256, :], part, TN).astype(BF16))
    if merge:
        for k in range(nodes // 2):
            coef_ref[32 * k : 32 * k + 32, :] = jnp.concatenate([ones[2 * k], ones[2 * k + 1]], axis=1)
        for m, top in enumerate(tops):
            at = 16 * nodes + 32 * m
            coef_ref[at : at + 32, :] = jnp.concatenate([top, top], axis=1)
        at = 2 * depth * 128
        for k in range(coef_ref.shape[0] // 80):
            xpay_ref[:, at + 128 * k : at + 128 * k + 128] = coef_ref[80 * k : 80 * k + 80, :]
    else:
        for k, value in enumerate(ones + tops):
            coef_ref[32 * k : 32 * k + 32, :] = value


def pack_kernel(merge, depth, q_ref, feat_ref, *refs):
    if merge:
        coef_ref, xr_ref, h_ref, even_ref, odd_ref, one_ref = refs
    else:
        xl_ref, xr_ref, h_ref, even_ref, odd_ref = refs
    row, col = lax.axis_index("row"), lax.axis_index("col")
    swap = swap_matrix()
    low = lower_half((80, 128))
    for z in range(depth):
        for y1 in range(2):
            at = (z * 2 + y1) * 128
            right = xr_ref[:, at : at + 128]
            left = right if merge else xl_ref[:, at : at + 128]
            turned = dot(right, swap).astype(BF16)
            h0 = jnp.where(low, right, turned if merge else dot(left, swap).astype(BF16))
            h1 = jnp.where(low, turned, left)
            at = (z * 4 + 2 * y1) * 128
            h_ref[:, at : at + 128] = h0
            h_ref[:, at + 128 : at + 256] = h1
    even = row % 2 == 0
    for pay, last_first in ((even_ref, even), (odd_ref, jnp.logical_not(even))):
        width = 3 * depth * 128
        for z in range(depth):
            for k in range(3):
                ends = []
                for y in (0, SIDE - 1):
                    if k < 2:
                        at = tile_of(z, y, k) * 128
                        ends.append((q_ref[:, at : at + 128], feat_ref[:, at : at + 128]))
                    else:
                        at = (z * 4 + y) * 128
                        ends.append((h_ref[0:64, at : at + 128], h_ref[64:80, at : at + 128]))
                at = (z * 3 + k) * 128
                pay[0:64, at : at + 128] = jnp.where(last_first, ends[1][0], ends[0][0])
                pay[64:80, at : at + 128] = jnp.where(last_first, ends[1][1], ends[0][1])
        x = coordinates(pay[64:80, 0:width].astype(F32))
        shift = jnp.where(last_first, -float(SIDE), float(SIDE))
        pay[64:80, 0:width] = feature_rows([x[0], x[1] + shift, x[2]])
    if merge:
        nodes = one_ref.shape[0] // 2
        width = 3 * depth * 128
        base = 2 * depth * 128
        got = jnp.concatenate(
            [xr_ref[:, base + 128 * k : base + 128 * k + 128] for k in range(coef_ref.shape[0] // 80)], axis=0
        )
        for side, value in enumerate((coef_ref[...], got)):
            for k in range(nodes // 2):
                block = value[32 * k : 32 * k + 32, :]
                one_ref[side * nodes + 2 * k] = block[:, 0:64]
                one_ref[side * nodes + 2 * k + 1] = block[:, 64:128]
        at = 16 * nodes
        even_ref[:, width : width + 128] = jnp.zeros((80, 128), BF16)
        own, other = coef_ref[at : at + 32, :], got[at : at + 32, :]
        even_ref[0:32, width : width + 128] = jnp.where(lower_half((32, 128)), own, other)


def scan_sources(depth, jobs_of, x_ref, mask_ref, acc_ref):
    def pair(xp, carry):
        add_all([job for sz in range(depth) for job in jobs_of(xp, sz)], depth, xp, x_ref, mask_ref, acc_ref)
        return carry

    lax.fori_loop(0, 2, pair, 0)


def pieces(ye):
    tiles = list(range(max(ye - 2, 0), min(ye, SIDE - 1) + 1))
    return [tiles[k : k + 2] for k in range(0, len(tiles), 2)]


def mask_row(mask_ref, at, dz, dy, k, ty):
    row = dz * 16 + dy * 4 + k
    m = mask_ref[at, row : row + 1, 128 * ty : 128 * ty + 128]
    m = jnp.broadcast_to(m, (16, 128)).astype(BF16)
    return jnp.concatenate([m] * 4, axis=0)


AHEAD = 2


def add_all(jobs, depth, xp, x_ref, mask_ref, acc_ref):
    steps = []
    for sz, ye, tiles, rows, charge, sides in jobs:
        for dz in range(3):
            if 0 <= sz + 1 - dz < depth:
                steps.append((xp * depth + sz + 1 - dz, dz, ye, tiles, rows, charge, sides))
    ready = []
    for i in range(len(steps) + AHEAD):
        if i < len(steps):
            at, dz, ye, tiles, rows, charge, sides = steps[i]
            lanes = slice(128 * tiles[0], 128 * tiles[-1] + 128)
            features = x_ref[at, 32:96, lanes] if sides else x_ref[at, 0:32, lanes]
            ready.append(lax.rsqrt(dot(rows(), features).astype(BF16)))
        if i >= AHEAD:
            at, dz, ye, tiles, rows, charge, sides = steps[i - AHEAD]
            inv = ready[i - AHEAD]
            ready[i - AHEAD] = None
            lanes = slice(128 * tiles[0], 128 * tiles[-1] + 128)
            blocks = []
            for j, ty in enumerate(tiles):
                part = inv[:, 128 * j : 128 * j + 128]
                halves = [part, part] if sides else [part[0:64], part[64:128]]
                first = 2 if sides else 0
                masked = [h * mask_row(mask_ref, at, dz, ye - ty, first + k, ty) for k, h in enumerate(halves)]
                blocks.append(jnp.concatenate(masked, axis=0))
            acc_ref[at, :, lanes] += dot(charge(), jnp.concatenate(blocks, axis=1))


def own_kernel(depth, q_ref, feat_ref, nl_ref, sel_ref, sel_x_ref, pick_ref, acc_ref, x_ref, mask_ref, yt_ref):
    columns = q_ref.shape[1]
    leaves = columns // 64
    x = dot(sel_x_ref[...], feat_ref[...])
    active = jnp.where(nl_ref[...] >= 0, 1.0, 0.0).astype(BF16)
    pick = dot(pick_ref[...], active, NT)
    pick = jnp.where(
        lax.broadcasted_iota(jnp.int32, (48, leaves), 1) % 2 == 0, pick[0:48], pick[48:96]
    ).astype(BF16)
    spread = jnp.where(
        lax.broadcasted_iota(jnp.int32, (leaves, columns), 0)
        == lax.broadcasted_iota(jnp.int32, (leaves, columns), 1) // 64,
        1.0,
        0.0,
    ).astype(BF16)
    masks = dot(pick, spread)
    low = lower_half((32, 128))
    for z in range(depth):
        for xp in range(2):
            for y in range(SIDE):
                at = tile_of(z, y, xp) * 128
                lanes = slice(128 * y, 128 * y + 128)
                tile = x[:, at : at + 128]
                x_ref[xp * depth + z, 0:32, lanes] = tile.astype(BF16)
                x_ref[xp * depth + z, 32:64, lanes] = jnp.where(low, 0.0, tile).astype(BF16)
                x_ref[xp * depth + z, 64:96, lanes] = jnp.where(low, tile, 0.0).astype(BF16)
                mask_ref[xp * depth + z, :, lanes] = masks[:, at : at + 128]
                rows = dot(feat_ref[:, at : at + 128], sel_ref[:, 0:32], TN)
                yt_ref[(xp * depth + z) * SIDE + y] = rows.astype(BF16)
    acc_ref[...] = jnp.zeros_like(acc_ref)

    def jobs_of(xp, sz):
        jobs = []
        for ye in range(1, SIDE + 1):
            base = pl.multiple_of(tile_of(sz, ye - 1, xp) * 128, 128)

            def charge(base=base):
                return q_ref[:, pl.ds(base, 128)]

            def rows(k=(xp * depth + sz) * SIDE + ye - 1):
                return yt_ref[k]

            jobs += [(sz, ye, tiles, rows, charge, False) for tiles in pieces(ye)]
        return jobs

    scan_sources(depth, jobs_of, x_ref, mask_ref, acc_ref)


def beside(right, left):
    return jnp.concatenate([right, left], axis=1)


def side_kernel(depth, q_ref, h_ref, sel_ref, x_ref, mask_ref, yt_ref, in_ref, acc_ref, c_ref, ys_ref):
    low = lower_half((64, 128))
    for z in range(depth):
        for y in range(SIDE):
            t = [q_ref[:, a * 128 : a * 128 + 128] for a in (tile_of(z, y, 0), tile_of(z, y, 1))]
            h = h_ref[:, (z * SIDE + y) * 128 : (z * SIDE + y) * 128 + 128]
            even, odd = z * SIDE + y, (depth + z) * SIDE + y
            c_ref[even] = jnp.where(low, t[1], h[0:64])
            c_ref[odd] = jnp.where(low, h[0:64], t[0])
            rows = dot(with_ones(h[64:80]), sel_ref[:, 0:32], TN).astype(BF16)
            ys_ref[even] = beside(yt_ref[odd, 0:64], rows[64:128])
            ys_ref[odd] = beside(rows[0:64], yt_ref[even, 64:128])

    def jobs_of(xp, sz):
        jobs = []
        for ye in range(1, SIDE + 1):
            k = (xp * depth + sz) * SIDE + ye - 1

            def charge(k=k):
                return c_ref[k]

            def rows(k=k):
                return ys_ref[k]

            jobs += [(sz, ye, tiles, rows, charge, True) for tiles in pieces(ye)]
        return jobs

    scan_sources(depth, jobs_of, x_ref, mask_ref, acc_ref)


def edge_kernel(depth, even_ref, odd_ref, sel_ref, x_ref, mask_ref, in_ref, acc_ref, c_ref, cs_ref, yt_ref, ys_ref):
    even = lax.axis_index("row") % 2 == 0
    low = lower_half((80, 128))
    for z in range(depth):
        for side in range(2):
            t = []
            for k in range(3):
                at = (z * 3 + k) * 128
                a, b = even_ref[:, at : at + 128], odd_ref[:, at : at + 128]
                t.append(jnp.where(even, b, a) if side == 0 else jnp.where(even, a, b))
            rows = [dot(with_ones(v[64:80]), sel_ref[:, 0:32], TN).astype(BF16) for v in t]
            even_k, odd_k = z * 2 + side, (depth + z) * 2 + side
            c_ref[even_k], c_ref[odd_k] = t[0][0:64], t[1][0:64]
            yt_ref[even_k], yt_ref[odd_k] = rows[0], rows[1]
            cs_ref[even_k] = jnp.where(low, t[1], t[2])[0:64]
            cs_ref[odd_k] = jnp.where(low, t[2], t[0])[0:64]
            ys_ref[even_k] = beside(rows[1][0:64], rows[2][64:128])
            ys_ref[odd_k] = beside(rows[2][0:64], rows[0][64:128])

    def jobs_of(xp, sz):
        jobs = []
        for side, ye in enumerate((0, SIDE + 1)):
            k = (xp * depth + sz) * 2 + side
            tiles = [0] if side == 0 else [SIDE - 1]
            for sides, r_ref, q_ref in ((False, yt_ref, c_ref), (True, ys_ref, cs_ref)):

                def charge(q_ref=q_ref, k=k):
                    return q_ref[k]

                def rows(r_ref=r_ref, k=k):
                    return r_ref[k]

                jobs.append((sz, ye, tiles, rows, charge, sides))
        return jobs

    scan_sources(depth, jobs_of, x_ref, mask_ref, acc_ref)


def couple_kernel(group, k1_ref, coef_ref, l1_ref, out_ref):
    row, col = lax.axis_index("row"), lax.axis_index("col")
    nodes, slots = l1_ref.shape
    start = row * group
    for n in range(nodes):
        total = jnp.zeros((32, 64), F32)
        for s in range(slots):
            v = l1_ref[n, s]
            i = jnp.clip(v - start, 0, group - 1)
            at = ((i // nodes) ^ col) * nodes + i % nodes
            partner = coef_ref[at]
            partner = jnp.where(v >= 0, partner, jnp.zeros_like(partner))
            total = total + dot(k1_ref[n, s], partner)
        out_ref[32 * n : 32 * n + 32, :] = total


def down_kernel(depth, wide, acc_ref, f1_ref, basis_ref, t1_ref, t2_ref, k2_ref, top_ref, l2_ref, out_ref, top_scr):
    row, col = lax.axis_index("row"), lax.axis_index("col")
    nodes = out_ref.shape[1] // 512
    per = nodes // 8
    me = row * lax.axis_size("col") + col
    if wide:
        for k in range(top_ref.shape[0]):
            top_scr[2 * k] = top_ref[k][:, 0:64]
            top_scr[2 * k + 1] = top_ref[k][:, 64:128]
    else:
        top_scr[...] = top_ref[...]
    for m in range(per):
        f2 = jnp.zeros((32, 64), F32)
        for s in range(l2_ref.shape[1]):
            v = l2_ref[m, s]
            at = ((v // per) ^ me) * per + v % per
            f2 = f2 + dot(k2_ref[m, s], top_scr[at])
        hi2, lo2 = split2(f2)
        t2 = t2_ref[256 * m : 256 * m + 256, :]
        down = f1_ref[256 * m : 256 * m + 256, :] + dot(t2, hi2) + dot(t2, lo2)
        hi1, lo1 = split2(down)
        for j in range(8):
            n = 8 * m + j
            t1 = t1_ref[256 * n : 256 * n + 256, :]
            rows = slice(32 * j, 32 * j + 32)
            leaf = (dot(t1, hi1[rows]) + dot(t1, lo1[rows])).astype(BF16)
            chunk = slice(512 * n, 512 * n + 512)
            far = dot(leaf, block_basis(basis_ref[:, chunk]), TN)
            z1, y1, x1 = j // 4, j // 2 % 2, j % 2
            for k in range(4):
                z, y = 4 * m + 2 * z1 + k // 2, 2 * y1 + k % 2
                part = acc_ref[x1 * depth + z, :, 128 * y : 128 * y + 128]
                total = part * (NEAR * 64) ** (-0.5) + far[:, 128 * k : 128 * k + 128]
                out_ref[:, 512 * n + 128 * k : 512 * n + 128 * k + 128] = total.astype(BF16)


def constants():
    sel = np.zeros((16, 160), np.float32)
    sel_x = np.zeros((32, 16), np.float32)
    rest, eps = np.float32(SOFTENING), []
    for _ in range(3):
        eps.append(np.asarray(rest).astype(jnp.bfloat16).astype(np.float32))
        rest = np.float32(rest - eps[-1])
    for f in range(21):
        source = f if f < 6 else f - 6 if f < 12 else 9 if f < 15 else f - 9 if f < 18 else 9
        for base in (0, 32, 128):
            sel[source, base + f] = 1
        if f < 12:
            sel_x[f, f % 3 + (3 if f >= 6 else 0)] = -2
        elif f < 15:
            sel_x[f, f - 6] = 1
        else:
            sel_x[f, 9] = 1 if f < 18 else eps[f - 18]
    pick = np.zeros((96, NEAR), np.float32)
    for dz in range(3):
        for dy in range(3):
            for k in range(4):
                for half, dx in enumerate(((0, 1, None, -1)[k], (-1, 0, 1, None)[k])):
                    if dx is not None:
                        pick[48 * half + dz * 16 + dy * 4 + k, 9 * dz + 3 * dy + dx + 1] = 1
    return [jnp.asarray(v, BF16) for v in (sel, sel_x, pick)]


def doubled(value, axis, start=1):
    size = lax.axis_size(axis)
    step = start
    while step < size:
        other = lax.ppermute(value, axis, [(i, i ^ step) for i in range(size)])
        value = jnp.concatenate([value, other], axis=0)
        step *= 2
    return value


def call(kernel, name, out_shape, ins, smem=0, scratch=(), flops=0, alias=None):
    single = not isinstance(out_shape, list)
    return pl.pallas_call(
        kernel,
        out_shape=out_shape,
        in_specs=[VMEM] * (len(ins) - smem) + [SMEM] * smem,
        out_specs=VMEM if single else [VMEM] * len(out_shape),
        scratch_shapes=list(scratch),
        input_output_aliases={alias: 0} if alias is not None else {},
        compiler_params=pltpu.CompilerParams(vmem_limit_bytes=40 * 1024 * 1024),
        cost_estimate=pl.CostEstimate(flops=flops, bytes_accessed=1 << 20, transcendentals=0) if flops else None,
        name=name,
    )(*ins)


def shards(
    charges, points, leaf_basis, transfer_one, transfer_two, couple_one, couple_two, near_list, list_one, list_two
):
    columns = charges.shape[1]
    leaves = near_list.shape[0]
    nodes = leaves // 8
    tops = nodes // 8
    depth = 4 * (leaves // 64)
    rows, cols = lax.axis_size("row"), lax.axis_size("col")
    merge = cols == 2 and tops == 1
    t1 = transfer_one.reshape(leaves * 32, 32)
    t2 = transfer_two.reshape(nodes * 32, 32)
    shape = jax.ShapeDtypeStruct
    face = 2 * depth * 128
    outs = call(
        functools.partial(up_kernel, merge, depth),
        "up",
        [shape((16, columns), BF16)]
        + (
            [shape((80, face + 256), BF16), shape((16 * nodes + 32, 128), BF16)]
            if merge
            else [shape((80, face), BF16), shape(((nodes + tops) * 32, 64), BF16), shape((80, face), BF16)]
        ),
        [charges, points, leaf_basis, t1, t2],
    )
    feat, pay, coef = outs[:3]
    if merge:
        faces = [coef, lax.ppermute(pay, "col", [(0, 1), (1, 0)])]
    else:
        up = [(i, i + 1) for i in range(cols - 1)]
        faces = [lax.ppermute(pay, "col", up), lax.ppermute(outs[3], "col", [(j, i) for i, j in up])]
    sel, sel_x, pick = constants()
    acc_shape = shape((2 * depth, 64, 512), F32)
    acc, x, mask, yt = call(
        functools.partial(own_kernel, depth),
        "own",
        [
            acc_shape,
            shape((2 * depth, 96, 512), BF16),
            shape((2 * depth, 48, 512), F32),
            shape((2 * depth * SIDE, 128, 32), BF16),
        ],
        [charges, feat, near_list, sel, sel_x, pick],
        flops=1 << 32,
    )
    edge = 3 * depth * 128
    packed = call(
        functools.partial(pack_kernel, merge, depth),
        "pack",
        [
            shape((80, 4 * depth * 128), BF16),
            shape((80, edge + (128 if merge else 0)), BF16),
            shape((80, edge), BF16),
        ]
        + ([shape((2 * nodes, 32, 64), BF16)] if merge else []),
        [charges, feat, *faces],
    )
    halo, even, odd = packed[:3]
    mine = even
    even = lax.ppermute(even, "row", [(i, i ^ 1) for i in range(rows)])
    odd = lax.ppermute(odd, "row", [p for i in range(1, rows - 1, 2) for p in ((i, i + 1), (i + 1, i))])
    acc = call(
        functools.partial(side_kernel, depth),
        "side",
        acc_shape,
        [charges, halo, sel, x, mask, yt, acc],
        alias=6,
        scratch=[pltpu.VMEM((2 * depth * SIDE, 64, 128), BF16), pltpu.VMEM((2 * depth * SIDE, 64, 64), BF16)],
        flops=1 << 32,
    )
    if merge:
        one = packed[3]
        top = jnp.stack([mine[0:32, edge:], even[0:32, edge:]])
        top = doubled(top, "row", 2)
    else:
        coef = doubled(coef.reshape(1, nodes + tops, 32, 64), "col")
        one = coef[:, :nodes].reshape(cols * nodes, 32, 64)
        top = doubled(coef[:, nodes:].reshape(1, cols * tops, 32, 64), "row").reshape(-1, 32, 64)
    field = call(
        functools.partial(couple_kernel, cols * nodes),
        "couple",
        shape((nodes * 32, 64), F32),
        [couple_one, one, list_one],
        smem=1,
        flops=1 << 30,
    )
    small = [pltpu.VMEM((4 * depth, 64, 128), BF16), pltpu.VMEM((4 * depth, 64, 128), BF16)]
    acc = call(
        functools.partial(edge_kernel, depth),
        "edge",
        acc_shape,
        [even, odd, sel, x, mask, acc],
        alias=5,
        scratch=small + [pltpu.VMEM((4 * depth, 128, 32), BF16), pltpu.VMEM((4 * depth, 64, 64), BF16)],
        flops=1 << 31,
    )
    return call(
        functools.partial(down_kernel, depth, merge),
        "down",
        shape((64, columns), BF16),
        [acc, field, leaf_basis, t1, t2, couple_two, top, list_two],
        smem=1,
        scratch=[pltpu.VMEM((rows * cols * tops, 32, 64), BF16)],
    )


def solution(mesh):
    line, block = P(None, ("row", "col")), P(("row", "col"))
    in_specs = (line, line, line) + (block,) * 7
    return jax.shard_map(shards, mesh=mesh, in_specs=in_specs, out_specs=line, check_vma=False)
```

time: 78.5 us -> 47.1 us (0.60)
  Pallas kernels: 45 us -> 25 us
  waiting for transfers between devices: 14.5 us -> 6.4 us
  local copies, waits for them, and re-layouts: 5.38 us -> 3.65 us
  starting transfers between devices: 12.5 us -> 11.5 us
    pallas_call x3 -> x7, Pallas kernels: 45 us -> 25 us  [call(): pl.pallas_call(kernel, out_shape=out_shape, in_specs=[VMEM] * (len(ins) -...]
    ppermute x5 -> x3, waiting for transfers between devices: 14.4 us -> 6.4 us  [doubled(): other = lax.ppermute(value, axis, [(i, i ^ step) for i in range(size)])]
    ppermute x5 -> x3, starting transfers between devices: 11.8 us -> 7.71 us  [doubled(): other = lax.ppermute(value, axis, [(i, i ^ step) for i in range(size)])]
    ppermute x1, starting transfers between devices: 0.02 us -> 3.03 us  [shards(): faces = [coef, lax.ppermute(pay, 'col', [(0, 1), (1, 0)])]]
    unnamed x17 -> x32, local copies, waits for them, and re-layouts: 4.71 us -> 3.63 us
  transfers between devices with their start and end apart: 8 -> 6, of which waited for: 4 -> 2; matrix products, arithmetic and copies ran while one was open for 3% -> 0% of each run, Pallas kernels for 3% -> 37%
where the time goes in v2:
time: 47.1 us; the launch traced here: 46.8 us
  Pallas kernels  25 us (53%)
  starting transfers between devices  11.5 us (24%)
  waiting for transfers between devices  6.4 us (14%)
  local copies, waits for them, and re-layouts  3.65 us (8%)
    pallas_call x7, Pallas kernels, call(): pl.pallas_call(kernel, out_shape=out_shape, in_specs=[VMEM] * (len(ins) -...  25 us
    ppermute x3, starting transfers between devices, doubled(): other = lax.ppermute(value, axis, [(i, i ^ step) for i in range(size)])  7.71 us
    ppermute x3, waiting for transfers between devices, doubled(): other = lax.ppermute(value, axis, [(i, i ^ step) for i in range(size)])  6.4 us
    unnamed x32, local copies, waits for them, and re-layouts  3.63 us
    ppermute x1, starting transfers between devices, shards(): faces = [coef, lax.ppermute(pay, 'col', [(0, 1), (1, 0)])]  3.03 us
  transfers between devices with their start and end apart: 6, of which 2 were waited for; matrix products, arithmetic and copies ran while one was open for 0% of the time, Pallas kernels for 37%

profile of v2, /device:TPU:0, one launch (start us, length us, event | category | flops | bytes accessed | tf_op | source)
XLA Modules:
  0.0 46.8 jit_solution(11104113332130417686)
XLA Ops:
  0.0 1.8 %copy.16 = bf16[64,32,32]{2,1,0:T(8,128)(2,1)S(1)} copy(bf16[64,32,32]{0,2,1:T(8,128)(2,1)} %param.16) | data formatting | bytes 262144 | tf_op args[3]
  1.8 0.0 copy-done
  1.8 0.0 copy-done.1
  1.8 0.0 copy-start.2
  1.8 0.8 %copy-done.2 = bf16[8,32,32]{2,1,0:T(8,128)(2,1)S(1)} copy-done((bf16[8,32,32]{2,1,0:T(8,128)(2,1)S(1)}, bf16[8,32,32]{2,1,0:T(8,128)(2,1)}, u32[]{:S(2)}) %copy-start.2) | copy-done | bytes 16408
  2.7 0.8 %copy-done.5 = f32[3,4096]{1,0:T(4,128)S(1)} copy-done((f32[3,4096]{1,0:T(4,128)S(1)}, f32[3,4096]{1,0:T(4,128)}, u32[]{:S(2)}) %copy-start.5) | copy-done | bytes 49176
  3.5 2.9 %up.1 = (bf16[16,4096]{1,0:T(8,128)(2,1)S(1)}, bf16[80,1280]{1,0:T(8,128)(2,1)S(1)}, bf16[160,128]{1,0:T(8,128)(2,1)S(1)}) custom-call(bf16[64,4096]{1,0:T(8,128)(2,1)S(1)} %copy-done, f32[3,4096]{1,0:T(4,128)S(1)} %copy-done.5, bf16[32,4096]{1,0:T(8,128)(2,1)S(1)} %copy-done.1, bf16[2048,32]{1,0:T(8,128)(2,1)S(1)} %bitcast.10, bf16[256,32]{1,0:T(8,128)(2,1)S(1)} %bitcast.12), custom_call_target="tpu_custom_call" | custom-call | tf_op jit(solution)/shard_map/up/pallas_call | solution.py:452
  6.4 0.0 copy-start.11
  6.4 3.0 %collective-permute-start = (bf16[80,1280]{1,0:T(8,128)(2,1)S(1)}, bf16[80,1280]{1,0:T(8,128)(2,1)S(1)}, u32[]{:S(2)}, u32[]{:S(2)}) collective-permute-start(bf16[80,1280]{1,0:T(8,128)(2,1)S(1)} %get-tuple-element.18), channel_id=1, source_target_pairs={{0,1},{1,0},{2,3},{3,2},{4,5},{5,4},{6,7},{7,6},{8,9},{9,8},{10,11... | collective-permute-start | bytes 614408 | tf_op jit(solution)/shard_map/ppermute | solution.py:492
  9.5 0.0 copy-done.12
  9.5 0.1 copy.17.nl_ref
  9.6 0.0 copy-done.9
  9.6 7.5 %own.1 = (f32[8,64,512]{2,1,0:T(8,128)S(1)}, bf16[8,96,512]{2,1,0:T(8,128)(2,1)S(1)}, f32[8,48,512]{2,1,0:T(8,128)S(1)}, bf16[32,128,32]{2,1,0:T(8,128)(2,1)S(1)}) custom-call(bf16[64,4096]{1,0:T(8,128)(2,1)S(1)} %copy-done, bf16[16,4096]{1,0:T(8,128)(2,1)S(1)} %get-tuple-element.16.feat_ref, s32[64,27]{1,0:T(8,128)S(1)} %copy.17.nl_ref, ...), custom_call_target="tpu_custom_call" | custom-call | flops 4294967296 | bytes 1048576 | tf_op jit(solution)/shard_map/own/pallas_call | solution.py:452
  17.1 0.0 collective-permute-done.refs_1_
  17.1 0.4 pack.1
  17.6 0.1 collective-permute-start.1
  17.7 0.7 %collective-permute-start.2 = (bf16[80,1536]{1,0:T(8,128)(2,1)S(1)}, bf16[80,1536]{1,0:T(8,128)(2,1)S(1)}, u32[]{:S(2)}, u32[]{:S(2)}) collective-permute-start(bf16[80,1536]{1,0:T(8,128)(2,1)S(1)} %get-tuple-element.20), channel_id=1, source_target_pairs={{2,4},{4,2},{6,8},{8,6},{10,12},{12,10},{14,16},{16,14},{18,20},{2... | collective-permute-start | bytes 737288 | tf_op jit(solution)/shard_map/ppermute | solution.py:525
  18.4 0.0 copy-start.7
  18.4 0.0 copy-start.8
  18.4 4.6 %side.1.in_ref = f32[8,64,512]{2,1,0:T(8,128)S(1)} custom-call(bf16[64,4096]{1,0:T(8,128)(2,1)S(1)} %copy-done, bf16[80,2048]{1,0:T(8,128)(2,1)S(1)} %get-tuple-element.23.h_ref, bf16[16,160]{1,0:T(8,128)(2,1)S(1)} %copy-done.10, bf16[8,96,512]{2,1,0:T(8,128)(2,1)S(1)} %get-tuple-element.21.x_ref, ...), custom_call_target="tpu_custom_call", output_to_operand_aliasing={{}: (6, {})} | custom-call | flops 4294967296 | bytes 1048576 | tf_op jit(solution)/shard_map/side/pallas_call | solution.py:452
  23.0 1.5 %couple.1.f1_ref = f32[256,64]{1,0:T(8,128)S(1)} custom-call(bf16[8,12,32,32]{3,2,1,0:T(8,128)(2,1)S(1)} %copy-done.7, bf16[16,32,64]{2,1,0:T(8,128)(2,1)S(1)} %get-tuple-element.26.coef_ref, s32[8,12]{1,0:T(8,128)S(1)} %copy-done.8), custom_call_target="tpu_custom_call" | custom-call | flops 1073741824 | bytes 1048576 | tf_op jit(solution)/shard_map/couple/pallas_call | solution.py:452
  24.5 0.0 collective-permute-done.1.even_ref
  24.5 3.4 %collective-permute-start.3 = (bf16[2,32,128]{2,1,0:T(8,128)(2,1)S(1)}, bf16[2,32,128]{2,1,0:T(8,128)(2,1)S(1)}, u32[]{:S(2)}, u32[]{:S(2)}) collective-permute-start(bf16[2,32,128]{2,1,0:T(8,128)(2,1)S(1)} %pad_maximum_fusion.2), channel_id=1, source_target_pairs={{0,4},{2,6},{4,0},{6,2},{8,12},{10,14},{12,8},{14,10},{16,20},{18,... | collective-permute-start | bytes 49160 | tf_op jit(solution)/shard_map/ppermute | solution.py:444
  27.9 0.0 collective-permute-done.2.odd_ref
  27.9 3.9 %edge.1.acc_ref = f32[8,64,512]{2,1,0:T(8,128)S(1)} custom-call(bf16[80,1664]{1,0:T(8,128)(2,1)S(1)} %collective-permute-done.1.even_ref, bf16[80,1536]{1,0:T(8,128)(2,1)S(1)} %collective-permute-done.2.odd_ref, bf16[16,160]{1,0:T(8,128)(2,1)S(1)} %copy-done.10, bf16[8,96,512]{2,1,0:T(8,128)(2,1)S(1)} %get-tuple-element.21.x_ref, ...), custom_call_target="tpu_custom_call", output_to_operand_aliasing={{}: (5, {})} | custom-call | flops 2147483648 | bytes 1048576 | tf_op jit(solution)/shard_map/edge/pallas_call | solution.py:452
  31.8 0.0 collective-permute-done.3
  31.9 1.6 %collective-permute-start.4 = (bf16[4,32,128]{2,1,0:T(8,128)(2,1)S(1)}, bf16[4,32,128]{2,1,0:T(8,128)(2,1)S(1)}, u32[]{:S(2)}, u32[]{:S(2)}) collective-permute-start(bf16[4,32,128]{2,1,0:T(8,128)(2,1)S(1)} %pad_maximum_fusion.1), channel_id=1, source_target_pairs={{0,8},{2,10},{4,12},{6,14},{8,0},{10,2},{12,4},{14,6},{16,24},{18,... | collective-permute-start | bytes 98312 | tf_op jit(solution)/shard_map/ppermute | solution.py:444
  33.5 2.5 %collective-permute-done.4 = bf16[4,32,128]{2,1,0:T(8,128)(2,1)S(1)} collective-permute-done((bf16[4,32,128]{2,1,0:T(8,128)(2,1)S(1)}, bf16[4,32,128]{2,1,0:T(8,128)(2,1)S(1)}, u32[]{:S(2)}, u32[]{:S(2)}) %collective-permute-start.4) | collective-permute-done | bytes 32800 | tf_op jit(solution)/shard_map/ppermute | solution.py:444
  36.0 0.0 copy-start.4
  36.0 2.7 %collective-permute-start.5 = (bf16[8,32,128]{2,1,0:T(8,128)(2,1)S(1)}, bf16[8,32,128]{2,1,0:T(8,128)(2,1)S(1)}, u32[]{:S(2)}, u32[]{:S(2)}) collective-permute-start(bf16[8,32,128]{2,1,0:T(8,128)(2,1)S(1)} %pad_maximum_fusion), channel_id=1, source_target_pairs={{0,16},{2,18},{4,20},{6,22},{8,24},{10,26},{12,28},{14,30},{16,0},... | collective-permute-start | bytes 196616 | tf_op jit(solution)/shard_map/ppermute | solution.py:444
  38.7 3.9 %collective-permute-done.5 = bf16[8,32,128]{2,1,0:T(8,128)(2,1)S(1)} collective-permute-done((bf16[8,32,128]{2,1,0:T(8,128)(2,1)S(1)}, bf16[8,32,128]{2,1,0:T(8,128)(2,1)S(1)}, u32[]{:S(2)}, u32[]{:S(2)}) %collective-permute-start.5) | collective-permute-done | bytes 65568 | tf_op jit(solution)/shard_map/ppermute | solution.py:444
  42.6 4.2 %down.1 = bf16[64,4096]{1,0:T(8,128)(2,1)} custom-call(f32[8,64,512]{2,1,0:T(8,128)S(1)} %edge.1.acc_ref, f32[256,64]{1,0:T(8,128)S(1)} %couple.1.f1_ref, bf16[32,4096]{1,0:T(8,128)(2,1)S(1)} %copy-done.1, bf16[2048,32]{1,0:T(8,128)(2,1)S(1)} %bitcast.11, bf16[256,32]{1,0:T(8,128)(2,1)S(1)} %bitcast.13, bf16[1,16,32,32]{3,2,1,0:T(8,128)(2,1)S(1)} %copy-done.4, ...), custom_call_target="tpu_custom_call" | custom-call | tf_op jit(solution)/shard_map/down/pallas_call | solution.py:452
  (25 shorter events, 0.1 us)
Async XLA Ops:
  0.0 1.8 %copy-start = (bf16[64,4096]{1,0:T(8,128)(2,1)S(1)}, bf16[64,4096]{1,0:T(8,128)(2,1)}, u32[]{:S(2)}) copy-start(bf16[64,4096]{1,0:T(8,128)(2,1)} %q_ref.7) | copy-start | bytes 1572868
  0.0 1.8 %copy-start.1 = (bf16[32,4096]{1,0:T(8,128)(2,1)S(1)}, bf16[32,4096]{1,0:T(8,128)(2,1)}, u32[]{:S(2)}) copy-start(bf16[32,4096]{1,0:T(8,128)(2,1)} %basis_ref.3) | copy-start | bytes 786436
  1.8 0.8 %copy-start.2 = (bf16[8,32,32]{2,1,0:T(8,128)(2,1)S(1)}, bf16[8,32,32]{2,1,0:T(8,128)(2,1)}, u32[]{:S(2)}) copy-start(bf16[8,32,32]{2,1,0:T(8,128)(2,1)} %param.17) | copy-start | bytes 49156
  2.7 0.8 %copy-start.5 = (f32[3,4096]{1,0:T(4,128)S(1)}, f32[3,4096]{1,0:T(4,128)}, u32[]{:S(2)}) copy-start(f32[3,4096]{1,0:T(4,128)} %pts_ref.1) | copy-start | bytes 147460
  3.5 6.0 %copy-start.12 = (s32[64,27]{0,1:T(8,128)S(1)}, s32[64,27]{0,1:T(8,128)}, u32[]{:S(2)}) copy-start(s32[64,27]{0,1:T(8,128)} %param.20) | copy-start | bytes 20740
  6.4 3.1 %copy-start.9 = (bf16[96,27]{1,0:T(8,128)(2,1)S(1)}, bf16[96,27]{1,0:T(8,128)(2,1)}, u32[]{:S(2)}) copy-start(bf16[96,27]{1,0:T(8,128)(2,1)} %constant.8.clone.pick_ref) | copy-start | bytes 15556
  6.4 3.1 %copy-start.10 = (bf16[16,160]{1,0:T(8,128)(2,1)S(1)}, bf16[16,160]{1,0:T(8,128)(2,1)}, u32[]{:S(2)}) copy-start(bf16[16,160]{1,0:T(8,128)(2,1)} %constant.6.clone.sel_ref) | copy-start | bytes 15364
  6.4 3.1 %copy-start.11 = (bf16[32,16]{1,0:T(8,128)(2,1)S(1)}, bf16[32,16]{1,0:T(8,128)(2,1)}, u32[]{:S(2)}) copy-start(bf16[32,16]{1,0:T(8,128)(2,1)} %constant.7.clone.sel_x_ref) | copy-start | bytes 3076
  6.4 10.7 %collective-permute-start = (bf16[80,1280]{1,0:T(8,128)(2,1)S(1)}, bf16[80,1280]{1,0:T(8,128)(2,1)S(1)}, u32[]{:S(2)}, u32[]{:S(2)}) collective-permute-start(bf16[80,1280]{1,0:T(8,128)(2,1)S(1)} %get-tuple-element.18), channel_id=1, source_target_pairs={{0,1},{1,0},{2,3},{3,2},{4,5},{5,4},{6,7},{7,6},{8,9},{9,8},{10,11... | collective-permute-start | bytes 614408 | tf_op jit(solution)/shard_map/ppermute | solution.py:492
  17.6 6.9 %collective-permute-start.1 = (bf16[80,1664]{1,0:T(8,128)(2,1)S(1)}, bf16[80,1664]{1,0:T(8,128)(2,1)S(1)}, u32[]{:S(2)}, u32[]{:S(2)}) collective-permute-start(bf16[80,1664]{1,0:T(8,128)(2,1)S(1)} %get-tuple-element.19), channel_id=1, source_target_pairs={{0,2},{2,0},{4,6},{6,4},{8,10},{10,8},{12,14},{14,12},{16,18},{18,... | collective-permute-start | bytes 798728 | tf_op jit(solution)/shard_map/ppermute | solution.py:524
  17.7 10.2 %collective-permute-start.2 = (bf16[80,1536]{1,0:T(8,128)(2,1)S(1)}, bf16[80,1536]{1,0:T(8,128)(2,1)S(1)}, u32[]{:S(2)}, u32[]{:S(2)}) collective-permute-start(bf16[80,1536]{1,0:T(8,128)(2,1)S(1)} %get-tuple-element.20), channel_id=1, source_target_pairs={{2,4},{4,2},{6,8},{8,6},{10,12},{12,10},{14,16},{16,14},{18,20},{2... | collective-permute-start | bytes 737288 | tf_op jit(solution)/shard_map/ppermute | solution.py:525
  18.4 4.6 %copy-start.7 = (bf16[8,12,32,32]{3,2,1,0:T(8,128)(2,1)S(1)}, bf16[8,12,32,32]{3,2,1,0:T(8,128)(2,1)}, u32[]{:S(2)}) copy-start(bf16[8,12,32,32]{3,2,1,0:T(8,128)(2,1)} %k1_ref.1) | copy-start | bytes 589828
  18.4 4.6 %copy-start.8 = (s32[8,12]{1,0:T(8,128)S(1)}, s32[8,12]{1,0:T(8,128)}, u32[]{:S(2)}) copy-start(s32[8,12]{1,0:T(8,128)} %l1_ref.1) | copy-start | bytes 1156
  24.5 7.4 %collective-permute-start.3 = (bf16[2,32,128]{2,1,0:T(8,128)(2,1)S(1)}, bf16[2,32,128]{2,1,0:T(8,128)(2,1)S(1)}, u32[]{:S(2)}, u32[]{:S(2)}) collective-permute-start(bf16[2,32,128]{2,1,0:T(8,128)(2,1)S(1)} %pad_maximum_fusion.2), channel_id=1, source_target_pairs={{0,4},{2,6},{4,0},{6,2},{8,12},{10,14},{12,8},{14,10},{16,20},{18,... | collective-permute-start | bytes 49160 | tf_op jit(solution)/shard_map/ppermute | solution.py:444
  27.9 14.7 %copy-start.6 = (s32[1,16]{1,0:T(1,128)S(1)}, s32[1,16]{1,0:T(1,128)}, u32[]{:S(2)}) copy-start(s32[1,16]{1,0:T(1,128)} %l2_ref.1) | copy-start | bytes 196
  31.9 4.1 %collective-permute-start.4 = (bf16[4,32,128]{2,1,0:T(8,128)(2,1)S(1)}, bf16[4,32,128]{2,1,0:T(8,128)(2,1)S(1)}, u32[]{:S(2)}, u32[]{:S(2)}) collective-permute-start(bf16[4,32,128]{2,1,0:T(8,128)(2,1)S(1)} %pad_maximum_fusion.1), channel_id=1, source_target_pairs={{0,8},{2,10},{4,12},{6,14},{8,0},{10,2},{12,4},{14,6},{16,24},{18,... | collective-permute-start | bytes 98312 | tf_op jit(solution)/shard_map/ppermute | solution.py:444
  36.0 6.6 %copy-start.4 = (bf16[1,16,32,32]{3,2,1,0:T(8,128)(2,1)S(1)}, bf16[1,16,32,32]{3,2,1,0:T(8,128)(2,1)}, u32[]{:S(2)}) copy-start(bf16[1,16,32,32]{3,2,1,0:T(8,128)(2,1)} %k2_ref.1) | copy-start | bytes 98308
  36.0 6.6 %collective-permute-start.5 = (bf16[8,32,128]{2,1,0:T(8,128)(2,1)S(1)}, bf16[8,32,128]{2,1,0:T(8,128)(2,1)S(1)}, u32[]{:S(2)}, u32[]{:S(2)}) collective-permute-start(bf16[8,32,128]{2,1,0:T(8,128)(2,1)S(1)} %pad_maximum_fusion), channel_id=1, source_target_pairs={{0,16},{2,18},{4,20},{6,22},{8,24},{10,26},{12,28},{14,30},{16,0},... | collective-permute-start | bytes 196616 | tf_op jit(solution)/shard_map/ppermute | solution.py:444
  38.7 4.0 %copy-start.3 = (bf16[8,32,32]{2,1,0:T(8,128)(2,1)S(1)}, bf16[8,32,32]{2,1,0:T(8,128)(2,1)}, u32[]{:S(2)}) copy-start(bf16[8,32,32]{2,1,0:T(8,128)(2,1)} %param.17) | copy-start | bytes 49156

commit v3 on v2

v3 whole, which is shorter than its diff:
```python
import functools

import jax
import jax.numpy as jnp
import numpy as np
from jax import lax
from jax.experimental import pallas as pl
from jax.experimental.pallas import tpu as pltpu
from jax.sharding import PartitionSpec as P


NEAR = 27
SIDE = 4
SOFTENING = 0.0025
F32 = jnp.float32
BF16 = jnp.bfloat16
NT = (((1,), (1,)), ((), ()))
TN = (((0,), (0,)), ((), ()))
NN = (((1,), (0,)), ((), ()))
VMEM = pl.BlockSpec(memory_space=pltpu.VMEM)
SMEM = pl.BlockSpec(memory_space=pltpu.SMEM)
HBM = pl.BlockSpec(memory_space=pltpu.MemorySpace.HBM)


def dot(a, b, dims=NN):
    return lax.dot_general(a, b, dims, preferred_element_type=F32)


def split2(v):
    hi = v.astype(BF16)
    lo = (v - hi.astype(F32)).astype(BF16)
    return hi, lo


def tile_of(z, y, x1):
    return (z // 4) * 32 + (z // 2 % 2) * 16 + (y // 2) * 8 + x1 * 4 + (z % 2) * 2 + (y % 2)


def lower_half(shape):
    return lax.broadcasted_iota(jnp.int32, shape, len(shape) - 1) % 128 < 64


def swap_matrix():
    a = lax.broadcasted_iota(jnp.int32, (128, 128), 0)
    b = lax.broadcasted_iota(jnp.int32, (128, 128), 1)
    return jnp.where((a + 64) % 128 == b, 1.0, 0.0).astype(BF16)


def block_basis(basis):
    rank, width = basis.shape
    leaf = lax.broadcasted_iota(jnp.int32, (rank, width), 1) // 64
    zero = jnp.zeros_like(basis)
    return jnp.concatenate([jnp.where(leaf == k, basis, zero) for k in range(8)], axis=0)


def feature_rows(x):
    pairs = [split2(v) for v in x]
    hi = [a.astype(F32) for a, _ in pairs]
    lo = [b.astype(F32) for _, b in pairs]
    y = [a + b for a, b in zip(hi, lo)]
    norm = y[0] * y[0] + y[1] * y[1] + y[2] * y[2]
    n1 = norm.astype(BF16).astype(F32)
    n2 = (norm - n1).astype(BF16).astype(F32)
    n3 = norm - n1 - n2
    width = norm.shape[1]
    index = lax.broadcasted_iota(jnp.int32, (16, width), 0)
    out = jnp.where(index == 9, 1.0, 0.0)
    for k, piece in enumerate(hi + lo + [n1, n2, n3]):
        out = jnp.where(index == k, piece, out)
    return out.astype(BF16)


def with_ones(rows):
    index = lax.broadcasted_iota(jnp.int32, rows.shape, 0)
    return jnp.where(index == 9, jnp.ones_like(rows), rows)


def coordinates(rows):
    return [rows[c : c + 1].astype(F32) + rows[c + 3 : c + 4].astype(F32) for c in range(3)]


def swapped(tiles):
    out = dot(jnp.concatenate(tiles, axis=0), swap_matrix()).astype(BF16)
    size = tiles[0].shape[0]
    return [out[size * k : size * k + size] for k in range(len(tiles))]


def halves(firsts, seconds, x1):
    low = lower_half(firsts[0].shape)
    if x1 == 1:
        return [jnp.where(low, a, b) for a, b in zip(swapped(firsts), seconds)]
    return [jnp.where(low, a, b) for a, b in zip(firsts, swapped(seconds))]


def unpacked(rights, lefts):
    low = lower_half(rights[0].shape)
    turned = swapped(rights)
    other = turned if rights is lefts else swapped(lefts)
    return [
        (jnp.where(low, r, o), jnp.where(low, t, l)) for r, l, t, o in zip(rights, lefts, turned, other)
    ]


def tiles_in(ref, first, count):
    return [ref[:, 128 * k : 128 * k + 128] for k in range(first, first + count)]


def transposed(tiles, sel_ref):
    rows = dot(jnp.concatenate(tiles, axis=1), sel_ref[:, 0:32], TN).astype(BF16)
    return [rows[128 * k : 128 * k + 128] for k in range(len(tiles))]


def send_rows(pay_ref, last_first, q_ref, feat, depth):
    width = 2 * depth * 128
    for z in range(depth):
        for k in range(2):
            ats = [tile_of(z, y, k) * 128 for y in (SIDE - 1, 0)]
            at = (z * 2 + k) * 128
            pay_ref[0:64, at : at + 128] = jnp.where(
                last_first, q_ref[:, ats[0] : ats[0] + 128], q_ref[:, ats[1] : ats[1] + 128]
            )
            pay_ref[64:80, at : at + 128] = jnp.where(
                last_first, feat[:, ats[0] : ats[0] + 128], feat[:, ats[1] : ats[1] + 128]
            )
    x = coordinates(pay_ref[64:80, 0:width].astype(F32))
    shift = jnp.where(last_first, -float(SIDE), float(SIDE))
    pay_ref[64:80, 0:width] = feature_rows([x[0], x[1] + shift, x[2]])


def face_kernel(merge, depth, q_hbm, pts_hbm, q_ref, feat_ref, odd_ref, xpay_ref, *more):
    pts_ref, sems = more[-2:]
    copies = [
        pltpu.make_async_copy(pts_hbm, pts_ref, sems.at[0]),
        pltpu.make_async_copy(q_hbm, q_ref, sems.at[1]),
    ]
    for copy in copies:
        copy.start()
    row, col = lax.axis_index("row"), lax.axis_index("col")
    columns = q_ref.shape[1]
    centre = (
        (SIDE * col + SIDE // 2).astype(F32),
        (SIDE * row + SIDE // 2).astype(F32),
        jnp.float32(depth / 2),
    )
    copies[0].wait()
    local = [pts_ref[c : c + 1, :] - centre[c] for c in range(3)]
    feat = feature_rows(local)
    feat_ref[...] = feat
    pair_x = lax.broadcasted_iota(jnp.int32, (1, columns), 1) // 512 % 2
    shift = jnp.where(pair_x == 1, -float(SIDE), float(SIDE))
    moved = feature_rows([local[0] + shift, local[1], local[2]])
    copies[1].wait()

    def tile(z, y, x1):
        at = tile_of(z, y, x1) * 128
        return jnp.concatenate([q_ref[:, at : at + 128], moved[:, at : at + 128]], axis=0)

    places = [(z, y1) for z in range(depth) for y1 in range(2)]
    sides = [[[tile(z, 2 * y1 + k, x1) for z, y1 in places] for k in range(2)] for x1 in range(2)]
    if merge:
        first = [jnp.where(col == 0, a, b) for a, b in zip(sides[1][0], sides[0][1])]
        second = [jnp.where(col == 0, a, b) for a, b in zip(sides[1][1], sides[0][0])]
        low = lower_half((80, 128)) == (col == 0)
        for k, (a, b) in enumerate(zip(swapped(first), second)):
            xpay_ref[:, 128 * k : 128 * k + 128] = jnp.where(low, a, b)
    else:
        for ref, x1 in ((xpay_ref, 1), (more[0], 0)):
            for k, value in enumerate(halves(*sides[x1], x1)):
                ref[:, 128 * k : 128 * k + 128] = value
    send_rows(odd_ref, row % 2 == 1, q_ref, feat, depth)


def up_kernel(merge, depth, q_ref, feat_ref, basis_ref, t1_ref, t2_ref, even_ref, coef_ref):
    nodes = q_ref.shape[1] // 512
    leaf = []
    for n in range(nodes):
        chunk = slice(512 * n, 512 * n + 512)
        leaf.append(dot(block_basis(basis_ref[:, chunk]), q_ref[:, chunk], NT).astype(BF16))
    ones = [dot(t1_ref[256 * n : 256 * n + 256, :], leaf[n], TN).astype(BF16) for n in range(nodes)]
    tops = []
    for m in range(nodes // 8):
        part = jnp.concatenate(ones[8 * m : 8 * m + 8], axis=0)
        tops.append(dot(t2_ref[256 * m : 256 * m + 256, :], part, TN).astype(BF16))
    send_rows(even_ref, lax.axis_index("row") % 2 == 0, q_ref, feat_ref, depth)
    if merge:
        for k in range(nodes // 2):
            coef_ref[32 * k : 32 * k + 32, :] = jnp.concatenate([ones[2 * k], ones[2 * k + 1]], axis=1)
        both = jnp.concatenate([tops[0], tops[0]], axis=1)
        coef_ref[16 * nodes : 16 * nodes + 32, :] = both
        width = 2 * depth * 128
        even_ref[0:32, width : width + 128] = both
        even_ref[32:80, width : width + 128] = jnp.zeros((48, 128), BF16)
    else:
        for k, value in enumerate(ones + tops):
            coef_ref[32 * k : 32 * k + 32, :] = value


def row_sides(even_ref, odd_ref):
    even = lax.axis_index("row") % 2 == 0

    def face(side, at):
        a, b = even_ref[:, at : at + 128], odd_ref[:, at : at + 128]
        return jnp.where(even, b, a) if side == 0 else jnp.where(even, a, b)

    return face


def corner_kernel(merge, depth, even_ref, odd_ref, *refs):
    col = lax.axis_index("col")
    face = row_sides(even_ref, odd_ref)
    coef_ref, pay_ref = refs if merge else (None, refs[0])
    tiles = [[[face(side, (z * 2 + k) * 128) for z in range(depth)] for side in range(2)] for k in range(2)]
    high, base = halves(*tiles[1], 1), halves(*tiles[0], 0)
    groups = [(pay_ref, jnp.concatenate(high, axis=1), -float(SIDE))]
    if merge:
        mine = jnp.where(col == 0, groups[0][1], jnp.concatenate(base, axis=1))
        groups = [(pay_ref, mine, jnp.where(col == 0, -float(SIDE), float(SIDE)))]
    else:
        groups.append((refs[1], jnp.concatenate(base, axis=1), float(SIDE)))
    width = depth * 128
    for ref, tile, shift in groups:
        ref[0:64, 0:width] = tile[0:64]
        x = coordinates(tile[64:80].astype(F32))
        ref[64:80, 0:width] = feature_rows([x[0] + shift, x[1], x[2]])
    if merge:
        rest = coef_ref.shape[0] - 32
        other = even_ref[0:32, 2 * depth * 128 : 2 * depth * 128 + 128]
        tops = jnp.where(lower_half((32, 128)), coef_ref[rest : rest + 32, :], other)
        blocks = jnp.concatenate([coef_ref[0:rest, :], tops], axis=0)
        for k in range(blocks.shape[0] // 80):
            pay_ref[:, width + 128 * k : width + 128 * k + 128] = blocks[80 * k : 80 * k + 80]


def layers_of(depth, tz):
    return [sz for sz in (tz - 1, tz, tz + 1) if 0 <= sz < depth]


def inner_steps(depth):
    steps = []
    for tz in range(depth):
        layers = layers_of(depth, tz)
        for sz in layers:
            steps.append((tz, (0, 1), [(sz, 1), (sz, 2)]))
            steps.append((tz, (2, 3), [(sz, 3), (sz, 4)]))
        steps.append((tz, (1,), [(sz, 3) for sz in layers]))
        steps.append((tz, (2,), [(sz, 2) for sz in layers]))
    return steps


def mask_row(mask_ref, at, dz, dy, k, ty):
    row = dz * 16 + dy * 4 + k
    m = mask_ref[at, row : row + 1, 128 * ty : 128 * ty + 128]
    m = jnp.broadcast_to(m, (16, 128)).astype(BF16)
    return jnp.concatenate([m] * 4, axis=0)


AHEAD = 6


def scan(steps, depth, rows_of, charge_of, x_ref, mask_ref, acc_ref, fresh=False):
    def pair(xp, carry):
        ready, seen = [], set()
        for i in range(len(steps) + AHEAD):
            if i < len(steps):
                sides, (tz, tiles, sources) = steps[i]
                lanes = slice(128 * tiles[0], 128 * tiles[-1] + 128)
                at = xp * depth + tz
                rows = jnp.concatenate([rows_of(sides, xp, sz, ye) for sz, ye in sources], axis=0)
                features = x_ref[at, 32:96, lanes] if sides else x_ref[at, 0:32, lanes]
                ready.append(lax.rsqrt(dot(rows, features).astype(BF16)))
            if i >= AHEAD:
                sides, (tz, tiles, sources) = steps[i - AHEAD]
                inv, ready[i - AHEAD] = ready[i - AHEAD], None
                lanes = slice(128 * tiles[0], 128 * tiles[-1] + 128)
                at = xp * depth + tz
                size = 64 if sides else 128
                columns = []
                for j, ty in enumerate(tiles):
                    blocks = []
                    for k, (sz, ye) in enumerate(sources):
                        part = inv[size * k : size * k + size, 128 * j : 128 * j + 128]
                        halves = [part, part] if sides else [part[0:64], part[64:128]]
                        first = 2 if sides else 0
                        blocks += [
                            h * mask_row(mask_ref, at, sz - tz + 1, ye - ty, first + c, ty) for c, h in enumerate(halves)
                        ]
                    columns.append(jnp.concatenate(blocks, axis=0))
                kernel = columns[0] if len(columns) == 1 else jnp.concatenate(columns, axis=1)
                charge = jnp.concatenate([charge_of(sides, xp, sz, ye) for sz, ye in sources], axis=1)
                value = dot(charge, kernel)
                if fresh and len(tiles) == 2 and (tz, tiles) not in seen:
                    seen.add((tz, tiles))
                    acc_ref[at, :, lanes] = value
                else:
                    acc_ref[at, :, lanes] += value
        return carry

    lax.fori_loop(0, 2, pair, 0)


def own_kernel(depth, q_ref, feat_ref, nl_ref, sel_ref, sel_x_ref, pick_ref, acc_ref, x_ref, mask_ref, yt_ref):
    columns = q_ref.shape[1]
    leaves = columns // 64
    x = dot(sel_x_ref[...], feat_ref[...])
    active = jnp.where(nl_ref[...] >= 0, 1.0, 0.0).astype(BF16)
    pick = dot(pick_ref[...], active)
    pick = jnp.where(
        lax.broadcasted_iota(jnp.int32, (48, leaves), 1) % 2 == 0, pick[0:48], pick[48:96]
    ).astype(BF16)
    spread = jnp.where(
        lax.broadcasted_iota(jnp.int32, (leaves, columns), 0)
        == lax.broadcasted_iota(jnp.int32, (leaves, columns), 1) // 64,
        1.0,
        0.0,
    ).astype(BF16)
    masks = dot(pick, spread)
    low = lower_half((32, 128))
    rows = dot(feat_ref[...], sel_ref[:, 0:32], TN).astype(BF16)
    for z in range(depth):
        for xp in range(2):
            for y in range(SIDE):
                at = tile_of(z, y, xp) * 128
                lanes = slice(128 * y, 128 * y + 128)
                tile = x[:, at : at + 128]
                x_ref[xp * depth + z, 0:32, lanes] = tile.astype(BF16)
                x_ref[xp * depth + z, 32:64, lanes] = jnp.where(low, 0.0, tile).astype(BF16)
                x_ref[xp * depth + z, 64:96, lanes] = jnp.where(low, tile, 0.0).astype(BF16)
                mask_ref[xp * depth + z, :, lanes] = masks[:, at : at + 128]
                yt_ref[(xp * depth + z) * SIDE + y] = rows[at : at + 128]

    def rows_of(sides, xp, sz, ye):
        return yt_ref[(xp * depth + sz) * SIDE + ye - 1]

    def charge_of(sides, xp, sz, ye):
        base = pl.multiple_of(tile_of(sz, ye - 1, xp) * 128, 128)
        return q_ref[:, pl.ds(base, 128)]

    steps = [(False, step) for step in inner_steps(depth)]
    scan(steps, depth, rows_of, charge_of, x_ref, mask_ref, acc_ref, fresh=True)


def beside(right, left):
    return jnp.concatenate([right, left], axis=1)


def side_kernel(merge, depth, q_ref, right_ref, *refs):
    if not merge:
        left_ref, *refs = refs
    sel_ref, x_ref, mask_ref, yt_ref, _, acc_ref, c_ref, ys_ref = refs
    low = lower_half((64, 128))
    count = right_ref.shape[1] // 128
    rights = tiles_in(right_ref, 0, count)
    lefts = rights if merge else tiles_in(left_ref, 0, count)
    beyond = [tile for pair in unpacked(rights, lefts) for tile in pair]
    turned = transposed([with_ones(h[64:80]) for h in beyond], sel_ref)
    for z in range(depth):
        for y in range(SIDE):
            t = [q_ref[:, a * 128 : a * 128 + 128] for a in (tile_of(z, y, 0), tile_of(z, y, 1))]
            even, odd = z * SIDE + y, (depth + z) * SIDE + y
            h, rows = beyond[even][0:64], turned[even]
            c_ref[even] = jnp.where(low, t[1], h)
            c_ref[odd] = jnp.where(low, h, t[0])
            ys_ref[even] = beside(yt_ref[odd, 0:64], rows[64:128])
            ys_ref[odd] = beside(rows[0:64], yt_ref[even, 64:128])

    def rows_of(sides, xp, sz, ye):
        return ys_ref[(xp * depth + sz) * SIDE + ye - 1]

    def charge_of(sides, xp, sz, ye):
        return c_ref[(xp * depth + sz) * SIDE + ye - 1]

    scan([(True, step) for step in inner_steps(depth)], depth, rows_of, charge_of, x_ref, mask_ref, acc_ref)


def edge_steps(depth, sides):
    steps = []
    for tz in range(depth):
        for side in range(2):
            sources = [(sz, side * (SIDE + 1)) for sz in layers_of(depth, tz)]
            steps.append((sides, (tz, (side * (SIDE - 1),), sources)))
    return steps


def edge_kernel(depth, even_ref, odd_ref, sel_ref, x_ref, mask_ref, in_ref, acc_ref, c_ref, yt_ref):
    face = row_sides(even_ref, odd_ref)
    places = [(k, z, side) for k in range(2) for z in range(depth) for side in range(2)]
    tiles = [face(side, (z * 2 + k) * 128) for k, z, side in places]
    for i, rows in enumerate(transposed([with_ones(tile[64:80]) for tile in tiles], sel_ref)):
        c_ref[i] = tiles[i][0:64]
        yt_ref[i] = rows

    def rows_of(sides, xp, sz, ye):
        return yt_ref[(xp * depth + sz) * 2 + (ye > 0)]

    def charge_of(sides, xp, sz, ye):
        return c_ref[(xp * depth + sz) * 2 + (ye > 0)]

    scan(edge_steps(depth, False), depth, rows_of, charge_of, x_ref, mask_ref, acc_ref)


def last_kernel(merge, depth, edge_c_ref, edge_y_ref, right_ref, *refs):
    if not merge:
        left_ref, *refs = refs
    sel_ref, x_ref, mask_ref, _, acc_ref, c_ref, ys_ref = refs
    low = lower_half((64, 128))
    rights = tiles_in(right_ref, 0, depth)
    lefts = rights if merge else tiles_in(left_ref, 0, depth)
    beyond = [tile for pair in unpacked(rights, lefts) for tile in pair]
    turned = transposed([with_ones(h[64:80]) for h in beyond], sel_ref)
    for z in range(depth):
        for side in range(2):
            even, odd = z * 2 + side, (depth + z) * 2 + side
            h, rows = beyond[even][0:64], turned[even]
            c_ref[even] = jnp.where(low, edge_c_ref[odd], h)
            c_ref[odd] = jnp.where(low, h, edge_c_ref[even])
            ys_ref[even] = beside(edge_y_ref[odd, 0:64], rows[64:128])
            ys_ref[odd] = beside(rows[0:64], edge_y_ref[even, 64:128])

    def rows_of(sides, xp, sz, ye):
        return ys_ref[(xp * depth + sz) * 2 + (ye > 0)]

    def charge_of(sides, xp, sz, ye):
        return c_ref[(xp * depth + sz) * 2 + (ye > 0)]

    scan(edge_steps(depth, True), depth, rows_of, charge_of, x_ref, mask_ref, acc_ref)


def couple_kernel(merge, group, k1_ref, *refs):
    col = lax.axis_index("col")
    if merge:
        own_ref, got_ref, l1_ref, out_ref, coef_ref = refs
        nodes = l1_ref.shape[0]
        at = got_ref.shape[1] - 256
        got = jnp.concatenate([got_ref[:, at : at + 128], got_ref[:, at + 128 : at + 256]], axis=0)
        for k in range(nodes // 2):
            for side, value in enumerate((own_ref[32 * k : 32 * k + 32, :], got[32 * k : 32 * k + 32])):
                coef_ref[side * nodes + 2 * k] = value[:, 0:64]
                coef_ref[side * nodes + 2 * k + 1] = value[:, 64:128]
        coef_ref[group] = jnp.zeros((32, 64), BF16)
    else:
        coef_ref, l1_ref, out_ref = refs
    nodes, slots = l1_ref.shape
    mask = col * nodes
    zero = jnp.zeros((32, 64), BF16)
    totals = []
    for n in range(nodes):
        parts = []
        for s in range(slots):
            v = l1_ref[n, s]
            at = (v & (group - 1)) ^ mask
            if merge:
                parts.append(coef_ref[jnp.where(v >= 0, at, group)])
            else:
                parts.append(jnp.where(v >= 0, coef_ref[at], zero))
        matrix = jnp.concatenate([k1_ref[n, s] for s in range(slots)], axis=1)
        totals.append(dot(matrix, jnp.concatenate(parts, axis=0)))
    for n in range(nodes):
        out_ref[32 * n : 32 * n + 32, :] = totals[n]


def down_kernel(depth, wide, acc_ref, f1_ref, basis_ref, t1_ref, t2_ref, k2_ref, top_ref, l2_ref, out_hbm, *refs):
    out_ref, sems, top_scr = refs
    row, col = lax.axis_index("row"), lax.axis_index("col")
    nodes = out_hbm.shape[1] // 512
    per = nodes // 8
    me = row * lax.axis_size("col") + col
    if wide:
        for k in range(top_ref.shape[0]):
            top_scr[(k // 2) * 4 + k % 2] = top_ref[k, :, 0:64]
            top_scr[(k // 2) * 4 + 2 + k % 2] = top_ref[k, :, 64:128]
    else:
        top_scr[...] = top_ref[...]
    copies = []
    for m in range(per):
        parts = []
        for s in range(l2_ref.shape[1]):
            v = l2_ref[m, s]
            at = v ^ me if per == 1 else ((v // per) ^ me) * per + v % per
            parts.append(top_scr[at])
        matrix = jnp.concatenate([k2_ref[m, s] for s in range(l2_ref.shape[1])], axis=1)
        hi2, lo2 = split2(dot(matrix, jnp.concatenate(parts, axis=0)))
        t2 = t2_ref[256 * m : 256 * m + 256, :]
        hi1, lo1 = split2(f1_ref[256 * m : 256 * m + 256, :] + dot(t2, hi2) + dot(t2, lo2))
        leaves = []
        for j in range(8):
            n = 8 * m + j
            t1 = t1_ref[256 * n : 256 * n + 256, :]
            rows = slice(32 * j, 32 * j + 32)
            leaves.append((dot(t1, hi1[rows]) + dot(t1, lo1[rows])).astype(BF16))
        for j in range(8):
            n = 8 * m + j
            far = dot(leaves[j], block_basis(basis_ref[:, 512 * n : 512 * n + 512]), TN)
            z1, y1, x1 = j // 4, j // 2 % 2, j % 2
            for k in range(4):
                z, y = 4 * m + 2 * z1 + k // 2, 2 * y1 + k % 2
                part = acc_ref[x1 * depth + z, :, 128 * y : 128 * y + 128]
                total = part * (NEAR * 64) ** (-0.5) + far[:, 128 * k : 128 * k + 128]
                out_ref[:, 512 * n + 128 * k : 512 * n + 128 * k + 128] = total.astype(BF16)
            lanes = pl.ds(512 * n, 512)
            copies.append(pltpu.make_async_copy(out_ref.at[:, lanes], out_hbm.at[:, lanes], sems.at[n]))
            copies[-1].start()
    for copy in copies:
        copy.wait()


def constants():
    sel = np.zeros((16, 160), np.float32)
    sel_x = np.zeros((32, 16), np.float32)
    rest, eps = np.float32(SOFTENING), []
    for _ in range(3):
        eps.append(np.asarray(rest).astype(jnp.bfloat16).astype(np.float32))
        rest = np.float32(rest - eps[-1])
    for f in range(21):
        source = f if f < 6 else f - 6 if f < 12 else 9 if f < 15 else f - 9 if f < 18 else 9
        for base in (0, 32, 128):
            sel[source, base + f] = 1
        if f < 12:
            sel_x[f, f % 3 + (3 if f >= 6 else 0)] = -2
        elif f < 15:
            sel_x[f, f - 6] = 1
        else:
            sel_x[f, 9] = 1 if f < 18 else eps[f - 18]
    pick = np.zeros((96, NEAR), np.float32)
    for dz in range(3):
        for dy in range(3):
            for k in range(4):
                for half, dx in enumerate(((0, 1, None, -1)[k], (-1, 0, 1, None)[k])):
                    if dx is not None:
                        pick[48 * half + dz * 16 + dy * 4 + k, 9 * dz + 3 * dy + dx + 1] = 1
    return [jnp.asarray(v, BF16) for v in (sel, sel_x, pick)]


def doubled(value, axis, start=1):
    size = lax.axis_size(axis)
    step = start
    while step < size:
        other = lax.ppermute(value, axis, [(i, i ^ step) for i in range(size)])
        value = jnp.concatenate([value, other], axis=0)
        step *= 2
    return value


def call(kernel, out_shape, ins, smem=0, scratch=(), flops=0, alias=None, hbm_in=0, hbm_out=False):
    single = not isinstance(out_shape, list)
    return pallas(kernel, out_shape, ins, smem, scratch, flops, alias, single, hbm_in, hbm_out)


def pallas(kernel, out_shape, ins, smem, scratch, flops, alias, single, hbm_in, hbm_out):
    return pl.pallas_call(
        kernel,
        out_shape=out_shape,
        in_specs=[HBM] * hbm_in + [VMEM] * (len(ins) - smem - hbm_in) + [SMEM] * smem,
        out_specs=(HBM if hbm_out else VMEM) if single else [VMEM] * len(out_shape),
        scratch_shapes=list(scratch),
        input_output_aliases={alias: 0} if alias is not None else {},
        compiler_params=pltpu.CompilerParams(vmem_limit_bytes=40 * 1024 * 1024),
        cost_estimate=pl.CostEstimate(flops=flops, bytes_accessed=1 << 20, transcendentals=0) if flops else None,
    )(*ins)


def shards(
    charges, points, leaf_basis, transfer_one, transfer_two, couple_one, couple_two, near_list, list_one, list_two
):
    columns = charges.shape[1]
    leaves = near_list.shape[0]
    nodes = leaves // 8
    tops = nodes // 8
    depth = 4 * (leaves // 64)
    rows, cols = lax.axis_size("row"), lax.axis_size("col")
    merge = cols == 2 and tops == 1
    t1 = transfer_one.reshape(leaves * 32, 32)
    t2 = transfer_two.reshape(nodes * 32, 32)
    shape = jax.ShapeDtypeStruct
    width = 2 * depth * 128
    face = shape((80, width), BF16)
    outs = call(
        functools.partial(face_kernel, merge, depth),
        [shape((64, columns), BF16), shape((16, columns), BF16), face, face] + ([] if merge else [face]),
        [charges, points],
        scratch=[pltpu.VMEM((3, columns), F32), pltpu.SemaphoreType.DMA((2,))],
        hbm_in=2,
    )
    charges, feat, odd = outs[:3]
    up = [(i, i + 1) for i in range(cols - 1)]
    down = [(j, i) for i, j in up]
    if merge:
        left = right = lax.ppermute(outs[3], "col", up + down)
    else:
        left, right = lax.ppermute(outs[3], "col", up), lax.ppermute(outs[4], "col", down)
    odd = lax.ppermute(odd, "row", [p for i in range(1, rows - 1, 2) for p in ((i, i + 1), (i + 1, i))])
    even, coef = call(
        functools.partial(up_kernel, merge, depth),
        [shape((80, width + (128 if merge else 0)), BF16)]
        + [shape((16 * nodes + 32, 128) if merge else ((nodes + tops) * 32, 64), BF16)],
        [charges, feat, leaf_basis, t1, t2],
        flops=1 << 31,
    )
    even = lax.ppermute(even, "row", [(i, i ^ 1) for i in range(rows)])
    sel, sel_x, pick = constants()
    acc_shape = shape((2 * depth, 64, 512), F32)
    acc, x, mask, yt = call(
        functools.partial(own_kernel, depth),
        [
            acc_shape,
            shape((2 * depth, 96, 512), BF16),
            shape((2 * depth, 48, 512), F32),
            shape((2 * depth * SIDE, 128, 32), BF16),
        ],
        [charges, feat, near_list.T, sel, sel_x, pick],
        flops=1 << 32,
    )
    corner = shape((80, depth * 128 + (256 if merge else 0)), BF16)
    packed = call(
        functools.partial(corner_kernel, merge, depth),
        [corner] if merge else [corner, corner],
        [even, odd] + ([coef] if merge else []),
    )
    if merge:
        corner_left = corner_right = lax.ppermute(packed[0], "col", up + down)
        at = depth * 128 + 128
        top = jnp.stack([packed[0][48:80, at:], corner_left[48:80, at:]])
        top = doubled(top, "row", 2)
        one = [coef, corner_left]
    else:
        corner_left = lax.ppermute(packed[0], "col", up)
        corner_right = lax.ppermute(packed[1], "col", down)
        coef = doubled(coef.reshape(1, nodes + tops, 32, 64), "col")
        one = [coef[:, :nodes].reshape(cols * nodes, 32, 64)]
        top = doubled(coef[:, nodes:].reshape(1, cols * tops, 32, 64), "row").reshape(-1, 32, 64)
    acc = call(
        functools.partial(side_kernel, merge, depth),
        acc_shape,
        [charges, right] + ([] if merge else [left]) + [sel, x, mask, yt, acc],
        alias=6 if merge else 7,
        scratch=[pltpu.VMEM((2 * depth * SIDE, 64, 128), BF16), pltpu.VMEM((2 * depth * SIDE, 64, 64), BF16)],
        flops=1 << 32,
    )
    acc, edge_c, edge_y = call(
        functools.partial(edge_kernel, depth),
        [acc_shape, shape((4 * depth, 64, 128), BF16), shape((4 * depth, 128, 32), BF16)],
        [even, odd, sel, x, mask, acc],
        alias=5,
        flops=1 << 31,
    )
    field = call(
        functools.partial(couple_kernel, merge, cols * nodes),
        shape((nodes * 32, 64), F32),
        [couple_one, *one, list_one],
        smem=1,
        scratch=[pltpu.VMEM((2 * nodes + 1, 32, 64), BF16)] if merge else [],
        flops=1 << 30,
    )
    acc = call(
        functools.partial(last_kernel, merge, depth),
        acc_shape,
        [edge_c, edge_y, corner_right] + ([] if merge else [corner_left]) + [sel, x, mask, acc],
        alias=6 if merge else 7,
        scratch=[pltpu.VMEM((4 * depth, 64, 128), BF16), pltpu.VMEM((4 * depth, 64, 64), BF16)],
        flops=1 << 31,
    )
    return call(
        functools.partial(down_kernel, depth, merge),
        shape((64, columns), BF16),
        [acc, field, leaf_basis, t1, t2, couple_two, top, list_two],
        smem=1,
        scratch=[
            pltpu.VMEM((64, columns), BF16),
            pltpu.SemaphoreType.DMA((nodes,)),
            pltpu.VMEM((rows * cols * tops, 32, 64), BF16),
        ],
        hbm_out=True,
    )


def solution(mesh):
    line, block = P(None, ("row", "col")), P(("row", "col"))
    in_specs = (line, line, line) + (block,) * 7

    return jax.shard_map(shards, mesh=mesh, in_specs=in_specs, out_specs=line, check_vma=False)
```

time: 47.1 us -> 38.9 us (0.83)
  Pallas kernels: 25 us -> 14.7 us
  starting transfers between devices: 11.5 us -> 15.6 us
  local copies, waits for them, and re-layouts: 3.65 us -> 1.96 us
    pallas_call x7 -> x9, Pallas kernels: 25 us -> 14.7 us  [pallas(): pl.pallas_call(kernel, out_shape=out_shape, in_specs=[HBM] * hbm_in + [VM...]
    ppermute x3, starting transfers between devices: 7.71 us -> 10.2 us  [doubled(): other = lax.ppermute(value, axis, [(i, i ^ step) for i in range(size)])]
    ppermute x3, waiting for transfers between devices: 6.4 us -> 4.39 us  [doubled(): other = lax.ppermute(value, axis, [(i, i ^ step) for i in range(size)])]
    ppermute x1 -> x2, waiting for transfers between devices: 0.01 us -> 1.86 us  [the longest x1 1.86 us: shards(): corner_left = corner_right = lax.ppermute(packed[0], 'col', up + down)]
    unnamed x32 -> x29, local copies, waits for them, and re-layouts: 3.63 us -> 1.94 us
    ppermute x1 -> x2, starting transfers between devices: 3.03 us -> 4.26 us  [the longest x1 2.57 us: shards(): left = right = lax.ppermute(outs[3], 'col', up + down)]
  transfers between devices with their start and end apart: 6 -> 7, of which waited for: 2 -> 3; matrix products, arithmetic and copies ran while one was open for 0% -> 0% of each run, Pallas kernels for 37% -> 26%
where the time goes in v3:
time: 38.9 us; the launch traced here: 38.7 us
  starting transfers between devices  15.6 us (40%)
  Pallas kernels  14.7 us (38%)
  waiting for transfers between devices  6.26 us (16%)
  local copies, waits for them, and re-layouts  1.96 us (5%)
    pallas_call x9, Pallas kernels, pallas(): pl.pallas_call(kernel, out_shape=out_shape, in_specs=[HBM] * hbm_in + [VM...  14.7 us
    ppermute x3, starting transfers between devices, doubled(): other = lax.ppermute(value, axis, [(i, i ^ step) for i in range(size)])  10.2 us
    ppermute x3, waiting for transfers between devices, doubled(): other = lax.ppermute(value, axis, [(i, i ^ step) for i in range(size)])  4.39 us
    ppermute x1, starting transfers between devices, shards(): left = right = lax.ppermute(outs[3], 'col', up + down)  2.57 us
    unnamed x29, local copies, waits for them, and re-layouts  1.94 us
    ppermute x1, waiting for transfers between devices, shards(): corner_left = corner_right = lax.ppermute(packed[0], 'col', up + down)  1.86 us
    ppermute x1, starting transfers between devices, shards(): corner_left = corner_right = lax.ppermute(packed[0], 'col', up + down)  1.7 us
  transfers between devices with their start and end apart: 7, of which 3 were waited for; matrix products, arithmetic and copies ran while one was open for 0% of the time, Pallas kernels for 26%

profile of v3, /device:TPU:0, one launch (start us, length us, event | category | flops | bytes accessed | tf_op | source)
XLA Modules:
  0.0 38.7 jit_solution(5271837486334925187)
XLA Ops:
  0.0 1.8 %copy.17 = bf16[64,32,32]{2,1,0:T(8,128)(2,1)S(1)} copy(bf16[64,32,32]{0,2,1:T(8,128)(2,1)} %param.16) | data formatting | bytes 262144 | tf_op args[3]
  1.8 0.0 copy-done
  1.8 0.0 copy-done.3
  1.8 0.0 copy-start.1
  1.8 0.0 copy-start.4
  1.8 0.8 %shard_map.127 = (bf16[64,4096]{1,0:T(8,128)(2,1)S(1)}, bf16[16,4096]{1,0:T(8,128)(2,1)S(1)}, bf16[80,1024]{1,0:T(8,128)(2,1)S(1)}, bf16[80,1024]{1,0:T(8,128)(2,1)S(1)}) custom-call(bf16[64,4096]{1,0:T(8,128)(2,1)S(1)} %copy-done, f32[3,4096]{1,0:T(4,128)S(1)} %copy-done.3), custom_call_target="tpu_custom_call" | custom-call | tf_op jit(solution)/shard_map/pallas_call | solution.py:549
  2.7 0.1 copy-done.1
  2.8 0.0 copy-start.11
  2.8 1.1 %shard_map.128 = (bf16[80,1152]{1,0:T(8,128)(2,1)S(1)}, bf16[160,128]{1,0:T(8,128)(2,1)S(1)}) custom-call(bf16[64,4096]{1,0:T(8,128)(2,1)S(1)} %get-tuple-element.18.q_ref, bf16[16,4096]{1,0:T(8,128)(2,1)S(1)} %get-tuple-element.19.feat_ref, bf16[32,4096]{1,0:T(8,128)(2,1)S(1)} %copy-done.1, bf16[2048,32]{1,0:T(8,128)(2,1)S(1)} %bitcast.11, ...), custom_call_target="tpu_custom_call" | custom-call | flops 2147483648 | bytes 1048576 | tf_op jit(solution)/shard_map/pallas_call | solution.py:549
  3.8 0.5 %collective-permute-start = (bf16[80,1152]{1,0:T(8,128)(2,1)S(1)}, bf16[80,1152]{1,0:T(8,128)(2,1)S(1)}, u32[]{:S(2)}, u32[]{:S(2)}) collective-permute-start(bf16[80,1152]{1,0:T(8,128)(2,1)S(1)} %get-tuple-element.20), channel_id=1, source_target_pairs={{0,2},{2,0},{4,6},{6,4},{8,10},{10,8},{12,14},{14,12},{16,18},{18,... | collective-permute-start | bytes 552968 | tf_op jit(solution)/shard_map/ppermute | solution.py:598
  4.4 0.7 %collective-permute-start.1 = (bf16[80,1024]{1,0:T(8,128)(2,1)S(1)}, bf16[80,1024]{1,0:T(8,128)(2,1)S(1)}, u32[]{:S(2)}, u32[]{:S(2)}) collective-permute-start(bf16[80,1024]{1,0:T(8,128)(2,1)S(1)} %get-tuple-element.21), channel_id=1, source_target_pairs={{2,4},{4,2},{6,8},{8,6},{10,12},{12,10},{14,16},{16,14},{18,20},{2... | collective-permute-start | bytes 491528 | tf_op jit(solution)/shard_map/ppermute | solution.py:590
  5.0 2.6 %collective-permute-start.2 = (bf16[80,1024]{1,0:T(8,128)(2,1)S(1)}, bf16[80,1024]{1,0:T(8,128)(2,1)S(1)}, u32[]{:S(2)}, u32[]{:S(2)}) collective-permute-start(bf16[80,1024]{1,0:T(8,128)(2,1)S(1)} %get-tuple-element.24), channel_id=1, source_target_pairs={{0,1},{1,0},{2,3},{3,2},{4,5},{5,4},{6,7},{7,6},{8,9},{9,8},{10,11... | collective-permute-start | bytes 491528 | tf_op jit(solution)/shard_map/ppermute | solution.py:587
  7.6 0.0 copy-done.11
  7.6 3.7 %shard_map.129 = (f32[8,64,512]{2,1,0:T(8,128)S(1)}, bf16[8,96,512]{2,1,0:T(8,128)(2,1)S(1)}, f32[8,48,512]{2,1,0:T(8,128)S(1)}, bf16[32,128,32]{2,1,0:T(8,128)(2,1)S(1)}) custom-call(bf16[64,4096]{1,0:T(8,128)(2,1)S(1)} %get-tuple-element.18.q_ref, bf16[16,4096]{1,0:T(8,128)(2,1)S(1)} %get-tuple-element.19.feat_ref, s32[27,64]{1,0:T(8,128)S(1)} %bitcast.15, ...), custom_call_target="tpu_custom_call" | custom-call | flops 4294967296 | bytes 1048576 | tf_op jit(solution)/shard_map/pallas_call | solution.py:549
  11.3 0.0 collective-permute-done.2.right_ref
  11.3 2.8 %shard_map.130.in_ref = f32[8,64,512]{2,1,0:T(8,128)S(1)} custom-call(bf16[64,4096]{1,0:T(8,128)(2,1)S(1)} %get-tuple-element.18.q_ref, bf16[80,1024]{1,0:T(8,128)(2,1)S(1)} %collective-permute-done.2.right_ref, bf16[16,160]{1,0:T(8,128)(2,1)S(1)} %copy-done.10, ...), custom_call_target="tpu_custom_call", output_to_operand_aliasing={{}: (6, {})} | custom-call | flops 4294967296 | bytes 1048576 | tf_op jit(solution)/shard_map/pallas_call | solution.py:549
  14.1 0.0 collective-permute-done.1.odd_ref
  14.1 0.0 collective-permute-done.even_ref
  14.1 0.2 shard_map.132
  14.3 1.7 %collective-permute-start.3 = (bf16[80,768]{1,0:T(8,128)(2,1)S(1)}, bf16[80,768]{1,0:T(8,128)(2,1)S(1)}, u32[]{:S(2)}, u32[]{:S(2)}) collective-permute-start(bf16[80,768]{1,0:T(8,128)(2,1)S(1)} %shard_map.132), channel_id=1, source_target_pairs={{0,1},{1,0},{2,3},{3,2},{4,5},{5,4},{6,7},{7,6},{8,9},{9,8},{10,11... | collective-permute-start | bytes 368648 | tf_op jit(solution)/shard_map/ppermute | solution.py:619
  16.0 1.4 %shard_map.131 = (f32[8,64,512]{2,1,0:T(8,128)S(1)}, bf16[16,64,128]{2,1,0:T(8,128)(2,1)S(1)}, bf16[16,128,32]{2,1,0:T(8,128)(2,1)S(1)}) custom-call(bf16[80,1152]{1,0:T(8,128)(2,1)S(1)} %collective-permute-done.even_ref, bf16[80,1024]{1,0:T(8,128)(2,1)S(1)} %collective-permute-done.1.odd_ref, ...), custom_call_target="tpu_custom_call", output_to_operand_aliasing={{0}: (5, {})} | custom-call | flops 2147483648 | bytes 1048576 | tf_op jit(solution)/shard_map/pallas_call | solution.py:549
  17.4 1.9 %collective-permute-done.3.right_ref.refs_1_ = bf16[80,768]{1,0:T(8,128)(2,1)S(1)} collective-permute-done((bf16[80,768]{1,0:T(8,128)(2,1)S(1)}, bf16[80,768]{1,0:T(8,128)(2,1)S(1)}, u32[]{:S(2)}, u32[]{:S(2)}) %collective-permute-start.3) | collective-permute-done | bytes 122912 | tf_op jit(solution)/shard_map/ppermute | solution.py:619
  19.3 5.4 %collective-permute-start.4 = (bf16[2,32,128]{2,1,0:T(8,128)(2,1)S(1)}, bf16[2,32,128]{2,1,0:T(8,128)(2,1)S(1)}, u32[]{:S(2)}, u32[]{:S(2)}) collective-permute-start(bf16[2,32,128]{2,1,0:T(8,128)(2,1)S(1)} %pad_maximum_fusion.2), channel_id=1, source_target_pairs={{0,4},{2,6},{4,0},{6,2},{8,12},{10,14},{12,8},{14,10},{16,20},{18,... | collective-permute-start | bytes 49160 | tf_op jit(solution)/shard_map/ppermute | solution.py:537
  24.7 1.3 %shard_map.133.acc_ref = f32[8,64,512]{2,1,0:T(8,128)S(1)} custom-call(bf16[16,64,128]{2,1,0:T(8,128)(2,1)S(1)} %get-tuple-element.27.edge_c_ref, bf16[16,128,32]{2,1,0:T(8,128)(2,1)S(1)} %get-tuple-element.28.edge_y_ref, bf16[80,768]{1,0:T(8,128)(2,1)S(1)} %collective-permute-done.3.right_ref.refs_1_, ...), custom_call_target="tpu_custom_call", output_to_operand_aliasing={{}: (6, {})} | custom-call | flops 2147483648 | bytes 1048576 | tf_op jit(solution)/shard_map/pallas_call | solution.py:549
  26.0 0.0 copy-done.6
  26.1 1.0 %shard_map.134.f1_ref = f32[256,64]{1,0:T(8,128)S(1)} custom-call(bf16[8,12,32,32]{3,2,1,0:T(8,128)(2,1)S(1)} %copy-done.6, bf16[160,128]{1,0:T(8,128)(2,1)S(1)} %get-tuple-element.29.refs_0_, bf16[80,768]{1,0:T(8,128)(2,1)S(1)} %collective-permute-done.3.right_ref.refs_1_, s32[8,12]{1,0:T(8,128)S(1)} %copy-done.8), custom_call_target="tpu_custom_call" | custom-call | flops 1073741824 | bytes 1048576 | tf_op jit(solution)/shard_map/pallas_call | solution.py:549
  27.1 0.0 collective-permute-done.4
  27.1 1.9 %collective-permute-start.5 = (bf16[4,32,128]{2,1,0:T(8,128)(2,1)S(1)}, bf16[4,32,128]{2,1,0:T(8,128)(2,1)S(1)}, u32[]{:S(2)}, u32[]{:S(2)}) collective-permute-start(bf16[4,32,128]{2,1,0:T(8,128)(2,1)S(1)} %pad_maximum_fusion.1), channel_id=1, source_target_pairs={{0,8},{2,10},{4,12},{6,14},{8,0},{10,2},{12,4},{14,6},{16,24},{18,... | collective-permute-start | bytes 98312 | tf_op jit(solution)/shard_map/ppermute | solution.py:537
  29.0 2.1 %collective-permute-done.5 = bf16[4,32,128]{2,1,0:T(8,128)(2,1)S(1)} collective-permute-done((bf16[4,32,128]{2,1,0:T(8,128)(2,1)S(1)}, bf16[4,32,128]{2,1,0:T(8,128)(2,1)S(1)}, u32[]{:S(2)}, u32[]{:S(2)}) %collective-permute-start.5) | collective-permute-done | bytes 32800 | tf_op jit(solution)/shard_map/ppermute | solution.py:537
  31.1 2.9 %collective-permute-start.6 = (bf16[8,32,128]{2,1,0:T(8,128)(2,1)S(1)}, bf16[8,32,128]{2,1,0:T(8,128)(2,1)S(1)}, u32[]{:S(2)}, u32[]{:S(2)}) collective-permute-start(bf16[8,32,128]{2,1,0:T(8,128)(2,1)S(1)} %pad_maximum_fusion), channel_id=1, source_target_pairs={{0,16},{2,18},{4,20},{6,22},{8,24},{10,26},{12,28},{14,30},{16,0},... | collective-permute-start | bytes 196616 | tf_op jit(solution)/shard_map/ppermute | solution.py:537
  34.0 2.3 %collective-permute-done.6 = bf16[8,32,128]{2,1,0:T(8,128)(2,1)S(1)} collective-permute-done((bf16[8,32,128]{2,1,0:T(8,128)(2,1)S(1)}, bf16[8,32,128]{2,1,0:T(8,128)(2,1)S(1)}, u32[]{:S(2)}, u32[]{:S(2)}) %collective-permute-start.6) | collective-permute-done | bytes 65568 | tf_op jit(solution)/shard_map/ppermute | solution.py:537
  36.3 2.4 %shard_map.135 = bf16[64,4096]{1,0:T(8,128)(2,1)} custom-call(f32[8,64,512]{2,1,0:T(8,128)S(1)} %shard_map.133.acc_ref, f32[256,64]{1,0:T(8,128)S(1)} %shard_map.134.f1_ref, bf16[32,4096]{1,0:T(8,128)(2,1)S(1)} %copy-done.1, bf16[2048,32]{1,0:T(8,128)(2,1)S(1)} %bitcast.12, bf16[256,32]{1,0:T(8,128)(2,1)S(1)} %bitcast.14, ...), custom_call_target="tpu_custom_call" | custom-call | tf_op jit(solution)/shard_map/pallas_call | solution.py:549
  (26 shorter events, 0.1 us)
Async XLA Ops:
  0.0 1.8 %copy-start = (bf16[64,4096]{1,0:T(8,128)(2,1)S(1)}, bf16[64,4096]{1,0:T(8,128)(2,1)}, u32[]{:S(2)}) copy-start(bf16[64,4096]{1,0:T(8,128)(2,1)} %q_hbm.1) | copy-start | bytes 1572868
  0.0 1.8 %copy-start.3 = (f32[3,4096]{1,0:T(4,128)S(1)}, f32[3,4096]{1,0:T(4,128)}, u32[]{:S(2)}) copy-start(f32[3,4096]{1,0:T(4,128)} %pts_hbm.1) | copy-start | bytes 147460
  1.8 1.0 %copy-start.1 = (bf16[32,4096]{1,0:T(8,128)(2,1)S(1)}, bf16[32,4096]{1,0:T(8,128)(2,1)}, u32[]{:S(2)}) copy-start(bf16[32,4096]{1,0:T(8,128)(2,1)} %basis_ref.3) | copy-start | bytes 786436
  1.8 0.9 %copy-start.4 = (bf16[8,32,32]{2,1,0:T(8,128)(2,1)S(1)}, bf16[8,32,32]{2,1,0:T(8,128)(2,1)}, u32[]{:S(2)}) copy-start(bf16[8,32,32]{2,1,0:T(8,128)(2,1)} %param.17) | copy-start | bytes 49156
  2.8 4.8 %copy-start.7 = (s32[64,27]{0,1:T(8,128)S(1)}, s32[64,27]{0,1:T(8,128)}, u32[]{:S(2)}) copy-start(s32[64,27]{0,1:T(8,128)} %param.20) | copy-start | bytes 20740
  2.8 4.8 %copy-start.9 = (bf16[96,27]{1,0:T(8,128)(2,1)S(1)}, bf16[96,27]{1,0:T(8,128)(2,1)}, u32[]{:S(2)}) copy-start(bf16[96,27]{1,0:T(8,128)(2,1)} %constant.8.clone.pick_ref) | copy-start | bytes 15556
  2.8 4.8 %copy-start.10 = (bf16[16,160]{1,0:T(8,128)(2,1)S(1)}, bf16[16,160]{1,0:T(8,128)(2,1)}, u32[]{:S(2)}) copy-start(bf16[16,160]{1,0:T(8,128)(2,1)} %constant.6.clone.sel_ref.refs_0_) | copy-start | bytes 15364
  2.8 4.8 %copy-start.11 = (bf16[32,16]{1,0:T(8,128)(2,1)S(1)}, bf16[32,16]{1,0:T(8,128)(2,1)}, u32[]{:S(2)}) copy-start(bf16[32,16]{1,0:T(8,128)(2,1)} %constant.7.clone.sel_x_ref) | copy-start | bytes 3076
  3.8 10.3 %collective-permute-start = (bf16[80,1152]{1,0:T(8,128)(2,1)S(1)}, bf16[80,1152]{1,0:T(8,128)(2,1)S(1)}, u32[]{:S(2)}, u32[]{:S(2)}) collective-permute-start(bf16[80,1152]{1,0:T(8,128)(2,1)S(1)} %get-tuple-element.20), channel_id=1, source_target_pairs={{0,2},{2,0},{4,6},{6,4},{8,10},{10,8},{12,14},{14,12},{16,18},{18,... | collective-permute-start | bytes 552968 | tf_op jit(solution)/shard_map/ppermute | solution.py:598
  4.4 9.7 %collective-permute-start.1 = (bf16[80,1024]{1,0:T(8,128)(2,1)S(1)}, bf16[80,1024]{1,0:T(8,128)(2,1)S(1)}, u32[]{:S(2)}, u32[]{:S(2)}) collective-permute-start(bf16[80,1024]{1,0:T(8,128)(2,1)S(1)} %get-tuple-element.21), channel_id=1, source_target_pairs={{2,4},{4,2},{6,8},{8,6},{10,12},{12,10},{14,16},{16,14},{18,20},{2... | collective-permute-start | bytes 491528 | tf_op jit(solution)/shard_map/ppermute | solution.py:590
  5.0 6.2 %collective-permute-start.2 = (bf16[80,1024]{1,0:T(8,128)(2,1)S(1)}, bf16[80,1024]{1,0:T(8,128)(2,1)S(1)}, u32[]{:S(2)}, u32[]{:S(2)}) collective-permute-start(bf16[80,1024]{1,0:T(8,128)(2,1)S(1)} %get-tuple-element.24), channel_id=1, source_target_pairs={{0,1},{1,0},{2,3},{3,2},{4,5},{5,4},{6,7},{7,6},{8,9},{9,8},{10,11... | collective-permute-start | bytes 491528 | tf_op jit(solution)/shard_map/ppermute | solution.py:587
  14.3 4.9 %collective-permute-start.3 = (bf16[80,768]{1,0:T(8,128)(2,1)S(1)}, bf16[80,768]{1,0:T(8,128)(2,1)S(1)}, u32[]{:S(2)}, u32[]{:S(2)}) collective-permute-start(bf16[80,768]{1,0:T(8,128)(2,1)S(1)} %shard_map.132), channel_id=1, source_target_pairs={{0,1},{1,0},{2,3},{3,2},{4,5},{5,4},{6,7},{7,6},{8,9},{9,8},{10,11... | collective-permute-start | bytes 368648 | tf_op jit(solution)/shard_map/ppermute | solution.py:619
  19.3 7.8 %collective-permute-start.4 = (bf16[2,32,128]{2,1,0:T(8,128)(2,1)S(1)}, bf16[2,32,128]{2,1,0:T(8,128)(2,1)S(1)}, u32[]{:S(2)}, u32[]{:S(2)}) collective-permute-start(bf16[2,32,128]{2,1,0:T(8,128)(2,1)S(1)} %pad_maximum_fusion.2), channel_id=1, source_target_pairs={{0,4},{2,6},{4,0},{6,2},{8,12},{10,14},{12,8},{14,10},{16,20},{18,... | collective-permute-start | bytes 49160 | tf_op jit(solution)/shard_map/ppermute | solution.py:537
  24.7 1.4 %copy-start.6 = (bf16[8,12,32,32]{3,2,1,0:T(8,128)(2,1)S(1)}, bf16[8,12,32,32]{3,2,1,0:T(8,128)(2,1)}, u32[]{:S(2)}) copy-start(bf16[8,12,32,32]{3,2,1,0:T(8,128)(2,1)} %k1_ref.1) | copy-start | bytes 589828
  24.7 1.4 %copy-start.8 = (s32[8,12]{1,0:T(8,128)S(1)}, s32[8,12]{1,0:T(8,128)}, u32[]{:S(2)}) copy-start(s32[8,12]{1,0:T(8,128)} %refs_2_.1) | copy-start | bytes 1156
  27.1 4.0 %collective-permute-start.5 = (bf16[4,32,128]{2,1,0:T(8,128)(2,1)S(1)}, bf16[4,32,128]{2,1,0:T(8,128)(2,1)S(1)}, u32[]{:S(2)}, u32[]{:S(2)}) collective-permute-start(bf16[4,32,128]{2,1,0:T(8,128)(2,1)S(1)} %pad_maximum_fusion.1), channel_id=1, source_target_pairs={{0,8},{2,10},{4,12},{6,14},{8,0},{10,2},{12,4},{14,6},{16,24},{18,... | collective-permute-start | bytes 98312 | tf_op jit(solution)/shard_map/ppermute | solution.py:537
  29.0 7.3 %copy-start.2 = (bf16[1,16,32,32]{3,2,1,0:T(8,128)(2,1)S(1)}, bf16[1,16,32,32]{3,2,1,0:T(8,128)(2,1)}, u32[]{:S(2)}) copy-start(bf16[1,16,32,32]{3,2,1,0:T(8,128)(2,1)} %k2_ref.1) | copy-start | bytes 98308
  31.1 5.2 %collective-permute-start.6 = (bf16[8,32,128]{2,1,0:T(8,128)(2,1)S(1)}, bf16[8,32,128]{2,1,0:T(8,128)(2,1)S(1)}, u32[]{:S(2)}, u32[]{:S(2)}) collective-permute-start(bf16[8,32,128]{2,1,0:T(8,128)(2,1)S(1)} %pad_maximum_fusion), channel_id=1, source_target_pairs={{0,16},{2,18},{4,20},{6,22},{8,24},{10,26},{12,28},{14,30},{16,0},... | collective-permute-start | bytes 196616 | tf_op jit(solution)/shard_map/ppermute | solution.py:537
  34.0 2.3 %copy-start.5 = (s32[1,16]{1,0:T(1,128)S(1)}, s32[1,16]{1,0:T(1,128)}, u32[]{:S(2)}) copy-start(s32[1,16]{1,0:T(1,128)} %l2_ref.1) | copy-start | bytes 196

commit v4 on v3

--- a/solution.py
+++ b/solution.py
@@ -17,6 +17,12 @@
 NT = (((1,), (1,)), ((), ()))
 TN = (((0,), (0,)), ((), ()))
 NN = (((1,), (0,)), ((), ()))
+
+
+def split_layers(depth):
+    return range(0, depth // 4), range(depth // 4, depth // 2), range(depth // 2, depth)
+
+
 VMEM = pl.BlockSpec(memory_space=pltpu.VMEM)
 SMEM = pl.BlockSpec(memory_space=pltpu.SMEM)
 HBM = pl.BlockSpec(memory_space=pltpu.MemorySpace.HBM)
@@ -127,14 +133,10 @@
     pay_ref[64:80, 0:width] = feature_rows([x[0], x[1] + shift, x[2]])
 
 
-def face_kernel(merge, depth, q_hbm, pts_hbm, q_ref, feat_ref, odd_ref, xpay_ref, *more):
-    pts_ref, sems = more[-2:]
-    copies = [
-        pltpu.make_async_copy(pts_hbm, pts_ref, sems.at[0]),
-        pltpu.make_async_copy(q_hbm, q_ref, sems.at[1]),
-    ]
-    for copy in copies:
-        copy.start()
+def face_kernel(merge, depth, q_ref, pts_ref, *refs):
+    if merge:
+        coef_ref, *refs = refs
+    feat_ref, even_ref, odd_ref, xpay_ref, *more = refs
     row, col = lax.axis_index("row"), lax.axis_index("col")
     columns = q_ref.shape[1]
     centre = (
@@ -142,14 +144,12 @@
         (SIDE * row + SIDE // 2).astype(F32),
         jnp.float32(depth / 2),
     )
-    copies[0].wait()
     local = [pts_ref[c : c + 1, :] - centre[c] for c in range(3)]
     feat = feature_rows(local)
     feat_ref[...] = feat
     pair_x = lax.broadcasted_iota(jnp.int32, (1, columns), 1) // 512 % 2
     shift = jnp.where(pair_x == 1, -float(SIDE), float(SIDE))
     moved = feature_rows([local[0] + shift, local[1], local[2]])
-    copies[1].wait()
 
     def tile(z, y, x1):
         at = tile_of(z, y, x1) * 128
@@ -163,14 +163,23 @@
         low = lower_half((80, 128)) == (col == 0)
         for k, (a, b) in enumerate(zip(swapped(first), second)):
             xpay_ref[:, 128 * k : 128 * k + 128] = jnp.where(low, a, b)
+        width = 2 * depth * 128
+        blocks = jnp.concatenate([coef_ref[...], jnp.zeros((160 - coef_ref.shape[0], 128), BF16)], axis=0)
+        for k in range(2):
+            xpay_ref[:, width + 128 * k : width + 128 * k + 128] = blocks[80 * k : 80 * k + 80]
     else:
         for ref, x1 in ((xpay_ref, 1), (more[0], 0)):
             for k, value in enumerate(halves(*sides[x1], x1)):
                 ref[:, 128 * k : 128 * k + 128] = value
     send_rows(odd_ref, row % 2 == 1, q_ref, feat, depth)
-
-
-def up_kernel(merge, depth, q_ref, feat_ref, basis_ref, t1_ref, t2_ref, even_ref, coef_ref):
+    send_rows(even_ref, row % 2 == 0, q_ref, feat, depth)
+
+
+def up_kernel(merge, q_ref, basis_ref, t1_ref, t2_ref, *refs):
+    if merge:
+        coef_ref, top_ref = refs
+    else:
+        coef_ref = refs[0]
     nodes = q_ref.shape[1] // 512
     leaf = []
     for n in range(nodes):
@@ -181,15 +190,11 @@
     for m in range(nodes // 8):
         part = jnp.concatenate(ones[8 * m : 8 * m + 8], axis=0)
         tops.append(dot(t2_ref[256 * m : 256 * m + 256, :], part, TN).astype(BF16))
-    send_rows(even_ref, lax.axis_index("row") % 2 == 0, q_ref, feat_ref, depth)
-    if merge:
-        for k in range(nodes // 2):
-            coef_ref[32 * k : 32 * k + 32, :] = jnp.concatenate([ones[2 * k], ones[2 * k + 1]], axis=1)
-        both = jnp.concatenate([tops[0], tops[0]], axis=1)
-        coef_ref[16 * nodes : 16 * nodes + 32, :] = both
-        width = 2 * depth * 128
-        even_ref[0:32, width : width + 128] = both
-        even_ref[32:80, width : width + 128] = jnp.zeros((48, 128), BF16)
+    if merge:
+        pairs = [jnp.concatenate([ones[2 * k], ones[2 * k + 1]], axis=1) for k in range(nodes // 2)]
+        for k, value in enumerate(pairs):
+            coef_ref[32 * k : 32 * k + 32, :] = value
+        top_ref[0] = tops[0]
     else:
         for k, value in enumerate(ones + tops):
             coef_ref[32 * k : 32 * k + 32, :] = value
@@ -208,7 +213,7 @@
 def corner_kernel(merge, depth, even_ref, odd_ref, *refs):
     col = lax.axis_index("col")
     face = row_sides(even_ref, odd_ref)
-    coef_ref, pay_ref = refs if merge else (None, refs[0])
+    pay_ref = refs[0]
     tiles = [[[face(side, (z * 2 + k) * 128) for z in range(depth)] for side in range(2)] for k in range(2)]
     high, base = halves(*tiles[1], 1), halves(*tiles[0], 0)
     groups = [(pay_ref, jnp.concatenate(high, axis=1), -float(SIDE))]
@@ -222,22 +227,21 @@
         ref[0:64, 0:width] = tile[0:64]
         x = coordinates(tile[64:80].astype(F32))
         ref[64:80, 0:width] = feature_rows([x[0] + shift, x[1], x[2]])
-    if merge:
-        rest = coef_ref.shape[0] - 32
-        other = even_ref[0:32, 2 * depth * 128 : 2 * depth * 128 + 128]
-        tops = jnp.where(lower_half((32, 128)), coef_ref[rest : rest + 32, :], other)
-        blocks = jnp.concatenate([coef_ref[0:rest, :], tops], axis=0)
-        for k in range(blocks.shape[0] // 80):
-            pay_ref[:, width + 128 * k : width + 128 * k + 128] = blocks[80 * k : 80 * k + 80]
+
+
+def tops_kernel(top_ref, out_ref):
+    half = out_ref.shape[0]
+    for k in range(half):
+        out_ref[k] = jnp.concatenate([top_ref[k], top_ref[half + k]], axis=1)
 
 
 def layers_of(depth, tz):
     return [sz for sz in (tz - 1, tz, tz + 1) if 0 <= sz < depth]
 
 
-def inner_steps(depth):
+def inner_steps(depth, targets):
     steps = []
-    for tz in range(depth):
+    for tz in targets:
         layers = layers_of(depth, tz)
         for sz in layers:
             steps.append((tz, (0, 1), [(sz, 1), (sz, 2)]))
@@ -258,18 +262,20 @@
 
 
 def scan(steps, depth, rows_of, charge_of, x_ref, mask_ref, acc_ref, fresh=False):
-    def pair(xp, carry):
+    steps = [(xp, *step) for xp in range(2) for step in steps]
+
+    def pair():
         ready, seen = [], set()
         for i in range(len(steps) + AHEAD):
             if i < len(steps):
-                sides, (tz, tiles, sources) = steps[i]
+                xp, sides, (tz, tiles, sources) = steps[i]
                 lanes = slice(128 * tiles[0], 128 * tiles[-1] + 128)
                 at = xp * depth + tz
                 rows = jnp.concatenate([rows_of(sides, xp, sz, ye) for sz, ye in sources], axis=0)
                 features = x_ref[at, 32:96, lanes] if sides else x_ref[at, 0:32, lanes]
                 ready.append(lax.rsqrt(dot(rows, features).astype(BF16)))
             if i >= AHEAD:
-                sides, (tz, tiles, sources) = steps[i - AHEAD]
+                xp, sides, (tz, tiles, sources) = steps[i - AHEAD]
                 inv, ready[i - AHEAD] = ready[i - AHEAD], None
                 lanes = slice(128 * tiles[0], 128 * tiles[-1] + 128)
                 at = xp * depth + tz
@@ -288,17 +294,16 @@
                 kernel = columns[0] if len(columns) == 1 else jnp.concatenate(columns, axis=1)
                 charge = jnp.concatenate([charge_of(sides, xp, sz, ye) for sz, ye in sources], axis=1)
                 value = dot(charge, kernel)
-                if fresh and len(tiles) == 2 and (tz, tiles) not in seen:
-                    seen.add((tz, tiles))
+                if fresh and len(tiles) == 2 and (xp, tz, tiles) not in seen:
+                    seen.add((xp, tz, tiles))
                     acc_ref[at, :, lanes] = value
                 else:
                     acc_ref[at, :, lanes] += value
-        return carry
-
-    lax.fori_loop(0, 2, pair, 0)
-
-
-def own_kernel(depth, q_ref, feat_ref, nl_ref, sel_ref, sel_x_ref, pick_ref, acc_ref, x_ref, mask_ref, yt_ref):
+
+    pair()
+
+
+def own_kernel(depth, targets, q_ref, feat_ref, nl_ref, sel_ref, sel_x_ref, pick_ref, acc_ref, x_ref, mask_ref, yt_ref):
     columns = q_ref.shape[1]
     leaves = columns // 64
     x = dot(sel_x_ref[...], feat_ref[...])
@@ -328,27 +333,35 @@
                 mask_ref[xp * depth + z, :, lanes] = masks[:, at : at + 128]
                 yt_ref[(xp * depth + z) * SIDE + y] = rows[at : at + 128]
 
+    own_steps(depth, targets, q_ref, x_ref, mask_ref, yt_ref, acc_ref)
+
+
+def own_steps(depth, targets, q_ref, x_ref, mask_ref, yt_ref, acc_ref):
     def rows_of(sides, xp, sz, ye):
         return yt_ref[(xp * depth + sz) * SIDE + ye - 1]
 
     def charge_of(sides, xp, sz, ye):
-        base = pl.multiple_of(tile_of(sz, ye - 1, xp) * 128, 128)
-        return q_ref[:, pl.ds(base, 128)]
-
-    steps = [(False, step) for step in inner_steps(depth)]
+        base = tile_of(sz, ye - 1, xp) * 128
+        return q_ref[:, base : base + 128]
+
+    steps = [(False, step) for step in inner_steps(depth, targets)]
     scan(steps, depth, rows_of, charge_of, x_ref, mask_ref, acc_ref, fresh=True)
+
+
+def more_own_kernel(depth, targets, q_ref, x_ref, mask_ref, yt_ref, in_ref, acc_ref):
+    own_steps(depth, targets, q_ref, x_ref, mask_ref, yt_ref, acc_ref)
 
 
 def beside(right, left):
     return jnp.concatenate([right, left], axis=1)
 
 
-def side_kernel(merge, depth, q_ref, right_ref, *refs):
+def side_kernel(merge, depth, targets, q_ref, right_ref, *refs):
     if not merge:
         left_ref, *refs = refs
     sel_ref, x_ref, mask_ref, yt_ref, _, acc_ref, c_ref, ys_ref = refs
     low = lower_half((64, 128))
-    count = right_ref.shape[1] // 128
+    count = 2 * depth
     rights = tiles_in(right_ref, 0, count)
     lefts = rights if merge else tiles_in(left_ref, 0, count)
     beyond = [tile for pair in unpacked(rights, lefts) for tile in pair]
@@ -363,13 +376,22 @@
             ys_ref[even] = beside(yt_ref[odd, 0:64], rows[64:128])
             ys_ref[odd] = beside(rows[0:64], yt_ref[even, 64:128])
 
+    side_steps(depth, targets, x_ref, mask_ref, c_ref, ys_ref, acc_ref)
+
+
+def side_steps(depth, targets, x_ref, mask_ref, c_ref, ys_ref, acc_ref):
     def rows_of(sides, xp, sz, ye):
         return ys_ref[(xp * depth + sz) * SIDE + ye - 1]
 
     def charge_of(sides, xp, sz, ye):
         return c_ref[(xp * depth + sz) * SIDE + ye - 1]
 
-    scan([(True, step) for step in inner_steps(depth)], depth, rows_of, charge_of, x_ref, mask_ref, acc_ref)
+    steps = [(True, step) for step in inner_steps(depth, targets)]
+    scan(steps, depth, rows_of, charge_of, x_ref, mask_ref, acc_ref)
+
+
+def more_side_kernel(depth, targets, x_ref, mask_ref, c_ref, ys_ref, in_ref, acc_ref):
+    side_steps(depth, targets, x_ref, mask_ref, c_ref, ys_ref, acc_ref)
 
 
 def edge_steps(depth, sides):
@@ -458,16 +480,24 @@
         out_ref[32 * n : 32 * n + 32, :] = totals[n]
 
 
-def down_kernel(depth, wide, acc_ref, f1_ref, basis_ref, t1_ref, t2_ref, k2_ref, top_ref, l2_ref, out_hbm, *refs):
-    out_ref, sems, top_scr = refs
+def down_kernel(depth, merge, acc_ref, f1_ref, basis_ref, t1_ref, t2_ref, k2_ref, top_ref, *refs):
+    if merge:
+        got_ref, *refs = refs
+    l2_ref, out_hbm, out_ref, sems, top_scr = refs
     row, col = lax.axis_index("row"), lax.axis_index("col")
     nodes = out_hbm.shape[1] // 512
     per = nodes // 8
     me = row * lax.axis_size("col") + col
-    if wide:
-        for k in range(top_ref.shape[0]):
-            top_scr[(k // 2) * 4 + k % 2] = top_ref[k, :, 0:64]
-            top_scr[(k // 2) * 4 + 2 + k % 2] = top_ref[k, :, 64:128]
+    if merge:
+        count = top_ref.shape[0]
+        bits = count.bit_length() - 1
+        place = [sum(((k >> b) & 1) << (bits - 1 - b) for b in range(bits)) for k in range(count)]
+        for k in range(count // 2):
+            block = got_ref[k]
+            top_scr[2 * place[k] + 1] = block[:, 0:64]
+            top_scr[2 * place[k + count // 2] + 1] = block[:, 64:128]
+        for k in range(count):
+            top_scr[2 * place[k]] = top_ref[k]
     else:
         top_scr[...] = top_ref[...]
     copies = []
@@ -530,11 +560,15 @@
     return [jnp.asarray(v, BF16) for v in (sel, sel_x, pick)]
 
 
+def permuted(value, axis, pairs):
+    return lax.ppermute(value, axis, pairs)
+
+
 def doubled(value, axis, start=1):
     size = lax.axis_size(axis)
     step = start
     while step < size:
-        other = lax.ppermute(value, axis, [(i, i ^ step) for i in range(size)])
+        other = permuted(value, axis, [(i, i ^ step) for i in range(size)])
         value = jnp.concatenate([value, other], axis=0)
         step *= 2
     return value
@@ -573,33 +607,47 @@
     shape = jax.ShapeDtypeStruct
     width = 2 * depth * 128
     face = shape((80, width), BF16)
+    up = [(i, i + 1) for i in range(cols - 1)]
+    down = [(j, i) for i, j in up]
+    corner_width = depth * 128
+    ups = call(
+        functools.partial(up_kernel, merge),
+        [shape((16 * nodes, 128), BF16), shape((1, 32, 64), BF16)]
+        if merge
+        else [shape(((nodes + tops) * 32, 64), BF16)],
+        [charges, leaf_basis, t1, t2],
+        flops=1 << 31,
+    )
+    coef = ups[0]
     outs = call(
         functools.partial(face_kernel, merge, depth),
-        [shape((64, columns), BF16), shape((16, columns), BF16), face, face] + ([] if merge else [face]),
-        [charges, points],
-        scratch=[pltpu.VMEM((3, columns), F32), pltpu.SemaphoreType.DMA((2,))],
-        hbm_in=2,
-    )
-    charges, feat, odd = outs[:3]
-    up = [(i, i + 1) for i in range(cols - 1)]
-    down = [(j, i) for i, j in up]
-    if merge:
-        left = right = lax.ppermute(outs[3], "col", up + down)
+        [shape((16, columns), BF16), face, face]
+        + ([shape((80, width + 256), BF16)] if merge else [face, face]),
+        [charges, points] + ([coef] if merge else []),
+        flops=1 << 31,
+    )
+    feat, even, odd, pay = outs[:4]
+    odd = permuted(odd, "row", [p for i in range(1, rows - 1, 2) for p in ((i, i + 1), (i + 1, i))])
+    even = permuted(even, "row", [(i, i ^ 1) for i in range(rows)])
+    if merge:
+        left = right = permuted(pay, "col", up + down)
+        top = ups[1]
+        step = rows // 2
+        while step:
+            other = permuted(top, "row", [(i, i ^ step) for i in range(rows)])
+            top = jnp.concatenate([top, other], axis=0)
+            step //= 2
+        one = [coef, right]
     else:
-        left, right = lax.ppermute(outs[3], "col", up), lax.ppermute(outs[4], "col", down)
-    odd = lax.ppermute(odd, "row", [p for i in range(1, rows - 1, 2) for p in ((i, i + 1), (i + 1, i))])
-    even, coef = call(
-        functools.partial(up_kernel, merge, depth),
-        [shape((80, width + (128 if merge else 0)), BF16)]
-        + [shape((16 * nodes + 32, 128) if merge else ((nodes + tops) * 32, 64), BF16)],
-        [charges, feat, leaf_basis, t1, t2],
-        flops=1 << 31,
-    )
-    even = lax.ppermute(even, "row", [(i, i ^ 1) for i in range(rows)])
+        left, right = permuted(pay, "col", up), permuted(outs[4], "col", down)
+        coef = doubled(coef.reshape(1, nodes + tops, 32, 64), "col")
+        one = [coef[:, :nodes].reshape(cols * nodes, 32, 64)]
+        top = doubled(coef[:, nodes:].reshape(1, cols * tops, 32, 64), "row").reshape(-1, 32, 64)
     sel, sel_x, pick = constants()
     acc_shape = shape((2 * depth, 64, 512), F32)
+    first, second, third = split_layers(depth)
     acc, x, mask, yt = call(
-        functools.partial(own_kernel, depth),
+        functools.partial(own_kernel, depth, first),
         [
             acc_shape,
             shape((2 * depth, 96, 512), BF16),
@@ -609,31 +657,36 @@
         [charges, feat, near_list.T, sel, sel_x, pick],
         flops=1 << 32,
     )
-    corner = shape((80, depth * 128 + (256 if merge else 0)), BF16)
-    packed = call(
-        functools.partial(corner_kernel, merge, depth),
-        [corner] if merge else [corner, corner],
-        [even, odd] + ([coef] if merge else []),
-    )
-    if merge:
-        corner_left = corner_right = lax.ppermute(packed[0], "col", up + down)
-        at = depth * 128 + 128
-        top = jnp.stack([packed[0][48:80, at:], corner_left[48:80, at:]])
-        top = doubled(top, "row", 2)
-        one = [coef, corner_left]
+    for targets in (second, third):
+        acc = call(
+            functools.partial(more_own_kernel, depth, targets),
+            acc_shape,
+            [charges, x, mask, yt, acc],
+            alias=4,
+            flops=1 << 31,
+        )
+    corner = shape((80, corner_width), BF16)
+    packed = call(functools.partial(corner_kernel, merge, depth), [corner] if merge else [corner, corner], [even, odd])
+    if merge:
+        corner_left = corner_right = permuted(packed[0], "col", up + down)
+        got = call(tops_kernel, shape((rows // 2, 32, 128), BF16), [top])
+        got = permuted(got, "col", up + down)
     else:
-        corner_left = lax.ppermute(packed[0], "col", up)
-        corner_right = lax.ppermute(packed[1], "col", down)
-        coef = doubled(coef.reshape(1, nodes + tops, 32, 64), "col")
-        one = [coef[:, :nodes].reshape(cols * nodes, 32, 64)]
-        top = doubled(coef[:, nodes:].reshape(1, cols * tops, 32, 64), "row").reshape(-1, 32, 64)
-    acc = call(
-        functools.partial(side_kernel, merge, depth),
-        acc_shape,
+        corner_left = permuted(packed[0], "col", up)
+        corner_right = permuted(packed[1], "col", down)
+    acc, side_c, side_y = call(
+        functools.partial(side_kernel, merge, depth, range(0, depth // 2)),
+        [acc_shape, shape((2 * depth * SIDE, 64, 128), BF16), shape((2 * depth * SIDE, 64, 64), BF16)],
         [charges, right] + ([] if merge else [left]) + [sel, x, mask, yt, acc],
         alias=6 if merge else 7,
-        scratch=[pltpu.VMEM((2 * depth * SIDE, 64, 128), BF16), pltpu.VMEM((2 * depth * SIDE, 64, 64), BF16)],
         flops=1 << 32,
+    )
+    acc = call(
+        functools.partial(more_side_kernel, depth, range(depth // 2, depth)),
+        acc_shape,
+        [x, mask, side_c, side_y, acc],
+        alias=4,
+        flops=1 << 31,
     )
     acc, edge_c, edge_y = call(
         functools.partial(edge_kernel, depth),
@@ -661,7 +714,7 @@
     return call(
         functools.partial(down_kernel, depth, merge),
         shape((64, columns), BF16),
-        [acc, field, leaf_basis, t1, t2, couple_two, top, list_two],
+        [acc, field, leaf_basis, t1, t2, couple_two, top] + ([got] if merge else []) + [list_two],
         smem=1,
         scratch=[
             pltpu.VMEM((64, columns), BF16),

time: 38.9 us -> 37.9 us (0.974)
  starting transfers between devices: 15.6 us -> 13.6 us
  local copies, waits for them, and re-layouts: 1.96 us -> 2.9 us
  Pallas kernels: 14.7 us -> 14.1 us
  waiting for transfers between devices: 6.26 us -> 6.72 us
    ppermute x7 -> x9, starting transfers between devices: 15.6 us -> 13.6 us  [permuted(): return lax.ppermute(value, axis, pairs)]
    unnamed x29, local copies, waits for them, and re-layouts: 1.94 us -> 2.89 us
    pallas_call x9 -> x13, Pallas kernels: 14.7 us -> 14.1 us  [pallas(): pl.pallas_call(kernel, out_shape=out_shape, in_specs=[HBM] * hbm_in + [VM...]
    ppermute x7 -> x9, waiting for transfers between devices: 6.26 us -> 6.72 us  [permuted(): return lax.ppermute(value, axis, pairs)]
  transfers between devices with their start and end apart: 7 -> 9, of which waited for: 3 -> 3; matrix products, arithmetic and copies ran while one was open for 0% -> 0% of each run, Pallas kernels for 26% -> 27%
where the time goes in v4:
time: 37.9 us; the launch traced here: 37.7 us
  Pallas kernels  14.1 us (37%)
  starting transfers between devices  13.6 us (36%)
  waiting for transfers between devices  6.72 us (18%)
  local copies, waits for them, and re-layouts  2.9 us (8%)
    pallas_call x13, Pallas kernels, pallas(): pl.pallas_call(kernel, out_shape=out_shape, in_specs=[HBM] * hbm_in + [VM...  14.1 us
    ppermute x9, starting transfers between devices, permuted(): return lax.ppermute(value, axis, pairs)  13.6 us
    ppermute x9, waiting for transfers between devices, permuted(): return lax.ppermute(value, axis, pairs)  6.72 us
    unnamed x29, local copies, waits for them, and re-layouts  2.89 us
  transfers between devices with their start and end apart: 9, of which 3 were waited for; matrix products, arithmetic and copies ran while one was open for 0% of the time, Pallas kernels for 27%

profile of v4, /device:TPU:0, one launch (start us, length us, event | category | flops | bytes accessed | tf_op | source)
XLA Modules:
  0.0 37.7 jit_solution(7093661324017858103)
XLA Ops:
  0.0 1.8 %copy.20 = bf16[64,32,32]{2,1,0:T(8,128)(2,1)S(1)} copy(bf16[64,32,32]{0,2,1:T(8,128)(2,1)} %param.16) | data formatting | bytes 262144 | tf_op args[3]
  1.8 0.0 copy-start.5
  1.8 1.0 %copy-done.5 = bf16[64,4096]{1,0:T(8,128)(2,1)S(1)} copy-done((bf16[64,4096]{1,0:T(8,128)(2,1)S(1)}, bf16[64,4096]{1,0:T(8,128)(2,1)}, u32[]{:S(2)}) %copy-start.5) | copy-done | bytes 524312
  2.8 0.9 %shard_map.127 = (bf16[128,128]{1,0:T(8,128)(2,1)S(1)}, bf16[1,32,64]{2,1,0:T(8,128)(2,1)S(1)}) custom-call(bf16[64,4096]{1,0:T(8,128)(2,1)S(1)} %copy-done.5, bf16[32,4096]{1,0:T(8,128)(2,1)S(1)} %copy-done, bf16[2048,32]{1,0:T(8,128)(2,1)S(1)} %bitcast.3, bf16[256,32]{1,0:T(8,128)(2,1)S(1)} %bitcast.5), custom_call_target="tpu_custom_call" | custom-call | flops 2147483648 | bytes 1048576 | tf_op jit(solution)/shard_map/pallas_call | solution.py:583
  3.8 0.0 copy-start.9
  3.8 0.0 copy-start.11
  3.8 0.6 %shard_map.128 = (bf16[16,4096]{1,0:T(8,128)(2,1)S(1)}, bf16[80,1024]{1,0:T(8,128)(2,1)S(1)}, bf16[80,1024]{1,0:T(8,128)(2,1)S(1)}, bf16[80,1280]{1,0:T(8,128)(2,1)S(1)}) custom-call(bf16[64,4096]{1,0:T(8,128)(2,1)S(1)} %copy-done.5, f32[3,4096]{1,0:T(4,128)S(1)} %copy-done.6, bf16[128,128]{1,0:T(8,128)(2,1)S(1)} %get-tuple-element.21.refs_0_), custom_call_target="tpu_custom_call" | custom-call | flops 2147483648 | bytes 1048576 | tf_op jit(solution)/shard_map/pallas_call | solution.py:583
  4.5 0.0 copy-start.10
  4.5 0.6 %collective-permute-start = (bf16[80,1024]{1,0:T(8,128)(2,1)S(1)}, bf16[80,1024]{1,0:T(8,128)(2,1)S(1)}, u32[]{:S(2)}, u32[]{:S(2)}) collective-permute-start(bf16[80,1024]{1,0:T(8,128)(2,1)S(1)} %get-tuple-element.22), channel_id=1, source_target_pairs={{0,2},{2,0},{4,6},{6,4},{8,10},{10,8},{12,14},{14,12},{16,18},{18,... | collective-permute-start | bytes 491528 | tf_op jit(solution)/shard_map/ppermute | solution.py:564
  5.0 0.7 %collective-permute-start.1 = (bf16[80,1024]{1,0:T(8,128)(2,1)S(1)}, bf16[80,1024]{1,0:T(8,128)(2,1)S(1)}, u32[]{:S(2)}, u32[]{:S(2)}) collective-permute-start(bf16[80,1024]{1,0:T(8,128)(2,1)S(1)} %get-tuple-element.23), channel_id=1, source_target_pairs={{2,4},{4,2},{6,8},{8,6},{10,12},{12,10},{14,16},{16,14},{18,20},{2... | collective-permute-start | bytes 491528 | tf_op jit(solution)/shard_map/ppermute | solution.py:564
  5.7 2.6 %collective-permute-start.2 = (bf16[80,1280]{1,0:T(8,128)(2,1)S(1)}, bf16[80,1280]{1,0:T(8,128)(2,1)S(1)}, u32[]{:S(2)}, u32[]{:S(2)}) collective-permute-start(bf16[80,1280]{1,0:T(8,128)(2,1)S(1)} %get-tuple-element.27), channel_id=1, source_target_pairs={{0,1},{1,0},{2,3},{3,2},{4,5},{5,4},{6,7},{7,6},{8,9},{9,8},{10,11... | collective-permute-start | bytes 614408 | tf_op jit(solution)/shard_map/ppermute | solution.py:564
  8.3 5.3 %collective-permute-start.4 = (bf16[1,32,64]{2,1,0:T(8,128)(2,1)S(1)}, bf16[1,32,64]{2,1,0:T(8,128)(2,1)S(1)}, u32[]{:S(2)}, u32[]{:S(2)}) collective-permute-start(bf16[1,32,64]{2,1,0:T(8,128)(2,1)S(1)} %get-tuple-element.36), channel_id=1, source_target_pairs={{0,16},{2,18},{4,20},{6,22},{8,24},{10,26},{12,28},{14,30},{16,0},... | collective-permute-start | bytes 12296 | tf_op jit(solution)/shard_map/ppermute | solution.py:564
  13.6 1.5 %shard_map.129 = (f32[8,64,512]{2,1,0:T(8,128)S(1)}, bf16[8,96,512]{2,1,0:T(8,128)(2,1)S(1)}, f32[8,48,512]{2,1,0:T(8,128)S(1)}, bf16[32,128,32]{2,1,0:T(8,128)(2,1)S(1)}) custom-call(bf16[64,4096]{1,0:T(8,128)(2,1)S(1)} %copy-done.5, bf16[16,4096]{1,0:T(8,128)(2,1)S(1)} %get-tuple-element.24.feat_ref, s32[27,64]{1,0:T(8,128)S(1)} %bitcast.7, ...), custom_call_target="tpu_custom_call" | custom-call | flops 4294967296 | bytes 1048576 | tf_op jit(solution)/shard_map/pallas_call | solution.py:583
  15.1 1.0 %shard_map.130.in_ref = f32[8,64,512]{2,1,0:T(8,128)S(1)} custom-call(bf16[64,4096]{1,0:T(8,128)(2,1)S(1)} %copy-done.5, bf16[8,96,512]{2,1,0:T(8,128)(2,1)S(1)} %get-tuple-element.25.x_ref.refs_1_, f32[8,48,512]{2,1,0:T(8,128)S(1)} %get-tuple-element.26.mask_ref.refs_2_, ...), custom_call_target="tpu_custom_call", output_to_operand_aliasing={{}: (4, {})} | custom-call | flops 2147483648 | bytes 1048576 | tf_op jit(solution)/shard_map/pallas_call | solution.py:583
  16.1 1.6 %shard_map.131.refs_4_ = f32[8,64,512]{2,1,0:T(8,128)S(1)} custom-call(bf16[64,4096]{1,0:T(8,128)(2,1)S(1)} %copy-done.5, bf16[8,96,512]{2,1,0:T(8,128)(2,1)S(1)} %get-tuple-element.25.x_ref.refs_1_, f32[8,48,512]{2,1,0:T(8,128)S(1)} %get-tuple-element.26.mask_ref.refs_2_, ...), custom_call_target="tpu_custom_call", output_to_operand_aliasing={{}: (4, {})} | custom-call | flops 2147483648 | bytes 1048576 | tf_op jit(solution)/shard_map/pallas_call | solution.py:583
  17.7 1.6 %collective-permute-start.5 = (bf16[2,32,64]{2,1,0:T(8,128)(2,1)S(1)}, bf16[2,32,64]{2,1,0:T(8,128)(2,1)S(1)}, u32[]{:S(2)}, u32[]{:S(2)}) collective-permute-start(bf16[2,32,64]{2,1,0:T(8,128)(2,1)S(1)} %pad_maximum_fusion.2), channel_id=1, source_target_pairs={{0,8},{2,10},{4,12},{6,14},{8,0},{10,2},{12,4},{14,6},{16,24},{18,... | collective-permute-start | bytes 24584 | tf_op jit(solution)/shard_map/ppermute | solution.py:564
  19.4 2.2 %collective-permute-done.5 = bf16[2,32,64]{2,1,0:T(8,128)(2,1)S(1)} collective-permute-done((bf16[2,32,64]{2,1,0:T(8,128)(2,1)S(1)}, bf16[2,32,64]{2,1,0:T(8,128)(2,1)S(1)}, u32[]{:S(2)}, u32[]{:S(2)}) %collective-permute-start.5) | collective-permute-done | bytes 8224 | tf_op jit(solution)/shard_map/ppermute | solution.py:564
  21.5 0.7 %collective-permute-start.6 = (bf16[4,32,64]{2,1,0:T(8,128)(2,1)S(1)}, bf16[4,32,64]{2,1,0:T(8,128)(2,1)S(1)}, u32[]{:S(2)}, u32[]{:S(2)}) collective-permute-start(bf16[4,32,64]{2,1,0:T(8,128)(2,1)S(1)} %pad_maximum_fusion.1), channel_id=1, source_target_pairs={{0,4},{2,6},{4,0},{6,2},{8,12},{10,14},{12,8},{14,10},{16,20},{18,... | collective-permute-start | bytes 49160 | tf_op jit(solution)/shard_map/ppermute | solution.py:564
  22.2 3.3 %collective-permute-done.6 = bf16[4,32,64]{2,1,0:T(8,128)(2,1)S(1)} collective-permute-done((bf16[4,32,64]{2,1,0:T(8,128)(2,1)S(1)}, bf16[4,32,64]{2,1,0:T(8,128)(2,1)S(1)}, u32[]{:S(2)}, u32[]{:S(2)}) %collective-permute-start.6) | collective-permute-done | bytes 16416 | tf_op jit(solution)/shard_map/ppermute | solution.py:564
  25.5 0.1 collective-permute-start.7
  25.6 1.2 %collective-permute-done.7 = bf16[8,32,64]{2,1,0:T(8,128)(2,1)S(1)} collective-permute-done((bf16[8,32,64]{2,1,0:T(8,128)(2,1)S(1)}, bf16[8,32,64]{2,1,0:T(8,128)(2,1)S(1)}, u32[]{:S(2)}, u32[]{:S(2)}) %collective-permute-start.7) | collective-permute-done | bytes 32800 | tf_op jit(solution)/shard_map/ppermute | solution.py:564
  26.9 0.1 shard_map.138
  27.0 0.6 %collective-permute-start.8 = (bf16[8,32,128]{2,1,0:T(8,128)(2,1)S(1)}, bf16[8,32,128]{2,1,0:T(8,128)(2,1)S(1)}, u32[]{:S(2)}, u32[]{:S(2)}) collective-permute-start(bf16[8,32,128]{2,1,0:T(8,128)(2,1)S(1)} %shard_map.138), channel_id=1, source_target_pairs={{0,1},{1,0},{2,3},{3,2},{4,5},{5,4},{6,7},{7,6},{8,9},{9,8},{10,11... | collective-permute-start | bytes 196616 | tf_op jit(solution)/shard_map/ppermute | solution.py:564
  27.6 0.2 shard_map.135
  27.8 1.6 %collective-permute-start.3 = (bf16[80,512]{1,0:T(8,128)(2,1)S(1)}, bf16[80,512]{1,0:T(8,128)(2,1)S(1)}, u32[]{:S(2)}, u32[]{:S(2)}) collective-permute-start(bf16[80,512]{1,0:T(8,128)(2,1)S(1)} %shard_map.135), channel_id=1, source_target_pairs={{0,1},{1,0},{2,3},{3,2},{4,5},{5,4},{6,7},{7,6},{8,9},{9,8},{10,11... | collective-permute-start | bytes 245768 | tf_op jit(solution)/shard_map/ppermute | solution.py:564
  29.4 1.5 %shard_map.132 = (f32[8,64,512]{2,1,0:T(8,128)S(1)}, bf16[32,64,128]{2,1,0:T(8,128)(2,1)S(1)}, bf16[32,64,64]{2,1,0:T(8,128)(2,1)S(1)}) custom-call(bf16[64,4096]{1,0:T(8,128)(2,1)S(1)} %copy-done.5, bf16[80,1280]{1,0:T(8,128)(2,1)S(1)} %collective-permute-done.2.right_ref.refs_1_, bf16[16,160]{1,0:T(8,128)(2,1)S(1)} %copy-done.10, ...), custom_call_target="tpu_custom_call", output_to_operand_aliasing={{0}: (6, {})} | custom-call | flops 4294967296 | bytes 1048576 | tf_op jit(solution)/shard_map/pallas_call | solution.py:583
  30.9 1.1 %shard_map.133.in_ref = f32[8,64,512]{2,1,0:T(8,128)S(1)} custom-call(bf16[8,96,512]{2,1,0:T(8,128)(2,1)S(1)} %get-tuple-element.25.x_ref.refs_1_, f32[8,48,512]{2,1,0:T(8,128)S(1)} %get-tuple-element.26.mask_ref.refs_2_, bf16[32,64,128]{2,1,0:T(8,128)(2,1)S(1)} %get-tuple-element.30.c_ref, ...), custom_call_target="tpu_custom_call", output_to_operand_aliasing={{}: (4, {})} | custom-call | flops 2147483648 | bytes 1048576 | tf_op jit(solution)/shard_map/pallas_call | solution.py:583
  32.1 1.1 %shard_map.134 = (f32[8,64,512]{2,1,0:T(8,128)S(1)}, bf16[16,64,128]{2,1,0:T(8,128)(2,1)S(1)}, bf16[16,128,32]{2,1,0:T(8,128)(2,1)S(1)}) custom-call(bf16[80,1024]{1,0:T(8,128)(2,1)S(1)} %collective-permute-done.even_ref, bf16[80,1024]{1,0:T(8,128)(2,1)S(1)} %collective-permute-done.1.odd_ref, ...), custom_call_target="tpu_custom_call", output_to_operand_aliasing={{0}: (5, {})} | custom-call | flops 2147483648 | bytes 1048576 | tf_op jit(solution)/shard_map/pallas_call | solution.py:583
  33.2 1.0 %shard_map.137.f1_ref = f32[256,64]{1,0:T(8,128)S(1)} custom-call(bf16[8,12,32,32]{3,2,1,0:T(8,128)(2,1)S(1)} %copy-done.4, bf16[128,128]{1,0:T(8,128)(2,1)S(1)} %get-tuple-element.21.refs_0_, bf16[80,1280]{1,0:T(8,128)(2,1)S(1)} %collective-permute-done.2.right_ref.refs_1_, s32[8,12]{1,0:T(8,128)S(1)} %copy-done.8), custom_call_target="tpu_custom_call" | custom-call | flops 1073741824 | bytes 1048576 | tf_op jit(solution)/shard_map/pallas_call | solution.py:583
  34.2 0.0 collective-permute-done.3.right_ref
  34.2 1.1 %shard_map.136.acc_ref = f32[8,64,512]{2,1,0:T(8,128)S(1)} custom-call(bf16[16,64,128]{2,1,0:T(8,128)(2,1)S(1)} %get-tuple-element.33.edge_c_ref, bf16[16,128,32]{2,1,0:T(8,128)(2,1)S(1)} %get-tuple-element.34.edge_y_ref, bf16[80,512]{1,0:T(8,128)(2,1)S(1)} %collective-permute-done.3.right_ref, ...), custom_call_target="tpu_custom_call", output_to_operand_aliasing={{}: (6, {})} | custom-call | flops 2147483648 | bytes 1048576 | tf_op jit(solution)/shard_map/pallas_call | solution.py:583
  35.4 2.4 %shard_map.139 = bf16[64,4096]{1,0:T(8,128)(2,1)} custom-call(f32[8,64,512]{2,1,0:T(8,128)S(1)} %shard_map.136.acc_ref, f32[256,64]{1,0:T(8,128)S(1)} %shard_map.137.f1_ref, bf16[32,4096]{1,0:T(8,128)(2,1)S(1)} %copy-done, bf16[2048,32]{1,0:T(8,128)(2,1)S(1)} %bitcast.4, bf16[256,32]{1,0:T(8,128)(2,1)S(1)} %bitcast.6, bf16[1,16,32,32]{3,2,1,0:T(8,128)(2,1)S(1)} %copy-done.1, ...), custom_call_target="tpu_custom_call" | custom-call | tf_op jit(solution)/shard_map/pallas_call | solution.py:583
  (32 shorter events, 0.1 us)
Async XLA Ops:
  0.0 1.8 %copy-start = (bf16[32,4096]{1,0:T(8,128)(2,1)S(1)}, bf16[32,4096]{1,0:T(8,128)(2,1)}, u32[]{:S(2)}) copy-start(bf16[32,4096]{1,0:T(8,128)(2,1)} %basis_ref.3) | copy-start | bytes 786436
  0.0 1.8 %copy-start.2 = (bf16[8,32,32]{2,1,0:T(8,128)(2,1)S(1)}, bf16[8,32,32]{2,1,0:T(8,128)(2,1)}, u32[]{:S(2)}) copy-start(bf16[8,32,32]{2,1,0:T(8,128)(2,1)} %param.17) | copy-start | bytes 49156
  1.8 1.0 %copy-start.5 = (bf16[64,4096]{1,0:T(8,128)(2,1)S(1)}, bf16[64,4096]{1,0:T(8,128)(2,1)}, u32[]{:S(2)}) copy-start(bf16[64,4096]{1,0:T(8,128)(2,1)} %q_ref.11) | copy-start | bytes 1572868
  2.8 0.9 %copy-start.6 = (f32[3,4096]{1,0:T(4,128)S(1)}, f32[3,4096]{1,0:T(4,128)}, u32[]{:S(2)}) copy-start(f32[3,4096]{1,0:T(4,128)} %pts_ref.1) | copy-start | bytes 147460
  3.8 9.8 %copy-start.7 = (s32[64,27]{0,1:T(8,128)S(1)}, s32[64,27]{0,1:T(8,128)}, u32[]{:S(2)}) copy-start(s32[64,27]{0,1:T(8,128)} %param.20) | copy-start | bytes 20740
  3.8 9.8 %copy-start.9 = (bf16[96,27]{1,0:T(8,128)(2,1)S(1)}, bf16[96,27]{1,0:T(8,128)(2,1)}, u32[]{:S(2)}) copy-start(bf16[96,27]{1,0:T(8,128)(2,1)} %constant.8.clone.pick_ref) | copy-start | bytes 15556
  3.8 9.8 %copy-start.11 = (bf16[32,16]{1,0:T(8,128)(2,1)S(1)}, bf16[32,16]{1,0:T(8,128)(2,1)}, u32[]{:S(2)}) copy-start(bf16[32,16]{1,0:T(8,128)(2,1)} %constant.7.clone.sel_x_ref) | copy-start | bytes 3076
  4.5 9.1 %copy-start.10 = (bf16[16,160]{1,0:T(8,128)(2,1)S(1)}, bf16[16,160]{1,0:T(8,128)(2,1)}, u32[]{:S(2)}) copy-start(bf16[16,160]{1,0:T(8,128)(2,1)} %constant.6.clone.sel_ref.refs_0_) | copy-start | bytes 15364
  4.5 23.1 %collective-permute-start = (bf16[80,1024]{1,0:T(8,128)(2,1)S(1)}, bf16[80,1024]{1,0:T(8,128)(2,1)S(1)}, u32[]{:S(2)}, u32[]{:S(2)}) collective-permute-start(bf16[80,1024]{1,0:T(8,128)(2,1)S(1)} %get-tuple-element.22), channel_id=1, source_target_pairs={{0,2},{2,0},{4,6},{6,4},{8,10},{10,8},{12,14},{14,12},{16,18},{18,... | collective-permute-start | bytes 491528 | tf_op jit(solution)/shard_map/ppermute | solution.py:564
  5.0 22.5 %collective-permute-start.1 = (bf16[80,1024]{1,0:T(8,128)(2,1)S(1)}, bf16[80,1024]{1,0:T(8,128)(2,1)S(1)}, u32[]{:S(2)}, u32[]{:S(2)}) collective-permute-start(bf16[80,1024]{1,0:T(8,128)(2,1)S(1)} %get-tuple-element.23), channel_id=1, source_target_pairs={{2,4},{4,2},{6,8},{8,6},{10,12},{12,10},{14,16},{16,14},{18,20},{2... | collective-permute-start | bytes 491528 | tf_op jit(solution)/shard_map/ppermute | solution.py:564
  5.7 23.7 %collective-permute-start.2 = (bf16[80,1280]{1,0:T(8,128)(2,1)S(1)}, bf16[80,1280]{1,0:T(8,128)(2,1)S(1)}, u32[]{:S(2)}, u32[]{:S(2)}) collective-permute-start(bf16[80,1280]{1,0:T(8,128)(2,1)S(1)} %get-tuple-element.27), channel_id=1, source_target_pairs={{0,1},{1,0},{2,3},{3,2},{4,5},{5,4},{6,7},{7,6},{8,9},{9,8},{10,11... | collective-permute-start | bytes 614408 | tf_op jit(solution)/shard_map/ppermute | solution.py:564
  8.3 9.4 %collective-permute-start.4 = (bf16[1,32,64]{2,1,0:T(8,128)(2,1)S(1)}, bf16[1,32,64]{2,1,0:T(8,128)(2,1)S(1)}, u32[]{:S(2)}, u32[]{:S(2)}) collective-permute-start(bf16[1,32,64]{2,1,0:T(8,128)(2,1)S(1)} %get-tuple-element.36), channel_id=1, source_target_pairs={{0,16},{2,18},{4,20},{6,22},{8,24},{10,26},{12,28},{14,30},{16,0},... | collective-permute-start | bytes 12296 | tf_op jit(solution)/shard_map/ppermute | solution.py:564
  17.7 3.8 %collective-permute-start.5 = (bf16[2,32,64]{2,1,0:T(8,128)(2,1)S(1)}, bf16[2,32,64]{2,1,0:T(8,128)(2,1)S(1)}, u32[]{:S(2)}, u32[]{:S(2)}) collective-permute-start(bf16[2,32,64]{2,1,0:T(8,128)(2,1)S(1)} %pad_maximum_fusion.2), channel_id=1, source_target_pairs={{0,8},{2,10},{4,12},{6,14},{8,0},{10,2},{12,4},{14,6},{16,24},{18,... | collective-permute-start | bytes 24584 | tf_op jit(solution)/shard_map/ppermute | solution.py:564
  21.5 4.0 %collective-permute-start.6 = (bf16[4,32,64]{2,1,0:T(8,128)(2,1)S(1)}, bf16[4,32,64]{2,1,0:T(8,128)(2,1)S(1)}, u32[]{:S(2)}, u32[]{:S(2)}) collective-permute-start(bf16[4,32,64]{2,1,0:T(8,128)(2,1)S(1)} %pad_maximum_fusion.1), channel_id=1, source_target_pairs={{0,4},{2,6},{4,0},{6,2},{8,12},{10,14},{12,8},{14,10},{16,20},{18,... | collective-permute-start | bytes 49160 | tf_op jit(solution)/shard_map/ppermute | solution.py:564
  25.5 1.3 %collective-permute-start.7 = (bf16[8,32,64]{2,1,0:T(8,128)(2,1)S(1)}, bf16[8,32,64]{2,1,0:T(8,128)(2,1)S(1)}, u32[]{:S(2)}, u32[]{:S(2)}) collective-permute-start(bf16[8,32,64]{2,1,0:T(8,128)(2,1)S(1)} %pad_maximum_fusion), channel_id=1, source_target_pairs={{0,2},{2,0},{4,6},{6,4},{8,10},{10,8},{12,14},{14,12},{16,18},{18,... | collective-permute-start | bytes 98312 | tf_op jit(solution)/shard_map/ppermute | solution.py:564
  27.0 8.4 %collective-permute-start.8 = (bf16[8,32,128]{2,1,0:T(8,128)(2,1)S(1)}, bf16[8,32,128]{2,1,0:T(8,128)(2,1)S(1)}, u32[]{:S(2)}, u32[]{:S(2)}) collective-permute-start(bf16[8,32,128]{2,1,0:T(8,128)(2,1)S(1)} %shard_map.138), channel_id=1, source_target_pairs={{0,1},{1,0},{2,3},{3,2},{4,5},{5,4},{6,7},{7,6},{8,9},{9,8},{10,11... | collective-permute-start | bytes 196616 | tf_op jit(solution)/shard_map/ppermute | solution.py:564
  27.8 6.4 %collective-permute-start.3 = (bf16[80,512]{1,0:T(8,128)(2,1)S(1)}, bf16[80,512]{1,0:T(8,128)(2,1)S(1)}, u32[]{:S(2)}, u32[]{:S(2)}) collective-permute-start(bf16[80,512]{1,0:T(8,128)(2,1)S(1)} %shard_map.135), channel_id=1, source_target_pairs={{0,1},{1,0},{2,3},{3,2},{4,5},{5,4},{6,7},{7,6},{8,9},{9,8},{10,11... | collective-permute-start | bytes 245768 | tf_op jit(solution)/shard_map/ppermute | solution.py:564
  32.0 1.1 %copy-start.4 = (bf16[8,12,32,32]{3,2,1,0:T(8,128)(2,1)S(1)}, bf16[8,12,32,32]{3,2,1,0:T(8,128)(2,1)}, u32[]{:S(2)}) copy-start(bf16[8,12,32,32]{3,2,1,0:T(8,128)(2,1)} %k1_ref.1) | copy-start | bytes 589828
  32.0 1.1 %copy-start.8 = (s32[8,12]{1,0:T(8,128)S(1)}, s32[8,12]{1,0:T(8,128)}, u32[]{:S(2)}) copy-start(s32[8,12]{1,0:T(8,128)} %refs_2_.1) | copy-start | bytes 1156
  34.2 1.1 %copy-start.1 = (bf16[1,16,32,32]{3,2,1,0:T(8,128)(2,1)S(1)}, bf16[1,16,32,32]{3,2,1,0:T(8,128)(2,1)}, u32[]{:S(2)}) copy-start(bf16[1,16,32,32]{3,2,1,0:T(8,128)(2,1)} %k2_ref.1) | copy-start | bytes 98308
  34.2 1.1 %copy-start.3 = (s32[1,16]{1,0:T(1,128)S(1)}, s32[1,16]{1,0:T(1,128)}, u32[]{:S(2)}) copy-start(s32[1,16]{1,0:T(1,128)} %refs_1_.1) | copy-start | bytes 196

commit v5 on v4

--- a/solution.py
+++ b/solution.py
@@ -175,17 +175,19 @@
     send_rows(even_ref, row % 2 == 0, q_ref, feat, depth)
 
 
-def up_kernel(merge, q_ref, basis_ref, t1_ref, t2_ref, *refs):
+def leaf_kernel(q_ref, basis_ref, out_ref):
+    for n in range(out_ref.shape[0]):
+        chunk = slice(512 * n, 512 * n + 512)
+        out_ref[n] = dot(block_basis(basis_ref[:, chunk]), q_ref[:, chunk], NT).astype(BF16)
+
+
+def up_kernel(merge, leaf_ref, t1_ref, t2_ref, *refs):
     if merge:
         coef_ref, top_ref = refs
     else:
         coef_ref = refs[0]
-    nodes = q_ref.shape[1] // 512
-    leaf = []
-    for n in range(nodes):
-        chunk = slice(512 * n, 512 * n + 512)
-        leaf.append(dot(block_basis(basis_ref[:, chunk]), q_ref[:, chunk], NT).astype(BF16))
-    ones = [dot(t1_ref[256 * n : 256 * n + 256, :], leaf[n], TN).astype(BF16) for n in range(nodes)]
+    nodes = leaf_ref.shape[0]
+    ones = [dot(t1_ref[256 * n : 256 * n + 256, :], leaf_ref[n], TN).astype(BF16) for n in range(nodes)]
     tops = []
     for m in range(nodes // 8):
         part = jnp.concatenate(ones[8 * m : 8 * m + 8], axis=0)
@@ -610,12 +612,13 @@
     up = [(i, i + 1) for i in range(cols - 1)]
     down = [(j, i) for i, j in up]
     corner_width = depth * 128
+    leaf = call(leaf_kernel, shape((nodes, 256, 64), BF16), [charges, leaf_basis], flops=1 << 31)
     ups = call(
         functools.partial(up_kernel, merge),
         [shape((16 * nodes, 128), BF16), shape((1, 32, 64), BF16)]
         if merge
         else [shape(((nodes + tops) * 32, 64), BF16)],
-        [charges, leaf_basis, t1, t2],
+        [leaf, t1, t2],
         flops=1 << 31,
     )
     coef = ups[0]

time: 37.9 us -> 37.6 us (level)
  local copies, waits for them, and re-layouts: 2.9 us -> 2.45 us
    unnamed x29, local copies, waits for them, and re-layouts: 2.89 us -> 2.44 us
    pallas_call x13 -> x14, Pallas kernels: 14.1 us -> 14.2 us  [pallas(): pl.pallas_call(kernel, out_shape=out_shape, in_specs=[HBM] * hbm_in + [VM...]
where the time goes in v5:
time: 37.6 us; the launch traced here: 37.3 us
  Pallas kernels  14.2 us (38%)
  starting transfers between devices  13.6 us (36%)
  waiting for transfers between devices  6.7 us (18%)
  local copies, waits for them, and re-layouts  2.45 us (7%)
    pallas_call x14, Pallas kernels, pallas(): pl.pallas_call(kernel, out_shape=out_shape, in_specs=[HBM] * hbm_in + [VM...  14.2 us
    ppermute x9, starting transfers between devices, permuted(): return lax.ppermute(value, axis, pairs)  13.6 us
    ppermute x9, waiting for transfers between devices, permuted(): return lax.ppermute(value, axis, pairs)  6.7 us
    unnamed x29, local copies, waits for them, and re-layouts  2.44 us
  transfers between devices with their start and end apart: 9, of which 3 were waited for; matrix products, arithmetic and copies ran while one was open for 0% of the time, Pallas kernels for 27%

profile of v5, /device:TPU:0, one launch (start us, length us, event | category | flops | bytes accessed | tf_op | source)
XLA Modules:
  0.0 37.3 jit_solution(3133637993677231361)
XLA Ops:
  0.0 1.8 %copy.20 = bf16[64,32,32]{2,1,0:T(8,128)(2,1)S(1)} copy(bf16[64,32,32]{0,2,1:T(8,128)(2,1)} %param.16) | data formatting | bytes 262144 | tf_op args[3]
  1.8 0.0 copy-start.2
  1.8 0.7 %shard_map.127.leaf_ref = bf16[8,256,64]{2,1,0:T(8,128)(2,1)S(1)} custom-call(bf16[64,4096]{1,0:T(8,128)(2,1)S(1)} %copy-done.5, bf16[32,4096]{1,0:T(8,128)(2,1)S(1)} %copy-done), custom_call_target="tpu_custom_call" | custom-call | flops 2147483648 | bytes 1048576 | tf_op jit(solution)/shard_map/pallas_call | solution.py:585
  2.5 0.1 copy-done.2
  2.7 0.4 %shard_map.128 = (bf16[128,128]{1,0:T(8,128)(2,1)S(1)}, bf16[1,32,64]{2,1,0:T(8,128)(2,1)S(1)}) custom-call(bf16[8,256,64]{2,1,0:T(8,128)(2,1)S(1)} %shard_map.127.leaf_ref, bf16[2048,32]{1,0:T(8,128)(2,1)S(1)} %bitcast.3, bf16[256,32]{1,0:T(8,128)(2,1)S(1)} %bitcast.5), custom_call_target="tpu_custom_call" | custom-call | flops 2147483648 | bytes 1048576 | tf_op jit(solution)/shard_map/pallas_call | solution.py:585
  3.1 0.4 %copy-done.6 = f32[3,4096]{1,0:T(4,128)S(1)} copy-done((f32[3,4096]{1,0:T(4,128)S(1)}, f32[3,4096]{1,0:T(4,128)}, u32[]{:S(2)}) %copy-start.6) | copy-done | bytes 49176
  3.5 0.6 %shard_map.129 = (bf16[16,4096]{1,0:T(8,128)(2,1)S(1)}, bf16[80,1024]{1,0:T(8,128)(2,1)S(1)}, bf16[80,1024]{1,0:T(8,128)(2,1)S(1)}, bf16[80,1280]{1,0:T(8,128)(2,1)S(1)}) custom-call(bf16[64,4096]{1,0:T(8,128)(2,1)S(1)} %copy-done.5, f32[3,4096]{1,0:T(4,128)S(1)} %copy-done.6, bf16[128,128]{1,0:T(8,128)(2,1)S(1)} %get-tuple-element.21.refs_0_), custom_call_target="tpu_custom_call" | custom-call | flops 2147483648 | bytes 1048576 | tf_op jit(solution)/shard_map/pallas_call | solution.py:585
  4.2 0.0 copy-start.10
  4.2 0.6 %collective-permute-start = (bf16[80,1024]{1,0:T(8,128)(2,1)S(1)}, bf16[80,1024]{1,0:T(8,128)(2,1)S(1)}, u32[]{:S(2)}, u32[]{:S(2)}) collective-permute-start(bf16[80,1024]{1,0:T(8,128)(2,1)S(1)} %get-tuple-element.22), channel_id=1, source_target_pairs={{0,2},{2,0},{4,6},{6,4},{8,10},{10,8},{12,14},{14,12},{16,18},{18,... | collective-permute-start | bytes 491528 | tf_op jit(solution)/shard_map/ppermute | solution.py:566
  4.7 0.7 %collective-permute-start.1 = (bf16[80,1024]{1,0:T(8,128)(2,1)S(1)}, bf16[80,1024]{1,0:T(8,128)(2,1)S(1)}, u32[]{:S(2)}, u32[]{:S(2)}) collective-permute-start(bf16[80,1024]{1,0:T(8,128)(2,1)S(1)} %get-tuple-element.23), channel_id=1, source_target_pairs={{2,4},{4,2},{6,8},{8,6},{10,12},{12,10},{14,16},{16,14},{18,20},{2... | collective-permute-start | bytes 491528 | tf_op jit(solution)/shard_map/ppermute | solution.py:566
  5.4 2.6 %collective-permute-start.2 = (bf16[80,1280]{1,0:T(8,128)(2,1)S(1)}, bf16[80,1280]{1,0:T(8,128)(2,1)S(1)}, u32[]{:S(2)}, u32[]{:S(2)}) collective-permute-start(bf16[80,1280]{1,0:T(8,128)(2,1)S(1)} %get-tuple-element.27), channel_id=1, source_target_pairs={{0,1},{1,0},{2,3},{3,2},{4,5},{5,4},{6,7},{7,6},{8,9},{9,8},{10,11... | collective-permute-start | bytes 614408 | tf_op jit(solution)/shard_map/ppermute | solution.py:566
  8.0 5.3 %collective-permute-start.4 = (bf16[1,32,64]{2,1,0:T(8,128)(2,1)S(1)}, bf16[1,32,64]{2,1,0:T(8,128)(2,1)S(1)}, u32[]{:S(2)}, u32[]{:S(2)}) collective-permute-start(bf16[1,32,64]{2,1,0:T(8,128)(2,1)S(1)} %get-tuple-element.36), channel_id=1, source_target_pairs={{0,16},{2,18},{4,20},{6,22},{8,24},{10,26},{12,28},{14,30},{16,0},... | collective-permute-start | bytes 12296 | tf_op jit(solution)/shard_map/ppermute | solution.py:566
  13.3 1.5 %shard_map.130 = (f32[8,64,512]{2,1,0:T(8,128)S(1)}, bf16[8,96,512]{2,1,0:T(8,128)(2,1)S(1)}, f32[8,48,512]{2,1,0:T(8,128)S(1)}, bf16[32,128,32]{2,1,0:T(8,128)(2,1)S(1)}) custom-call(bf16[64,4096]{1,0:T(8,128)(2,1)S(1)} %copy-done.5, bf16[16,4096]{1,0:T(8,128)(2,1)S(1)} %get-tuple-element.24.feat_ref, s32[27,64]{1,0:T(8,128)S(1)} %bitcast.7, ...), custom_call_target="tpu_custom_call" | custom-call | flops 4294967296 | bytes 1048576 | tf_op jit(solution)/shard_map/pallas_call | solution.py:585
  14.8 1.0 %shard_map.131.in_ref = f32[8,64,512]{2,1,0:T(8,128)S(1)} custom-call(bf16[64,4096]{1,0:T(8,128)(2,1)S(1)} %copy-done.5, bf16[8,96,512]{2,1,0:T(8,128)(2,1)S(1)} %get-tuple-element.25.x_ref.refs_1_, f32[8,48,512]{2,1,0:T(8,128)S(1)} %get-tuple-element.26.mask_ref.refs_2_, ...), custom_call_target="tpu_custom_call", output_to_operand_aliasing={{}: (4, {})} | custom-call | flops 2147483648 | bytes 1048576 | tf_op jit(solution)/shard_map/pallas_call | solution.py:585
  15.8 1.5 %shard_map.132.refs_4_ = f32[8,64,512]{2,1,0:T(8,128)S(1)} custom-call(bf16[64,4096]{1,0:T(8,128)(2,1)S(1)} %copy-done.5, bf16[8,96,512]{2,1,0:T(8,128)(2,1)S(1)} %get-tuple-element.25.x_ref.refs_1_, f32[8,48,512]{2,1,0:T(8,128)S(1)} %get-tuple-element.26.mask_ref.refs_2_, ...), custom_call_target="tpu_custom_call", output_to_operand_aliasing={{}: (4, {})} | custom-call | flops 2147483648 | bytes 1048576 | tf_op jit(solution)/shard_map/pallas_call | solution.py:585
  17.3 1.6 %collective-permute-start.5 = (bf16[2,32,64]{2,1,0:T(8,128)(2,1)S(1)}, bf16[2,32,64]{2,1,0:T(8,128)(2,1)S(1)}, u32[]{:S(2)}, u32[]{:S(2)}) collective-permute-start(bf16[2,32,64]{2,1,0:T(8,128)(2,1)S(1)} %pad_maximum_fusion.2), channel_id=1, source_target_pairs={{0,8},{2,10},{4,12},{6,14},{8,0},{10,2},{12,4},{14,6},{16,24},{18,... | collective-permute-start | bytes 24584 | tf_op jit(solution)/shard_map/ppermute | solution.py:566
  19.0 2.2 %collective-permute-done.5 = bf16[2,32,64]{2,1,0:T(8,128)(2,1)S(1)} collective-permute-done((bf16[2,32,64]{2,1,0:T(8,128)(2,1)S(1)}, bf16[2,32,64]{2,1,0:T(8,128)(2,1)S(1)}, u32[]{:S(2)}, u32[]{:S(2)}) %collective-permute-start.5) | collective-permute-done | bytes 8224 | tf_op jit(solution)/shard_map/ppermute | solution.py:566
  21.2 0.7 %collective-permute-start.6 = (bf16[4,32,64]{2,1,0:T(8,128)(2,1)S(1)}, bf16[4,32,64]{2,1,0:T(8,128)(2,1)S(1)}, u32[]{:S(2)}, u32[]{:S(2)}) collective-permute-start(bf16[4,32,64]{2,1,0:T(8,128)(2,1)S(1)} %pad_maximum_fusion.1), channel_id=1, source_target_pairs={{0,4},{2,6},{4,0},{6,2},{8,12},{10,14},{12,8},{14,10},{16,20},{18,... | collective-permute-start | bytes 49160 | tf_op jit(solution)/shard_map/ppermute | solution.py:566
  21.8 3.3 %collective-permute-done.6 = bf16[4,32,64]{2,1,0:T(8,128)(2,1)S(1)} collective-permute-done((bf16[4,32,64]{2,1,0:T(8,128)(2,1)S(1)}, bf16[4,32,64]{2,1,0:T(8,128)(2,1)S(1)}, u32[]{:S(2)}, u32[]{:S(2)}) %collective-permute-start.6) | collective-permute-done | bytes 16416 | tf_op jit(solution)/shard_map/ppermute | solution.py:566
  25.2 0.1 collective-permute-start.7
  25.3 1.2 %collective-permute-done.7 = bf16[8,32,64]{2,1,0:T(8,128)(2,1)S(1)} collective-permute-done((bf16[8,32,64]{2,1,0:T(8,128)(2,1)S(1)}, bf16[8,32,64]{2,1,0:T(8,128)(2,1)S(1)}, u32[]{:S(2)}, u32[]{:S(2)}) %collective-permute-start.7) | collective-permute-done | bytes 32800 | tf_op jit(solution)/shard_map/ppermute | solution.py:566
  26.5 0.1 shard_map.139
  26.6 0.6 %collective-permute-start.8 = (bf16[8,32,128]{2,1,0:T(8,128)(2,1)S(1)}, bf16[8,32,128]{2,1,0:T(8,128)(2,1)S(1)}, u32[]{:S(2)}, u32[]{:S(2)}) collective-permute-start(bf16[8,32,128]{2,1,0:T(8,128)(2,1)S(1)} %shard_map.139), channel_id=1, source_target_pairs={{0,1},{1,0},{2,3},{3,2},{4,5},{5,4},{6,7},{7,6},{8,9},{9,8},{10,11... | collective-permute-start | bytes 196616 | tf_op jit(solution)/shard_map/ppermute | solution.py:566
  27.2 0.2 shard_map.136
  27.4 1.6 %collective-permute-start.3 = (bf16[80,512]{1,0:T(8,128)(2,1)S(1)}, bf16[80,512]{1,0:T(8,128)(2,1)S(1)}, u32[]{:S(2)}, u32[]{:S(2)}) collective-permute-start(bf16[80,512]{1,0:T(8,128)(2,1)S(1)} %shard_map.136), channel_id=1, source_target_pairs={{0,1},{1,0},{2,3},{3,2},{4,5},{5,4},{6,7},{7,6},{8,9},{9,8},{10,11... | collective-permute-start | bytes 245768 | tf_op jit(solution)/shard_map/ppermute | solution.py:566
  29.0 1.5 %shard_map.133 = (f32[8,64,512]{2,1,0:T(8,128)S(1)}, bf16[32,64,128]{2,1,0:T(8,128)(2,1)S(1)}, bf16[32,64,64]{2,1,0:T(8,128)(2,1)S(1)}) custom-call(bf16[64,4096]{1,0:T(8,128)(2,1)S(1)} %copy-done.5, bf16[80,1280]{1,0:T(8,128)(2,1)S(1)} %collective-permute-done.2.right_ref.refs_1_, bf16[16,160]{1,0:T(8,128)(2,1)S(1)} %copy-done.10, ...), custom_call_target="tpu_custom_call", output_to_operand_aliasing={{0}: (6, {})} | custom-call | flops 4294967296 | bytes 1048576 | tf_op jit(solution)/shard_map/pallas_call | solution.py:585
  30.5 1.1 %shard_map.134.in_ref = f32[8,64,512]{2,1,0:T(8,128)S(1)} custom-call(bf16[8,96,512]{2,1,0:T(8,128)(2,1)S(1)} %get-tuple-element.25.x_ref.refs_1_, f32[8,48,512]{2,1,0:T(8,128)S(1)} %get-tuple-element.26.mask_ref.refs_2_, bf16[32,64,128]{2,1,0:T(8,128)(2,1)S(1)} %get-tuple-element.30.c_ref, ...), custom_call_target="tpu_custom_call", output_to_operand_aliasing={{}: (4, {})} | custom-call | flops 2147483648 | bytes 1048576 | tf_op jit(solution)/shard_map/pallas_call | solution.py:585
  31.6 1.1 %shard_map.135 = (f32[8,64,512]{2,1,0:T(8,128)S(1)}, bf16[16,64,128]{2,1,0:T(8,128)(2,1)S(1)}, bf16[16,128,32]{2,1,0:T(8,128)(2,1)S(1)}) custom-call(bf16[80,1024]{1,0:T(8,128)(2,1)S(1)} %collective-permute-done.even_ref, bf16[80,1024]{1,0:T(8,128)(2,1)S(1)} %collective-permute-done.1.odd_ref, ...), custom_call_target="tpu_custom_call", output_to_operand_aliasing={{0}: (5, {})} | custom-call | flops 2147483648 | bytes 1048576 | tf_op jit(solution)/shard_map/pallas_call | solution.py:585
  32.8 1.0 %shard_map.138.f1_ref = f32[256,64]{1,0:T(8,128)S(1)} custom-call(bf16[8,12,32,32]{3,2,1,0:T(8,128)(2,1)S(1)} %copy-done.4, bf16[128,128]{1,0:T(8,128)(2,1)S(1)} %get-tuple-element.21.refs_0_, bf16[80,1280]{1,0:T(8,128)(2,1)S(1)} %collective-permute-done.2.right_ref.refs_1_, s32[8,12]{1,0:T(8,128)S(1)} %copy-done.8), custom_call_target="tpu_custom_call" | custom-call | flops 1073741824 | bytes 1048576 | tf_op jit(solution)/shard_map/pallas_call | solution.py:585
  33.8 0.0 collective-permute-done.3.right_ref
  33.8 1.1 %shard_map.137.acc_ref = f32[8,64,512]{2,1,0:T(8,128)S(1)} custom-call(bf16[16,64,128]{2,1,0:T(8,128)(2,1)S(1)} %get-tuple-element.33.edge_c_ref, bf16[16,128,32]{2,1,0:T(8,128)(2,1)S(1)} %get-tuple-element.34.edge_y_ref, bf16[80,512]{1,0:T(8,128)(2,1)S(1)} %collective-permute-done.3.right_ref, ...), custom_call_target="tpu_custom_call", output_to_operand_aliasing={{}: (6, {})} | custom-call | flops 2147483648 | bytes 1048576 | tf_op jit(solution)/shard_map/pallas_call | solution.py:585
  34.9 2.4 %shard_map.140 = bf16[64,4096]{1,0:T(8,128)(2,1)} custom-call(f32[8,64,512]{2,1,0:T(8,128)S(1)} %shard_map.137.acc_ref, f32[256,64]{1,0:T(8,128)S(1)} %shard_map.138.f1_ref, bf16[32,4096]{1,0:T(8,128)(2,1)S(1)} %copy-done, bf16[2048,32]{1,0:T(8,128)(2,1)S(1)} %bitcast.4, bf16[256,32]{1,0:T(8,128)(2,1)S(1)} %bitcast.6, bf16[1,16,32,32]{3,2,1,0:T(8,128)(2,1)S(1)} %copy-done.1, ...), custom_call_target="tpu_custom_call" | custom-call | tf_op jit(solution)/shard_map/pallas_call | solution.py:585
  (33 shorter events, 0.1 us)
Async XLA Ops:
  0.0 1.8 %copy-start.5 = (bf16[64,4096]{1,0:T(8,128)(2,1)S(1)}, bf16[64,4096]{1,0:T(8,128)(2,1)}, u32[]{:S(2)}) copy-start(bf16[64,4096]{1,0:T(8,128)(2,1)} %q_ref.11) | copy-start | bytes 1572868
  0.0 1.8 %copy-start = (bf16[32,4096]{1,0:T(8,128)(2,1)S(1)}, bf16[32,4096]{1,0:T(8,128)(2,1)}, u32[]{:S(2)}) copy-start(bf16[32,4096]{1,0:T(8,128)(2,1)} %basis_ref.3) | copy-start | bytes 786436
  1.8 0.8 %copy-start.2 = (bf16[8,32,32]{2,1,0:T(8,128)(2,1)S(1)}, bf16[8,32,32]{2,1,0:T(8,128)(2,1)}, u32[]{:S(2)}) copy-start(bf16[8,32,32]{2,1,0:T(8,128)(2,1)} %param.17) | copy-start | bytes 49156
  2.7 0.8 %copy-start.6 = (f32[3,4096]{1,0:T(4,128)S(1)}, f32[3,4096]{1,0:T(4,128)}, u32[]{:S(2)}) copy-start(f32[3,4096]{1,0:T(4,128)} %pts_ref.1) | copy-start | bytes 147460
  3.5 9.8 %copy-start.7 = (s32[64,27]{0,1:T(8,128)S(1)}, s32[64,27]{0,1:T(8,128)}, u32[]{:S(2)}) copy-start(s32[64,27]{0,1:T(8,128)} %param.20) | copy-start | bytes 20740
  3.5 9.8 %copy-start.9 = (bf16[96,27]{1,0:T(8,128)(2,1)S(1)}, bf16[96,27]{1,0:T(8,128)(2,1)}, u32[]{:S(2)}) copy-start(bf16[96,27]{1,0:T(8,128)(2,1)} %constant.8.clone.pick_ref) | copy-start | bytes 15556
  3.5 9.8 %copy-start.11 = (bf16[32,16]{1,0:T(8,128)(2,1)S(1)}, bf16[32,16]{1,0:T(8,128)(2,1)}, u32[]{:S(2)}) copy-start(bf16[32,16]{1,0:T(8,128)(2,1)} %constant.7.clone.sel_x_ref) | copy-start | bytes 3076
  4.2 9.1 %copy-start.10 = (bf16[16,160]{1,0:T(8,128)(2,1)S(1)}, bf16[16,160]{1,0:T(8,128)(2,1)}, u32[]{:S(2)}) copy-start(bf16[16,160]{1,0:T(8,128)(2,1)} %constant.6.clone.sel_ref.refs_0_) | copy-start | bytes 15364
  4.2 23.0 %collective-permute-start = (bf16[80,1024]{1,0:T(8,128)(2,1)S(1)}, bf16[80,1024]{1,0:T(8,128)(2,1)S(1)}, u32[]{:S(2)}, u32[]{:S(2)}) collective-permute-start(bf16[80,1024]{1,0:T(8,128)(2,1)S(1)} %get-tuple-element.22), channel_id=1, source_target_pairs={{0,2},{2,0},{4,6},{6,4},{8,10},{10,8},{12,14},{14,12},{16,18},{18,... | collective-permute-start | bytes 491528 | tf_op jit(solution)/shard_map/ppermute | solution.py:566
  4.7 22.5 %collective-permute-start.1 = (bf16[80,1024]{1,0:T(8,128)(2,1)S(1)}, bf16[80,1024]{1,0:T(8,128)(2,1)S(1)}, u32[]{:S(2)}, u32[]{:S(2)}) collective-permute-start(bf16[80,1024]{1,0:T(8,128)(2,1)S(1)} %get-tuple-element.23), channel_id=1, source_target_pairs={{2,4},{4,2},{6,8},{8,6},{10,12},{12,10},{14,16},{16,14},{18,20},{2... | collective-permute-start | bytes 491528 | tf_op jit(solution)/shard_map/ppermute | solution.py:566
  5.4 23.6 %collective-permute-start.2 = (bf16[80,1280]{1,0:T(8,128)(2,1)S(1)}, bf16[80,1280]{1,0:T(8,128)(2,1)S(1)}, u32[]{:S(2)}, u32[]{:S(2)}) collective-permute-start(bf16[80,1280]{1,0:T(8,128)(2,1)S(1)} %get-tuple-element.27), channel_id=1, source_target_pairs={{0,1},{1,0},{2,3},{3,2},{4,5},{5,4},{6,7},{7,6},{8,9},{9,8},{10,11... | collective-permute-start | bytes 614408 | tf_op jit(solution)/shard_map/ppermute | solution.py:566
  8.0 9.3 %collective-permute-start.4 = (bf16[1,32,64]{2,1,0:T(8,128)(2,1)S(1)}, bf16[1,32,64]{2,1,0:T(8,128)(2,1)S(1)}, u32[]{:S(2)}, u32[]{:S(2)}) collective-permute-start(bf16[1,32,64]{2,1,0:T(8,128)(2,1)S(1)} %get-tuple-element.36), channel_id=1, source_target_pairs={{0,16},{2,18},{4,20},{6,22},{8,24},{10,26},{12,28},{14,30},{16,0},... | collective-permute-start | bytes 12296 | tf_op jit(solution)/shard_map/ppermute | solution.py:566
  17.3 3.8 %collective-permute-start.5 = (bf16[2,32,64]{2,1,0:T(8,128)(2,1)S(1)}, bf16[2,32,64]{2,1,0:T(8,128)(2,1)S(1)}, u32[]{:S(2)}, u32[]{:S(2)}) collective-permute-start(bf16[2,32,64]{2,1,0:T(8,128)(2,1)S(1)} %pad_maximum_fusion.2), channel_id=1, source_target_pairs={{0,8},{2,10},{4,12},{6,14},{8,0},{10,2},{12,4},{14,6},{16,24},{18,... | collective-permute-start | bytes 24584 | tf_op jit(solution)/shard_map/ppermute | solution.py:566
  21.2 4.0 %collective-permute-start.6 = (bf16[4,32,64]{2,1,0:T(8,128)(2,1)S(1)}, bf16[4,32,64]{2,1,0:T(8,128)(2,1)S(1)}, u32[]{:S(2)}, u32[]{:S(2)}) collective-permute-start(bf16[4,32,64]{2,1,0:T(8,128)(2,1)S(1)} %pad_maximum_fusion.1), channel_id=1, source_target_pairs={{0,4},{2,6},{4,0},{6,2},{8,12},{10,14},{12,8},{14,10},{16,20},{18,... | collective-permute-start | bytes 49160 | tf_op jit(solution)/shard_map/ppermute | solution.py:566
  25.2 1.3 %collective-permute-start.7 = (bf16[8,32,64]{2,1,0:T(8,128)(2,1)S(1)}, bf16[8,32,64]{2,1,0:T(8,128)(2,1)S(1)}, u32[]{:S(2)}, u32[]{:S(2)}) collective-permute-start(bf16[8,32,64]{2,1,0:T(8,128)(2,1)S(1)} %pad_maximum_fusion), channel_id=1, source_target_pairs={{0,2},{2,0},{4,6},{6,4},{8,10},{10,8},{12,14},{14,12},{16,18},{18,... | collective-permute-start | bytes 98312 | tf_op jit(solution)/shard_map/ppermute | solution.py:566
  26.6 8.3 %collective-permute-start.8 = (bf16[8,32,128]{2,1,0:T(8,128)(2,1)S(1)}, bf16[8,32,128]{2,1,0:T(8,128)(2,1)S(1)}, u32[]{:S(2)}, u32[]{:S(2)}) collective-permute-start(bf16[8,32,128]{2,1,0:T(8,128)(2,1)S(1)} %shard_map.139), channel_id=1, source_target_pairs={{0,1},{1,0},{2,3},{3,2},{4,5},{5,4},{6,7},{7,6},{8,9},{9,8},{10,11... | collective-permute-start | bytes 196616 | tf_op jit(solution)/shard_map/ppermute | solution.py:566
  27.4 6.4 %collective-permute-start.3 = (bf16[80,512]{1,0:T(8,128)(2,1)S(1)}, bf16[80,512]{1,0:T(8,128)(2,1)S(1)}, u32[]{:S(2)}, u32[]{:S(2)}) collective-permute-start(bf16[80,512]{1,0:T(8,128)(2,1)S(1)} %shard_map.136), channel_id=1, source_target_pairs={{0,1},{1,0},{2,3},{3,2},{4,5},{5,4},{6,7},{7,6},{8,9},{9,8},{10,11... | collective-permute-start | bytes 245768 | tf_op jit(solution)/shard_map/ppermute | solution.py:566
  31.6 1.1 %copy-start.4 = (bf16[8,12,32,32]{3,2,1,0:T(8,128)(2,1)S(1)}, bf16[8,12,32,32]{3,2,1,0:T(8,128)(2,1)}, u32[]{:S(2)}) copy-start(bf16[8,12,32,32]{3,2,1,0:T(8,128)(2,1)} %k1_ref.1) | copy-start | bytes 589828
  31.6 1.1 %copy-start.8 = (s32[8,12]{1,0:T(8,128)S(1)}, s32[8,12]{1,0:T(8,128)}, u32[]{:S(2)}) copy-start(s32[8,12]{1,0:T(8,128)} %refs_2_.1) | copy-start | bytes 1156
  33.8 1.1 %copy-start.1 = (bf16[1,16,32,32]{3,2,1,0:T(8,128)(2,1)S(1)}, bf16[1,16,32,32]{3,2,1,0:T(8,128)(2,1)}, u32[]{:S(2)}) copy-start(bf16[1,16,32,32]{3,2,1,0:T(8,128)(2,1)} %k2_ref.1) | copy-start | bytes 98308
  33.8 1.1 %copy-start.3 = (s32[1,16]{1,0:T(1,128)S(1)}, s32[1,16]{1,0:T(1,128)}, u32[]{:S(2)}) copy-start(s32[1,16]{1,0:T(1,128)} %refs_1_.1) | copy-start | bytes 196
